TPU v7x, 1024 devices: a whole 4x4x32 slice. The times are simulated.
1024 devices in a mesh: dp: 16 (over y, z_hi, core), mp: 64 (over z_lo, x).
Axes of the slice: x: 4, y: 4, z: 32 (z_hi: 2, z_lo: 16; z = z_hi * 16 + z_lo), core: 2. Of those that a mesh axis runs over, the one named last changes fastest.
Arguments:
- activations: bfloat16 [4096, 8192], P('dp', 'mp'), may hold values from -40 to 40
- out_grads: bfloat16 [4096, 8192], P('dp', 'mp'), may hold values from -40 to 40
- basis_in: bfloat16 [8192, 8192], P(None, 'mp'), may hold values from -1 to 1
- basis_out: bfloat16 [8192, 8192], P(None, 'mp'), may hold values from -1 to 1
- grad_eigen: bfloat16 [8192, 8192], P('mp', 'dp'), may hold values from -8 to 8
Outputs:
- precond: bfloat16 [8192, 8192], P(('mp', 'dp'))
All inputs are finite; a program needn't handle non-finite values.
Results may differ from a plain program's by a relative error of at most 0.015.
Values may be sent and summed in bfloat16 or wider, within the bound.
No kernel may reach another device: no remote copies, remote signals or barrier semaphores. Data moves between devices by JAX's collectives and lax.ppermute only.
A program may use at most 32 MiB of HBM per device.

v0:
```python
import jax
import jax.numpy as jnp
from jax import lax
from jax.sharding import PartitionSpec as P

damping = 0.1


def projector(basis, piece):
    return jnp.dot(piece, basis, preferred_element_type=jnp.float32)


def per_device(activations, out_grads, basis_in, basis_out, grad_eigen):
    tok_rows = activations.shape[0]
    groups = lax.axis_size("dp")
    proj_in = projector(basis_in, lax.all_gather(activations, "mp", axis=1, tiled=True))
    proj_out = projector(basis_out, lax.all_gather(out_grads, "mp", axis=1, tiled=True))
    squares_in = (proj_in * proj_in).astype(jnp.bfloat16)
    squares_out = (proj_out * proj_out).astype(jnp.bfloat16)
    partial_sums = lax.dot_general(
        squares_in,
        lax.all_gather(squares_out, "mp", axis=1, tiled=True),
        (((0,), (0,)), ((), ())),
        preferred_element_type=jnp.float32,
    )
    summed = lax.psum_scatter(
        partial_sums.astype(jnp.bfloat16), "dp", scatter_dimension=1, tiled=True
    ).astype(jnp.float32)
    scaling = summed / (tok_rows * groups)
    block_result = (grad_eigen.astype(jnp.float32) / (scaling + damping)).astype(jnp.bfloat16)
    return lax.all_to_all(block_result, "dp", split_axis=0, concat_axis=1, tiled=True)


def solution(mesh):
    placed = (P("dp", "mp"), P("dp", "mp"), P(None, "mp"), P(None, "mp"), P("mp", "dp"))
    return jax.shard_map(
        per_device, mesh=mesh, in_specs=placed, out_specs=P(("mp", "dp"), None), check_vma=False
    )
```

profile of v0, /device:TPU:1, one launch (start us, length us, event | category | flops | bytes accessed | tf_op | source)
XLA Modules:
  0.0 1918.1 jit_solution(9744599158950357817)
XLA Ops:
  6.5 0.0 copy-start
  6.5 0.0 all-gather.6.cloned.1.call-start
  6.5 0.7 all-gather.6.cloned.1.call-update
  7.3 0.0 all-gather.4.cloned.1.call-start
  7.3 0.7 all-gather.4.cloned.1.call-update
  8.0 0.0 all-gather.8.cloned.1.call-start
  8.1 531.8 %all-gather.6.cloned.1.call-done = bf16[256,8192]{1,0:T(8,128)(2,1)} async-done(((bf16[256,128]{1,0:T(8,128)(2,1)}), bf16[256,8192]{1,0:T(8,128)(2,1)}) %all-gather.6.cloned.1.call-update) | async-done | bytes 4194320 | tf_op jit(solution)/shard_map/all_gather | solution.py:17
  539.8 4.7 fusion.1
  544.6 0.0 all-gather.8.cloned.1.call-update
  544.6 0.0 copy-start.1
  544.6 0.0 reduce-scatter.2.cloned.1.call-start
  544.7 550.8 %all-gather.4.cloned.1.call-done = bf16[256,8192]{1,0:T(8,128)(2,1)} async-done(((bf16[256,128]{1,0:T(8,128)(2,1)}), bf16[256,8192]{1,0:T(8,128)(2,1)}) %all-gather.4.cloned.1.call-update) | async-done | bytes 4194320 | tf_op jit(solution)/shard_map/all_gather | solution.py:16
  1095.5 555.6 %all-gather.8.cloned.1.call-done = bf16[256,8192]{1,0:T(8,128)(2,1)} async-done(((bf16[256,128]{1,0:T(8,128)(2,1)}), bf16[256,8192]{1,0:T(8,128)(2,1)}) %all-gather.8.cloned.1.call-update) | async-done | bytes 4194320 | tf_op jit(solution)/shard_map/all_gather | solution.py:22
  1651.1 0.0 copy-done
  1651.1 6.8 convolution_convert_fusion
  1657.9 0.0 reduce-scatter.2.cloned.1.call-update
  1658.0 221.8 %reduce-scatter.2.cloned.1.call-done = bf16[128,512]{1,0:T(8,128)(2,1)} async-done(((bf16[128,8192]{1,0:T(8,128)(2,1)}), bf16[128,512]{1,0:T(8,128)(2,1)}) %reduce-scatter.2.cloned.1.call-update) | async-done | bytes 131088 | tf_op jit(solution)/shard_map/reduce_scatter | solution.py:26
  1879.8 0.0 copy-done.1
  1879.8 1.0 fusion.2
  1880.7 30.1 %all_to_all.19 = bf16[16,8,512]{2,1,0:T(8,128)(2,1)S(1)} all-to-all(bf16[16,8,512]{2,1,0:T(8,128)(2,1)S(1)} %fusion.2), channel_id=1, replica_groups=mesh['dp'=16,'mp'=64] {'dp'}, dimensions={0} | all-to-all | bytes 262144 | tf_op jit(solution)/shard_map/all_to_all | solution.py:31
  1910.9 0.7 copy.7
Async XLA Ops:
  6.5 1644.6 %copy-start = (bf16[8192,128]{1,0:T(8,128)(2,1)S(1)}, bf16[8192,128]{1,0:T(8,128)(2,1)}, u32[]{:S(2)}) copy-start(bf16[8192,128]{1,0:T(8,128)(2,1)} %param.7) | copy-start | bytes 6291460
  6.5 533.3 %all-gather.6.cloned.1.call-start = ((), (), s32[]{:S(2)}) async-start(), calls=%async_computation.3 | async-start | bytes 4259840 | tf_op jit(solution)/shard_map/all_gather | solution.py:17
  7.3 1088.2 %all-gather.4.cloned.1.call-start = ((), (), s32[]{:S(2)}) async-start(), calls=%async_computation.2 | async-start | bytes 4259840 | tf_op jit(solution)/shard_map/all_gather | solution.py:16
  8.0 1643.1 %all-gather.8.cloned.1.call-start = ((), (), s32[]{:S(2)}) async-start(), calls=%async_computation.4 | async-start | bytes 4259840 | tf_op jit(solution)/shard_map/all_gather | solution.py:22
  544.6 1335.2 %copy-start.1 = (bf16[128,512]{1,0:T(8,128)(2,1)S(1)}, bf16[128,512]{1,0:T(8,128)(2,1)}, u32[]{:S(2)}) copy-start(bf16[128,512]{1,0:T(8,128)(2,1)} %param.9) | copy-start | bytes 393220
  544.6 1335.1 %reduce-scatter.2.cloned.1.call-start = ((), (), s32[]{:S(2)}) async-start(), calls=%async_computation.5 | async-start | bytes 2228224 | tf_op jit(solution)/shard_map/reduce_scatter | solution.py:26
Sparse Core Ops, SparseCore 0:
  9.9 529.8 all-gather.5
  542.4 552.9 all-gather.3
  1098.1 552.9 all-gather.7
  1658.1 221.6 reduce-scatter.1
where the time goes:
time: 1920 us
  waiting for transfers between devices  1860 us (97%)
  blocking collectives  30.1 us (2%)
    all_gather x1, waiting for transfers between devices, per_device(): lax.all_gather(squares_out, 'mp', axis=1, tiled=True)  556 us
    all_gather x1, waiting for transfers between devices, per_device(): lax.all_gather(activations, 'mp', axis=1, tiled=True)  551 us
    all_gather x1, waiting for transfers between devices, per_device(): lax.all_gather(out_grads, 'mp', axis=1, tiled=True)  532 us
    reduce_scatter x1, waiting for transfers between devices, per_device(): lax.psum_scatter(partial_sums.astype(jnp.bfloat16), 'dp', scatter_dimensi...  222 us
  transfers between devices with their start and end apart: 4, of which 4 were waited for; matrix products, arithmetic and copies ran while one was open for 0% of the time, Pallas kernels for 0%

commit v1 on v0

v1 whole, which is shorter than its diff:
```python
import jax
import jax.numpy as jnp
from jax import lax
from jax.sharding import Mesh, PartitionSpec as P

damping = 0.1
Y, ZH, C, X = 4, 2, 2, 4
Z_BITS = ("z8", "z4", "z2", "z1")
AXES = ("y", "zh", "c") + Z_BITS + ("x",)
f32, bf16 = jnp.float32, jnp.bfloat16


def swap(value, axis):
    return lax.ppermute(value, axis, [(0, 1), (1, 0)])


def gather_z(block):
    have = block[None]
    for axis in Z_BITS:
        other = swap(have, axis)
        upper = lax.axis_index(axis) == 1
        low = jnp.where(upper, other, have)
        high = jnp.where(upper, have, other)
        have = jnp.stack([low, high], axis=1).reshape((-1,) + block.shape)
    return have


def basis_over_x(basis):
    blocks = basis.reshape(16, X, 128, 128)
    return lax.all_to_all(blocks, "x", split_axis=1, concat_axis=1, tiled=True)


def add_over(value, axis):
    parts = lax.all_to_all(value, axis, split_axis=0, concat_axis=0, tiled=True)
    return jnp.sum(parts.astype(f32), axis=0)


def per_device(activations, out_grads, basis_in, basis_out, grad_eigen):
    tokens = activations.shape[0]
    z_out = gather_z(out_grads)
    z_in = gather_z(activations)
    b_out = basis_over_x(basis_out)
    b_in = basis_over_x(basis_in)

    part_out = jnp.einsum("ztf,zxfc->xtc", z_out, b_out, preferred_element_type=f32)
    proj_out = add_over(part_out.astype(bf16), "x")
    squares_out = (proj_out * proj_out).astype(bf16)
    z_squares = gather_z(squares_out)

    part_in = jnp.einsum("zxfc,ztf->xct", b_in, z_in, preferred_element_type=f32)
    proj_in = add_over(part_in.astype(bf16), "x")
    squares_in = (proj_in * proj_in).astype(bf16)
    rows_in = lax.all_gather(squares_in, "x", axis=0, tiled=False)
    rows_in = rows_in.reshape(X, Y, ZH, C, 8, tokens)
    rows_in = rows_in.transpose(3, 1, 2, 0, 4, 5).reshape(C * Y * ZH * X * 8, tokens)

    partial = jnp.einsum("rt,ztc->rzc", rows_in, z_squares, preferred_element_type=f32)
    partial = partial.reshape(C, Y * ZH * X * 8, 2048).astype(bf16)
    partial = add_over(partial, "c").astype(bf16)
    partial = add_over(partial.reshape(Y, ZH * X * 8, 2048), "y").astype(bf16)
    summed = add_over(partial.reshape(ZH, X * 8, 2048), "zh").astype(bf16)
    rows = lax.all_to_all(summed.reshape(X, 8, 2048), "x", split_axis=0, concat_axis=0, tiled=True)
    rows = rows.reshape(X, 8, 16, 128).transpose(1, 2, 0, 3).reshape(8, 8192)

    grad = grad_eigen.reshape(Y * ZH * C, 8, 512)
    grad = lax.all_to_all(grad, ("y", "zh", "c"), split_axis=0, concat_axis=0, tiled=True)
    grad = grad.transpose(1, 0, 2).reshape(8, 8192)
    scaling = rows.astype(f32) / (tokens * Y * ZH * C)
    return (grad.astype(f32) / (scaling + damping)).astype(bf16)


def solution(mesh):
    fine = Mesh(mesh.devices.reshape(Y, ZH, C, 2, 2, 2, 2, X), AXES)
    dp, mp = ("y", "zh", "c"), Z_BITS + ("x",)
    placed = (P(dp, mp), P(dp, mp), P(None, mp), P(None, mp), P(mp, dp))
    return jax.shard_map(
        per_device, mesh=fine, in_specs=placed, out_specs=P(mp + dp, None), check_vma=False
    )
```

time: 1920 us -> 334 us (0.17)
  the two profiles are of different devices: /device:TPU:1 before, /device:TPU:32 now
where the time goes in v1:
time: 334 us; the launch traced here: 333 us
  waiting for transfers between devices  107 us (32%)
  blocking collectives  104 us (31%)
  starting transfers between devices  103 us (31%)
  local copies, waits for them, and re-layouts  6.7 us (2%)
  matrix products  6.54 us (2%)
  other arithmetic  4.34 us (1%)
    all_to_all x3, blocking collectives, add_over(): parts = lax.all_to_all(value, axis, split_axis=0, concat_axis=0, tiled=True)  93.3 us
    ppermute x12, starting transfers between devices, swap(): return lax.ppermute(value, axis, [(0, 1), (1, 0)])  80.1 us
    ppermute x12, waiting for transfers between devices, swap(): return lax.ppermute(value, axis, [(0, 1), (1, 0)])  61.9 us
    all_to_all x1, waiting for transfers between devices, per_device(): lax.all_to_all(grad, ('y', 'zh', 'c'), split_axis=0, concat_axis=0, tiled...  26.7 us
    all_gather x1, blocking collectives, per_device(): rows_in = lax.all_gather(squares_in, 'x', axis=0, tiled=False)  11.1 us
    all_to_all x2, starting transfers between devices, basis_over_x(): return lax.all_to_all(blocks, 'x', split_axis=1, concat_axis=1, tiled=True)  9.03 us
    all_to_all x2, starting transfers between devices, add_over(): parts = lax.all_to_all(value, axis, split_axis=0, concat_axis=0, tiled=True)  7.52 us
    all_to_all x2, waiting for transfers between devices, basis_over_x(): return lax.all_to_all(blocks, 'x', split_axis=1, concat_axis=1, tiled=True)  7.09 us
  transfers between devices with their start and end apart: 18, of which 14 were waited for; matrix products, arithmetic and copies ran while one was open for 3% of the time, Pallas kernels for 0%

profile of v1, /device:TPU:32, one launch (start us, length us, event | category | flops | bytes accessed | tf_op | source)
XLA Modules:
  0.0 333.2 jit_solution(11681964623735001146)
XLA Ops:
  0.0 15.8 %collective-permute-start.4 = (bf16[1,256,128]{2,1,0:T(8,128)(2,1)}, bf16[1,256,128]{2,1,0:T(8,128)(2,1)S(1)}, u32[]{:S(2)}, u32[]{:S(2)}) collective-permute-start(bf16[1,256,128]{2,1,0:T(8,128)(2,1)} %bitcast.173), channel_id=1, source_target_pairs={{0,32},{32,0},{1,33},{33,1},{2,34},{34,2},{3,35},{35,3},{4,36},{36... | collective-permute-start | bytes 196616 | tf_op jit(solution)/shard_map/ppermute | solution.py:14
  15.9 5.2 %collective-permute-done.4 = bf16[1,256,128]{2,1,0:T(8,128)(2,1)S(1)} collective-permute-done((bf16[1,256,128]{2,1,0:T(8,128)(2,1)}, bf16[1,256,128]{2,1,0:T(8,128)(2,1)S(1)}, u32[]{:S(2)}, u32[]{:S(2)}) %collective-permute-start.4) | collective-permute-done | bytes 65568 | tf_op jit(solution)/shard_map/ppermute | solution.py:14
  22.0 10.3 %collective-permute-start.5 = (bf16[2,256,128]{2,1,0:T(8,128)(2,1)S(1)}, bf16[2,256,128]{2,1,0:T(8,128)(2,1)S(1)}, u32[]{:S(2)}, u32[]{:S(2)}) collective-permute-start(bf16[2,256,128]{2,1,0:T(8,128)(2,1)S(1)} %maximum_bitcast_fusion.1), channel_id=1, source_target_pairs={{0,16},{16,0},{1,17},{17,1},{2,18},{18,2},{3,19},{19,3},{4,20},{20... | collective-permute-start | bytes 393224 | tf_op jit(solution)/shard_map/ppermute | solution.py:14
  32.3 9.4 %collective-permute-done.5 = bf16[2,256,128]{2,1,0:T(8,128)(2,1)S(1)} collective-permute-done((bf16[2,256,128]{2,1,0:T(8,128)(2,1)S(1)}, bf16[2,256,128]{2,1,0:T(8,128)(2,1)S(1)}, u32[]{:S(2)}, u32[]{:S(2)}) %collective-permute-start.5) | collective-permute-done | bytes 131104 | tf_op jit(solution)/shard_map/ppermute | solution.py:14
  41.8 4.9 %collective-permute-start.6 = (bf16[4,256,128]{2,1,0:T(8,128)(2,1)S(1)}, bf16[4,256,128]{2,1,0:T(8,128)(2,1)S(1)}, u32[]{:S(2)}, u32[]{:S(2)}) collective-permute-start(bf16[4,256,128]{2,1,0:T(8,128)(2,1)S(1)} %bitcast.171), channel_id=1, source_target_pairs={{0,8},{8,0},{1,9},{9,1},{2,10},{10,2},{3,11},{11,3},{4,12},{12,4},... | collective-permute-start | bytes 786440 | tf_op jit(solution)/shard_map/ppermute | solution.py:14
  48.1 4.3 %all-to-all-start.3 = ((bf16[16,4,128,128]{3,2,0,1:T(8,128)(2,1)}), bf16[16,4,128,128]{3,2,0,1:T(8,128)(2,1)S(1)}, u32[]{:S(2)}, u32[]{:S(2)}) async-start(bf16[16,4,128,128]{3,2,0,1:T(8,128)(2,1)} %copy.59), calls=%async_computation.3 | async-start | bytes 4194304 | tf_op jit(solution)/shard_map/all_to_all | solution.py:30
  55.5 3.9 %collective-permute-start.7 = (bf16[8,256,128]{2,1,0:T(8,128)(2,1)S(1)}, bf16[8,256,128]{2,1,0:T(8,128)(2,1)S(1)}, u32[]{:S(2)}, u32[]{:S(2)}) collective-permute-start(bf16[8,256,128]{2,1,0:T(8,128)(2,1)S(1)} %bitcast.160), channel_id=1, source_target_pairs={{0,4},{4,0},{1,5},{5,1},{2,6},{6,2},{3,7},{7,3},{8,12},{12,8},{9,1... | collective-permute-start | bytes 1572872 | tf_op jit(solution)/shard_map/ppermute | solution.py:14
  59.5 11.8 %collective-permute-done.7 = bf16[8,256,128]{2,1,0:T(8,128)(2,1)S(1)} collective-permute-done((bf16[8,256,128]{2,1,0:T(8,128)(2,1)S(1)}, bf16[8,256,128]{2,1,0:T(8,128)(2,1)S(1)}, u32[]{:S(2)}, u32[]{:S(2)}) %collective-permute-start.7) | collective-permute-done | bytes 524320 | tf_op jit(solution)/shard_map/ppermute | solution.py:14
  71.6 7.1 %all-to-all-done.3 = bf16[16,4,128,128]{3,2,0,1:T(8,128)(2,1)S(1)} async-done(((bf16[16,4,128,128]{3,2,0,1:T(8,128)(2,1)}), bf16[16,4,128,128]{3,2,0,1:T(8,128)(2,1)S(1)}, u32[]{:S(2)}, u32[]{:S(2)}) %all-to-all-start.3) | async-done | bytes 2097184 | tf_op jit(solution)/shard_map/all_to_all | solution.py:30
  80.0 3.1 fusion.2
  83.2 3.4 %all-to-all-start.4 = ((bf16[4,256,128]{2,1,0:T(8,128)(2,1)}), bf16[4,256,128]{2,1,0:T(8,128)(2,1)S(1)}, u32[]{:S(2)}, u32[]{:S(2)}) async-start(bf16[4,256,128]{2,1,0:T(8,128)(2,1)} %fusion.2), calls=%async_computation.4 | async-start | bytes 524288 | tf_op jit(solution)/shard_map/all_to_all | solution.py:34
  86.6 13.0 %collective-permute-start = (bf16[1,256,128]{2,1,0:T(8,128)(2,1)S(1)}, bf16[1,256,128]{2,1,0:T(8,128)(2,1)S(1)}, u32[]{:S(2)}, u32[]{:S(2)}) collective-permute-start(bf16[1,256,128]{2,1,0:T(8,128)(2,1)S(1)} %bitcast.174), channel_id=1, source_target_pairs={{0,32},{32,0},{1,33},{33,1},{2,34},{34,2},{3,35},{35,3},{4,36},{36... | collective-permute-start | bytes 196616 | tf_op jit(solution)/shard_map/ppermute | solution.py:14
  99.7 6.6 %collective-permute-start.8 = (bf16[1,256,128]{2,1,0:T(8,128)(2,1)S(1)}, bf16[1,256,128]{2,1,0:T(8,128)(2,1)S(1)}, u32[]{:S(2)}, u32[]{:S(2)}) collective-permute-start(bf16[1,256,128]{2,1,0:T(8,128)(2,1)S(1)} %fusion.4), channel_id=1, source_target_pairs={{0,32},{32,0},{1,33},{33,1},{2,34},{34,2},{3,35},{35,3},{4,36},{36... | collective-permute-start | bytes 196616 | tf_op jit(solution)/shard_map/ppermute | solution.py:14
  106.5 12.5 %collective-permute-done.8 = bf16[1,256,128]{2,1,0:T(8,128)(2,1)S(1)} collective-permute-done((bf16[1,256,128]{2,1,0:T(8,128)(2,1)S(1)}, bf16[1,256,128]{2,1,0:T(8,128)(2,1)S(1)}, u32[]{:S(2)}, u32[]{:S(2)}) %collective-permute-start.8) | collective-permute-done | bytes 65568 | tf_op jit(solution)/shard_map/ppermute | solution.py:14
  119.0 4.3 %collective-permute-start.1 = (bf16[2,256,128]{2,1,0:T(8,128)(2,1)S(1)}, bf16[2,256,128]{2,1,0:T(8,128)(2,1)S(1)}, u32[]{:S(2)}, u32[]{:S(2)}) collective-permute-start(bf16[2,256,128]{2,1,0:T(8,128)(2,1)S(1)} %maximum_bitcast_fusion), channel_id=1, source_target_pairs={{0,16},{16,0},{1,17},{17,1},{2,18},{18,2},{3,19},{19,3},{4,20},{20... | collective-permute-start | bytes 393224 | tf_op jit(solution)/shard_map/ppermute | solution.py:14
  124.8 4.7 %all-to-all-start.1 = ((bf16[16,4,128,128]{3,2,0,1:T(8,128)(2,1)}), bf16[16,4,128,128]{3,2,0,1:T(8,128)(2,1)S(1)}, u32[]{:S(2)}, u32[]{:S(2)}) async-start(bf16[16,4,128,128]{3,2,0,1:T(8,128)(2,1)} %copy.53), calls=%async_computation.1 | async-start | bytes 4194304 | tf_op jit(solution)/shard_map/all_to_all | solution.py:30
  129.6 4.3 %collective-permute-start.9 = (bf16[2,256,128]{2,1,0:T(8,128)(2,1)S(1)}, bf16[2,256,128]{2,1,0:T(8,128)(2,1)S(1)}, u32[]{:S(2)}, u32[]{:S(2)}) collective-permute-start(bf16[2,256,128]{2,1,0:T(8,128)(2,1)S(1)} %maximum_bitcast_fusion.2), channel_id=1, source_target_pairs={{0,16},{16,0},{1,17},{17,1},{2,18},{18,2},{3,19},{19,3},{4,20},{20... | collective-permute-start | bytes 393224 | tf_op jit(solution)/shard_map/ppermute | solution.py:14
  134.0 8.5 %collective-permute-start.2 = (bf16[4,256,128]{2,1,0:T(8,128)(2,1)S(1)}, bf16[4,256,128]{2,1,0:T(8,128)(2,1)S(1)}, u32[]{:S(2)}, u32[]{:S(2)}) collective-permute-start(bf16[4,256,128]{2,1,0:T(8,128)(2,1)S(1)} %bitcast.169), channel_id=1, source_target_pairs={{0,8},{8,0},{1,9},{9,1},{2,10},{10,2},{3,11},{11,3},{4,12},{12,4},... | collective-permute-start | bytes 786440 | tf_op jit(solution)/shard_map/ppermute | solution.py:14
  142.5 8.2 %collective-permute-done.9 = bf16[2,256,128]{2,1,0:T(8,128)(2,1)S(1)} collective-permute-done((bf16[2,256,128]{2,1,0:T(8,128)(2,1)S(1)}, bf16[2,256,128]{2,1,0:T(8,128)(2,1)S(1)}, u32[]{:S(2)}, u32[]{:S(2)}) %collective-permute-start.9) | collective-permute-done | bytes 131104 | tf_op jit(solution)/shard_map/ppermute | solution.py:14
  152.9 4.6 %collective-permute-start.3 = (bf16[8,256,128]{2,1,0:T(8,128)(2,1)S(1)}, bf16[8,256,128]{2,1,0:T(8,128)(2,1)S(1)}, u32[]{:S(2)}, u32[]{:S(2)}) collective-permute-start(bf16[8,256,128]{2,1,0:T(8,128)(2,1)S(1)} %bitcast.159), channel_id=1, source_target_pairs={{0,4},{4,0},{1,5},{5,1},{2,6},{6,2},{3,7},{7,3},{8,12},{12,8},{9,1... | collective-permute-start | bytes 1572872 | tf_op jit(solution)/shard_map/ppermute | solution.py:14
  157.5 5.3 %collective-permute-done.10 = bf16[4,256,128]{2,1,0:T(8,128)(2,1)S(1)} collective-permute-done((bf16[4,256,128]{2,1,0:T(8,128)(2,1)S(1)}, bf16[4,256,128]{2,1,0:T(8,128)(2,1)S(1)}, u32[]{:S(2)}, u32[]{:S(2)}) %collective-permute-start.10) | collective-permute-done | bytes 262176 | tf_op jit(solution)/shard_map/ppermute | solution.py:14
  164.9 5.4 %collective-permute-done.3 = bf16[8,256,128]{2,1,0:T(8,128)(2,1)S(1)} collective-permute-done((bf16[8,256,128]{2,1,0:T(8,128)(2,1)S(1)}, bf16[8,256,128]{2,1,0:T(8,128)(2,1)S(1)}, u32[]{:S(2)}, u32[]{:S(2)}) %collective-permute-start.3) | collective-permute-done | bytes 524320 | tf_op jit(solution)/shard_map/ppermute | solution.py:14
  174.2 4.1 %all-to-all-start.2 = ((bf16[4,128,256]{1,2,0:T(8,128)(2,1)}), bf16[4,128,256]{1,2,0:T(8,128)(2,1)S(1)}, u32[]{:S(2)}, u32[]{:S(2)}) async-start(bf16[4,128,256]{1,2,0:T(8,128)(2,1)} %fusion.3), calls=%async_computation.2 | async-start | bytes 524288 | tf_op jit(solution)/shard_map/all_to_all | solution.py:34
  180.1 5.7 %all-to-all-done.2 = bf16[4,128,256]{1,2,0:T(8,128)(2,1)S(1)} async-done(((bf16[4,128,256]{1,2,0:T(8,128)(2,1)}), bf16[4,128,256]{1,2,0:T(8,128)(2,1)S(1)}, u32[]{:S(2)}, u32[]{:S(2)}) %all-to-all-start.2) | async-done | bytes 262176 | tf_op jit(solution)/shard_map/all_to_all | solution.py:34
  185.8 11.1 %all-gather = bf16[512,256]{0,1:T(8,128)(2,1)S(1)} all-gather(bf16[128,256]{0,1:T(8,128)(2,1)S(1)} %multiply_convert_fusion.1), channel_id=2, replica_groups=mesh['y'=4,'zh'=2,'c'=2,'z8'=2,'z4'=2,'z2'=2,'z1'=2,'x'=4] {'x'}, dimensions={0}, use_global_device_ids=true | all-gather | bytes 327680 | tf_op jit(solution)/shard_map/all_gather | solution.py:53
  197.8 5.4 %all_to_all.45 = bf16[2,256,2048]{2,1,0:T(8,128)(2,1)S(1)} all-to-all(bf16[2,256,2048]{2,1,0:T(8,128)(2,1)S(1)} %convolution_convert_fusion), channel_id=1, replica_groups=mesh['y'=4,'zh'=2,'c'=2,'z8'=2,'z4'=2,'z2'=2,'z1'=2,'x'=4] {'c'}, dimensions={0} | all-to-all | bytes 4194304 | tf_op jit(solution)/shard_map/all_to_all | solution.py:34
  203.8 19.7 %all_to_all.46 = bf16[4,64,2048]{2,1,0:T(8,128)(2,1)S(1)} all-to-all(bf16[4,64,2048]{2,1,0:T(8,128)(2,1)S(1)} %bitcast.157), channel_id=1, replica_groups=mesh['y'=4,'zh'=2,'c'=2,'z8'=2,'z4'=2,'z2'=2,'z1'=2,'x'=4] {'y'}, dimensions={0} | all-to-all | bytes 2097152 | tf_op jit(solution)/shard_map/all_to_all | solution.py:34
  223.7 68.2 %all_to_all.47 = bf16[2,32,2048]{2,1,0:T(8,128)(2,1)S(1)} all-to-all(bf16[2,32,2048]{2,1,0:T(8,128)(2,1)S(1)} %bitcast.163), channel_id=1, replica_groups=mesh['y'=4,'zh'=2,'c'=2,'z8'=2,'z4'=2,'z2'=2,'z1'=2,'x'=4] {'zh'}, dimensions={0} | all-to-all | bytes 524288 | tf_op jit(solution)/shard_map/all_to_all | solution.py:34
  291.9 3.5 %all-to-all-start = ((bf16[16,8,512]{2,1,0:T(8,128)(2,1)}), bf16[16,8,512]{2,1,0:T(8,128)(2,1)S(1)}, u32[]{:S(2)}, u32[]{:S(2)}) async-start(bf16[16,8,512]{2,1,0:T(8,128)(2,1)} %bitcast), calls=%async_computation | async-start | bytes 262144 | tf_op jit(solution)/shard_map/all_to_all | solution.py:66
  296.2 26.7 %all-to-all-done = bf16[16,8,512]{2,1,0:T(8,128)(2,1)S(1)} async-done(((bf16[16,8,512]{2,1,0:T(8,128)(2,1)}), bf16[16,8,512]{2,1,0:T(8,128)(2,1)S(1)}, u32[]{:S(2)}, u32[]{:S(2)}) %all-to-all-start) | async-done | bytes 131104 | tf_op jit(solution)/shard_map/all_to_all | solution.py:66
  322.9 3.3 all-to-all-start.8
  326.2 5.9 %all-to-all-done.8 = bf16[4,8,2048]{2,1,0:T(8,128)(2,1)S(1)} async-done(((bf16[4,8,2048]{2,1,0:T(8,128)(2,1)}), bf16[4,8,2048]{2,1,0:T(8,128)(2,1)S(1)}, u32[]{:S(2)}, u32[]{:S(2)}) %all-to-all-start.8) | async-done | bytes 131104 | tf_op jit(solution)/shard_map/all_to_all | solution.py:62
  (68 shorter events, 22.3 us)
Async XLA Ops:
  0.0 46.7 %copy-start = (bf16[8192,128]{1,0:T(8,128)(2,1)S(1)}, bf16[8192,128]{1,0:T(8,128)(2,1)}, u32[]{:S(2)}) copy-start(bf16[8192,128]{1,0:T(8,128)(2,1)} %param.8) | copy-start | bytes 6291460
  0.0 21.1 %collective-permute-start.4 = (bf16[1,256,128]{2,1,0:T(8,128)(2,1)}, bf16[1,256,128]{2,1,0:T(8,128)(2,1)S(1)}, u32[]{:S(2)}, u32[]{:S(2)}) collective-permute-start(bf16[1,256,128]{2,1,0:T(8,128)(2,1)} %bitcast.173), channel_id=1, source_target_pairs={{0,32},{32,0},{1,33},{33,1},{2,34},{34,2},{3,35},{35,3},{4,36},{36... | collective-permute-start | bytes 196616 | tf_op jit(solution)/shard_map/ppermute | solution.py:14
  22.0 19.7 %collective-permute-start.5 = (bf16[2,256,128]{2,1,0:T(8,128)(2,1)S(1)}, bf16[2,256,128]{2,1,0:T(8,128)(2,1)S(1)}, u32[]{:S(2)}, u32[]{:S(2)}) collective-permute-start(bf16[2,256,128]{2,1,0:T(8,128)(2,1)S(1)} %maximum_bitcast_fusion.1), channel_id=1, source_target_pairs={{0,16},{16,0},{1,17},{17,1},{2,18},{18,2},{3,19},{19,3},{4,20},{20... | collective-permute-start | bytes 393224 | tf_op jit(solution)/shard_map/ppermute | solution.py:14
  41.8 13.6 %collective-permute-start.6 = (bf16[4,256,128]{2,1,0:T(8,128)(2,1)S(1)}, bf16[4,256,128]{2,1,0:T(8,128)(2,1)S(1)}, u32[]{:S(2)}, u32[]{:S(2)}) collective-permute-start(bf16[4,256,128]{2,1,0:T(8,128)(2,1)S(1)} %bitcast.171), channel_id=1, source_target_pairs={{0,8},{8,0},{1,9},{9,1},{2,10},{10,2},{3,11},{11,3},{4,12},{12,4},... | collective-permute-start | bytes 786440 | tf_op jit(solution)/shard_map/ppermute | solution.py:14
  48.1 30.5 %all-to-all-start.3 = ((bf16[16,4,128,128]{3,2,0,1:T(8,128)(2,1)}), bf16[16,4,128,128]{3,2,0,1:T(8,128)(2,1)S(1)}, u32[]{:S(2)}, u32[]{:S(2)}) async-start(bf16[16,4,128,128]{3,2,0,1:T(8,128)(2,1)} %copy.59), calls=%async_computation.3 | async-start | bytes 4194304 | tf_op jit(solution)/shard_map/all_to_all | solution.py:30
  55.5 15.7 %collective-permute-start.7 = (bf16[8,256,128]{2,1,0:T(8,128)(2,1)S(1)}, bf16[8,256,128]{2,1,0:T(8,128)(2,1)S(1)}, u32[]{:S(2)}, u32[]{:S(2)}) collective-permute-start(bf16[8,256,128]{2,1,0:T(8,128)(2,1)S(1)} %bitcast.160), channel_id=1, source_target_pairs={{0,4},{4,0},{1,5},{5,1},{2,6},{6,2},{3,7},{7,3},{8,12},{12,8},{9,1... | collective-permute-start | bytes 1572872 | tf_op jit(solution)/shard_map/ppermute | solution.py:14
  78.7 1.3 copy-start.2
  80.0 6.6 %copy-start.3 = (bf16[256,128]{1,0:T(8,128)(2,1)S(1)}, bf16[256,128]{1,0:T(8,128)(2,1)}, u32[]{:S(2)}) copy-start(bf16[256,128]{1,0:T(8,128)(2,1)} %param.5) | copy-start | bytes 196612
  80.0 43.3 %copy-start.1 = (bf16[8192,128]{1,0:T(8,128)(2,1)S(1)}, bf16[8192,128]{1,0:T(8,128)(2,1)}, u32[]{:S(2)}) copy-start(bf16[8192,128]{1,0:T(8,128)(2,1)} %param.7) | copy-start | bytes 6291460
  83.2 16.4 %all-to-all-start.4 = ((bf16[4,256,128]{2,1,0:T(8,128)(2,1)}), bf16[4,256,128]{2,1,0:T(8,128)(2,1)S(1)}, u32[]{:S(2)}, u32[]{:S(2)}) async-start(bf16[4,256,128]{2,1,0:T(8,128)(2,1)} %fusion.2), calls=%async_computation.4 | async-start | bytes 524288 | tf_op jit(solution)/shard_map/all_to_all | solution.py:34
  86.6 19.9 %collective-permute-start = (bf16[1,256,128]{2,1,0:T(8,128)(2,1)S(1)}, bf16[1,256,128]{2,1,0:T(8,128)(2,1)S(1)}, u32[]{:S(2)}, u32[]{:S(2)}) collective-permute-start(bf16[1,256,128]{2,1,0:T(8,128)(2,1)S(1)} %bitcast.174), channel_id=1, source_target_pairs={{0,32},{32,0},{1,33},{33,1},{2,34},{34,2},{3,35},{35,3},{4,36},{36... | collective-permute-start | bytes 196616 | tf_op jit(solution)/shard_map/ppermute | solution.py:14
  99.7 19.3 %collective-permute-start.8 = (bf16[1,256,128]{2,1,0:T(8,128)(2,1)S(1)}, bf16[1,256,128]{2,1,0:T(8,128)(2,1)S(1)}, u32[]{:S(2)}, u32[]{:S(2)}) collective-permute-start(bf16[1,256,128]{2,1,0:T(8,128)(2,1)S(1)} %fusion.4), channel_id=1, source_target_pairs={{0,32},{32,0},{1,33},{33,1},{2,34},{34,2},{3,35},{35,3},{4,36},{36... | collective-permute-start | bytes 196616 | tf_op jit(solution)/shard_map/ppermute | solution.py:14
  119.0 14.9 %collective-permute-start.1 = (bf16[2,256,128]{2,1,0:T(8,128)(2,1)S(1)}, bf16[2,256,128]{2,1,0:T(8,128)(2,1)S(1)}, u32[]{:S(2)}, u32[]{:S(2)}) collective-permute-start(bf16[2,256,128]{2,1,0:T(8,128)(2,1)S(1)} %maximum_bitcast_fusion), channel_id=1, source_target_pairs={{0,16},{16,0},{1,17},{17,1},{2,18},{18,2},{3,19},{19,3},{4,20},{20... | collective-permute-start | bytes 393224 | tf_op jit(solution)/shard_map/ppermute | solution.py:14
  124.8 46.8 %all-to-all-start.1 = ((bf16[16,4,128,128]{3,2,0,1:T(8,128)(2,1)}), bf16[16,4,128,128]{3,2,0,1:T(8,128)(2,1)S(1)}, u32[]{:S(2)}, u32[]{:S(2)}) async-start(bf16[16,4,128,128]{3,2,0,1:T(8,128)(2,1)} %copy.53), calls=%async_computation.1 | async-start | bytes 4194304 | tf_op jit(solution)/shard_map/all_to_all | solution.py:30
  129.6 21.1 %collective-permute-start.9 = (bf16[2,256,128]{2,1,0:T(8,128)(2,1)S(1)}, bf16[2,256,128]{2,1,0:T(8,128)(2,1)S(1)}, u32[]{:S(2)}, u32[]{:S(2)}) collective-permute-start(bf16[2,256,128]{2,1,0:T(8,128)(2,1)S(1)} %maximum_bitcast_fusion.2), channel_id=1, source_target_pairs={{0,16},{16,0},{1,17},{17,1},{2,18},{18,2},{3,19},{19,3},{4,20},{20... | collective-permute-start | bytes 393224 | tf_op jit(solution)/shard_map/ppermute | solution.py:14
  134.0 18.8 %collective-permute-start.2 = (bf16[4,256,128]{2,1,0:T(8,128)(2,1)S(1)}, bf16[4,256,128]{2,1,0:T(8,128)(2,1)S(1)}, u32[]{:S(2)}, u32[]{:S(2)}) collective-permute-start(bf16[4,256,128]{2,1,0:T(8,128)(2,1)S(1)} %bitcast.169), channel_id=1, source_target_pairs={{0,8},{8,0},{1,9},{9,1},{2,10},{10,2},{3,11},{11,3},{4,12},{12,4},... | collective-permute-start | bytes 786440 | tf_op jit(solution)/shard_map/ppermute | solution.py:14
  150.8 12.0 %collective-permute-start.10 = (bf16[4,256,128]{2,1,0:T(8,128)(2,1)S(1)}, bf16[4,256,128]{2,1,0:T(8,128)(2,1)S(1)}, u32[]{:S(2)}, u32[]{:S(2)}) collective-permute-start(bf16[4,256,128]{2,1,0:T(8,128)(2,1)S(1)} %bitcast.170), channel_id=1, source_target_pairs={{0,8},{8,0},{1,9},{9,1},{2,10},{10,2},{3,11},{11,3},{4,12},{12,4},... | collective-permute-start | bytes 786440 | tf_op jit(solution)/shard_map/ppermute | solution.py:14
  152.9 17.4 %collective-permute-start.3 = (bf16[8,256,128]{2,1,0:T(8,128)(2,1)S(1)}, bf16[8,256,128]{2,1,0:T(8,128)(2,1)S(1)}, u32[]{:S(2)}, u32[]{:S(2)}) collective-permute-start(bf16[8,256,128]{2,1,0:T(8,128)(2,1)S(1)} %bitcast.159), channel_id=1, source_target_pairs={{0,4},{4,0},{1,5},{5,1},{2,6},{6,2},{3,7},{7,3},{8,12},{12,8},{9,1... | collective-permute-start | bytes 1572872 | tf_op jit(solution)/shard_map/ppermute | solution.py:14
  162.9 16.3 %collective-permute-start.11 = (bf16[8,256,128]{2,1,0:T(8,128)(2,1)S(1)}, bf16[8,256,128]{2,1,0:T(8,128)(2,1)S(1)}, u32[]{:S(2)}, u32[]{:S(2)}) collective-permute-start(bf16[8,256,128]{2,1,0:T(8,128)(2,1)S(1)} %bitcast.158), channel_id=1, source_target_pairs={{0,4},{4,0},{1,5},{5,1},{2,6},{6,2},{3,7},{7,3},{8,12},{12,8},{9,1... | collective-permute-start | bytes 1572872 | tf_op jit(solution)/shard_map/ppermute | solution.py:14
  174.2 11.5 %all-to-all-start.2 = ((bf16[4,128,256]{1,2,0:T(8,128)(2,1)}), bf16[4,128,256]{1,2,0:T(8,128)(2,1)S(1)}, u32[]{:S(2)}, u32[]{:S(2)}) async-start(bf16[4,128,256]{1,2,0:T(8,128)(2,1)} %fusion.3), calls=%async_computation.2 | async-start | bytes 524288 | tf_op jit(solution)/shard_map/all_to_all | solution.py:34
  291.9 30.9 %all-to-all-start = ((bf16[16,8,512]{2,1,0:T(8,128)(2,1)}), bf16[16,8,512]{2,1,0:T(8,128)(2,1)S(1)}, u32[]{:S(2)}, u32[]{:S(2)}) async-start(bf16[16,8,512]{2,1,0:T(8,128)(2,1)} %bitcast), calls=%async_computation | async-start | bytes 262144 | tf_op jit(solution)/shard_map/all_to_all | solution.py:66
  322.9 9.3 %all-to-all-start.8 = ((bf16[4,8,2048]{2,1,0:T(8,128)(2,1)}), bf16[4,8,2048]{2,1,0:T(8,128)(2,1)S(1)}, u32[]{:S(2)}, u32[]{:S(2)}) async-start(bf16[4,8,2048]{2,1,0:T(8,128)(2,1)} %bitcast.61), calls=%async_computation.8 | async-start | bytes 262144 | tf_op jit(solution)/shard_map/all_to_all | solution.py:62

commit v2 on v1

v2 whole, which is shorter than its diff:
```python
import jax
import jax.numpy as jnp
from jax import lax
from jax.sharding import Mesh, PartitionSpec as P

damping = 0.1
Y, ZH, C, X = 4, 2, 2, 4
Z_BITS = ("z8", "z4", "z2", "z1")
AXES = ("y", "zh", "c") + Z_BITS + ("x",)
f32, bf16 = jnp.float32, jnp.bfloat16


def swap(value, axis):
    return lax.ppermute(value, axis, [(0, 1), (1, 0)])


def double_z(have, axis):
    other = swap(have, axis)
    upper = lax.axis_index(axis) == 1
    low = jnp.where(upper, other, have)
    high = jnp.where(upper, have, other)
    return jnp.stack([low, high], axis=1).reshape((-1,) + have.shape[1:])


def basis_over_x(basis):
    blocks = basis.reshape(16, X, 128, 128)
    return lax.all_to_all(blocks, "x", split_axis=1, concat_axis=1, tiled=True)


def add_over(value, axis):
    parts = lax.all_to_all(value, axis, split_axis=0, concat_axis=0, tiled=True)
    return jnp.sum(parts.astype(f32), axis=0)


def together(*values):
    return lax.optimization_barrier(values)


def per_device(activations, out_grads, basis_in, basis_out, grad_eigen):
    tokens = activations.shape[0]
    z_out = double_z(out_grads[None], "z8")
    z_out, z_in = together(z_out, activations[None])
    b_out = basis_over_x(basis_out)
    z_out, z_in = together(double_z(z_out, "z4"), double_z(z_in, "z8"))
    z_out, z_in, b_out, basis_in = together(double_z(z_out, "z2"), double_z(z_in, "z4"), b_out, basis_in)
    b_in = basis_over_x(basis_in)
    z_out, z_in, b_in = together(double_z(z_out, "z1"), double_z(z_in, "z2"), b_in)

    part_out = jnp.einsum("ztf,zxfc->xtc", z_out, b_out, preferred_element_type=f32)
    z_in = double_z(z_in, "z1")
    proj_out = add_over(part_out.astype(bf16), "x")
    squares_out = (proj_out * proj_out).astype(bf16)
    squares_out, z_in = together(squares_out, z_in)

    z_squares = double_z(squares_out[None], "z8")
    part_in = jnp.einsum("zxfc,ztf->xct", b_in, z_in, preferred_element_type=f32)
    proj_in = add_over(part_in.astype(bf16), "x")
    squares_in = (proj_in * proj_in).astype(bf16)
    z_squares, squares_in = together(z_squares, squares_in)

    z_squares = double_z(z_squares, "z4")
    rows_in = lax.all_gather(squares_in, "x", axis=0, tiled=False)
    rows_in = rows_in.reshape(X, Y, ZH, C, 8, tokens)
    rows_in = rows_in.transpose(3, 1, 2, 0, 4, 5).reshape(C * Y * ZH * X * 8, tokens)
    z_squares, rows_in, grad = together(z_squares, rows_in, grad_eigen)

    grad = grad.reshape(Y * ZH * C, 8, 512)
    grad = lax.all_to_all(grad, ("y", "zh", "c"), split_axis=0, concat_axis=0, tiled=True)
    z_squares = double_z(double_z(z_squares, "z2"), "z1")
    z_squares, grad = together(z_squares, grad)
    grad = grad.transpose(1, 0, 2).reshape(8, 8192)

    partial = jnp.einsum("rt,ztc->rzc", rows_in, z_squares, preferred_element_type=f32)
    partial = partial.reshape(C, Y * ZH * X * 8, 2048).astype(bf16)
    partial = add_over(partial, "c").astype(bf16)
    partial = add_over(partial.reshape(Y, ZH * X * 8, 2048), "y").astype(bf16)
    partial = partial.reshape(ZH, X * 8, 2048)
    upper = lax.axis_index("zh") == 1
    other = swap(jnp.where(upper, partial[0], partial[1]), "zh").astype(f32)
    summed = (jnp.where(upper, partial[1], partial[0]).astype(f32) + other).astype(bf16)
    rows = lax.all_to_all(summed.reshape(X, 8, 2048), "x", split_axis=0, concat_axis=0, tiled=True)
    rows = rows.reshape(X, 8, 16, 128).transpose(1, 2, 0, 3).reshape(8, 8192)

    scaling = rows.astype(f32) / (tokens * Y * ZH * C)
    return (grad.astype(f32) / (scaling + damping)).astype(bf16)


def solution(mesh):
    fine = Mesh(mesh.devices.reshape(Y, ZH, C, 2, 2, 2, 2, X), AXES)
    dp, mp = ("y", "zh", "c"), Z_BITS + ("x",)
    placed = (P(dp, mp), P(dp, mp), P(None, mp), P(None, mp), P(mp, dp))
    return jax.shard_map(
        per_device, mesh=fine, in_specs=placed, out_specs=P(mp + dp, None), check_vma=False
    )
```

time: 334 us -> 320 us (0.958)
  the two profiles are of different devices: /device:TPU:32 before, /device:TPU:160 now
where the time goes in v2:
time: 320 us; the launch traced here: 318 us
  waiting for transfers between devices  138 us (43%)
  starting transfers between devices  134 us (42%)
  blocking collectives  19.4 us (6%)
  local copies, waits for them, and re-layouts  14.3 us (4%)
  other arithmetic  6.64 us (2%)
  matrix products  5.47 us (2%)
    ppermute x13, waiting for transfers between devices, swap(): return lax.ppermute(value, axis, [(0, 1), (1, 0)])  107 us
    ppermute x13, starting transfers between devices, swap(): return lax.ppermute(value, axis, [(0, 1), (1, 0)])  81.5 us
    all_to_all x1, starting transfers between devices, per_device(): lax.all_to_all(grad, ('y', 'zh', 'c'), split_axis=0, concat_axis=0, tiled...  25.1 us
    all_to_all x3, waiting for transfers between devices, add_over(): parts = lax.all_to_all(value, axis, split_axis=0, concat_axis=0, tiled=True)  20.1 us
    all_to_all x3, starting transfers between devices, add_over(): parts = lax.all_to_all(value, axis, split_axis=0, concat_axis=0, tiled=True)  15.2 us
    all_gather x1, blocking collectives, per_device(): rows_in = lax.all_gather(squares_in, 'x', axis=0, tiled=False)  12.8 us
    all_to_all x2, starting transfers between devices, basis_over_x(): return lax.all_to_all(blocks, 'x', split_axis=1, concat_axis=1, tiled=True)  8.73 us
    all_to_all x1, blocking collectives, add_over(): parts = lax.all_to_all(value, axis, split_axis=0, concat_axis=0, tiled=True)  6.61 us
  transfers between devices with their start and end apart: 20, of which 15 were waited for; matrix products, arithmetic and copies ran while one was open for 3% of the time, Pallas kernels for 0%

profile of v2, /device:TPU:160, one launch (start us, length us, event | category | flops | bytes accessed | tf_op | source)
XLA Modules:
  0.0 318.2 jit_solution(3934050664875994300)
XLA Ops:
  0.9 15.7 %collective-permute-start = (bf16[1,256,128]{1,2,0:T(8,128)(2,1)S(1)}, bf16[1,256,128]{1,2,0:T(8,128)(2,1)S(1)}, u32[]{:S(2)}, u32[]{:S(2)}) collective-permute-start(bf16[1,256,128]{1,2,0:T(8,128)(2,1)S(1)} %bitcast.144), channel_id=1, source_target_pairs={{0,32},{32,0},{1,33},{33,1},{2,34},{34,2},{3,35},{35,3},{4,36},{36... | collective-permute-start | bytes 196616 | tf_op jit(solution)/shard_map/ppermute | solution.py:14
  17.6 5.2 %collective-permute-done = bf16[1,256,128]{1,2,0:T(8,128)(2,1)S(1)} collective-permute-done((bf16[1,256,128]{1,2,0:T(8,128)(2,1)S(1)}, bf16[1,256,128]{1,2,0:T(8,128)(2,1)S(1)}, u32[]{:S(2)}, u32[]{:S(2)}) %collective-permute-start) | collective-permute-done | bytes 65568 | tf_op jit(solution)/shard_map/ppermute | solution.py:14
  22.9 13.2 %collective-permute-start.2 = (bf16[1,256,128]{1,2,0:T(8,128)(2,1)S(1)}, bf16[1,256,128]{1,2,0:T(8,128)(2,1)S(1)}, u32[]{:S(2)}, u32[]{:S(2)}) collective-permute-start(bf16[1,256,128]{1,2,0:T(8,128)(2,1)S(1)} %bitcast.142), channel_id=1, source_target_pairs={{0,32},{32,0},{1,33},{33,1},{2,34},{34,2},{3,35},{35,3},{4,36},{36... | collective-permute-start | bytes 196616 | tf_op jit(solution)/shard_map/ppermute | solution.py:14
  36.1 3.9 %copy.69 = bf16[16,4,128,128]{2,3,0,1:T(8,128)(2,1)} copy(bf16[16,4,128,128]{3,2,1,0:T(8,128)(2,1)} %bitcast.127) | data formatting | bytes 4194304 | tf_op jit(solution)/shard_map/reshape | solution.py:26
  40.0 4.5 %all-to-all-start = ((bf16[16,4,128,128]{2,3,0,1:T(8,128)(2,1)}), bf16[16,4,128,128]{2,3,0,1:T(8,128)(2,1)}, u32[]{:S(2)}, u32[]{:S(2)}) async-start(bf16[16,4,128,128]{2,3,0,1:T(8,128)(2,1)} %copy.69), calls=%async_computation | async-start | bytes 4194304 | tf_op jit(solution)/shard_map/all_to_all | solution.py:27
  46.5 10.5 %collective-permute-done.1 = bf16[2,256,128]{1,2,0:T(8,128)(2,1)S(1)} collective-permute-done((bf16[2,256,128]{1,2,0:T(8,128)(2,1)S(1)}, bf16[2,256,128]{1,2,0:T(8,128)(2,1)S(1)}, u32[]{:S(2)}, u32[]{:S(2)}) %collective-permute-start.1) | collective-permute-done | bytes 131104 | tf_op jit(solution)/shard_map/ppermute | solution.py:14
  57.2 6.3 %collective-permute-start.4 = (bf16[2,256,128]{1,2,0:T(8,128)(2,1)S(1)}, bf16[2,256,128]{1,2,0:T(8,128)(2,1)S(1)}, u32[]{:S(2)}, u32[]{:S(2)}) collective-permute-start(bf16[2,256,128]{1,2,0:T(8,128)(2,1)S(1)} %maximum_bitcast_fusion.1), channel_id=1, source_target_pairs={{0,16},{16,0},{1,17},{17,1},{2,18},{18,2},{3,19},{19,3},{4,20},{20... | collective-permute-start | bytes 393224 | tf_op jit(solution)/shard_map/ppermute | solution.py:14
  63.5 6.7 %collective-permute-start.3 = (bf16[4,256,128]{2,1,0:T(8,128)(2,1)S(1)}, bf16[4,256,128]{2,1,0:T(8,128)(2,1)S(1)}, u32[]{:S(2)}, u32[]{:S(2)}) collective-permute-start(bf16[4,256,128]{2,1,0:T(8,128)(2,1)S(1)} %bitcast.137), channel_id=1, source_target_pairs={{0,8},{8,0},{1,9},{9,1},{2,10},{10,2},{3,11},{11,3},{4,12},{12,4},... | collective-permute-start | bytes 786440 | tf_op jit(solution)/shard_map/ppermute | solution.py:14
  72.7 11.8 %collective-permute-done.3 = bf16[4,256,128]{2,1,0:T(8,128)(2,1)S(1)} collective-permute-done((bf16[4,256,128]{2,1,0:T(8,128)(2,1)S(1)}, bf16[4,256,128]{2,1,0:T(8,128)(2,1)S(1)}, u32[]{:S(2)}, u32[]{:S(2)}) %collective-permute-start.3) | collective-permute-done | bytes 262176 | tf_op jit(solution)/shard_map/ppermute | solution.py:14
  87.3 4.3 %all-to-all-start.1 = ((bf16[16,4,128,128]{2,3,0,1:T(8,128)(2,1)}), bf16[16,4,128,128]{2,3,0,1:T(8,128)(2,1)S(1)}, u32[]{:S(2)}, u32[]{:S(2)}) async-start(bf16[16,4,128,128]{2,3,0,1:T(8,128)(2,1)} %copy.72), calls=%async_computation.1 | async-start | bytes 4194304 | tf_op jit(solution)/shard_map/all_to_all | solution.py:27
  91.5 5.3 %collective-permute-start.6 = (bf16[4,256,128]{2,1,0:T(8,128)(2,1)S(1)}, bf16[4,256,128]{2,1,0:T(8,128)(2,1)S(1)}, u32[]{:S(2)}, u32[]{:S(2)}) collective-permute-start(bf16[4,256,128]{2,1,0:T(8,128)(2,1)S(1)} %bitcast.135), channel_id=1, source_target_pairs={{0,8},{8,0},{1,9},{9,1},{2,10},{10,2},{3,11},{11,3},{4,12},{12,4},... | collective-permute-start | bytes 786440 | tf_op jit(solution)/shard_map/ppermute | solution.py:14
  98.8 5.2 %collective-permute-done.6 = bf16[4,256,128]{2,1,0:T(8,128)(2,1)S(1)} collective-permute-done((bf16[4,256,128]{2,1,0:T(8,128)(2,1)S(1)}, bf16[4,256,128]{2,1,0:T(8,128)(2,1)S(1)}, u32[]{:S(2)}, u32[]{:S(2)}) %collective-permute-start.6) | collective-permute-done | bytes 262176 | tf_op jit(solution)/shard_map/ppermute | solution.py:14
  104.1 8.0 %collective-permute-done.5 = bf16[8,256,128]{2,1,0:T(8,128)(2,1)} collective-permute-done((bf16[8,256,128]{2,1,0:T(8,128)(2,1)S(1)}, bf16[8,256,128]{2,1,0:T(8,128)(2,1)}, u32[]{:S(2)}, u32[]{:S(2)}) %collective-permute-start.5) | collective-permute-done | bytes 524320 | tf_op jit(solution)/shard_map/ppermute | solution.py:14
  114.4 3.6 %all-to-all-done.1 = bf16[16,4,128,128]{2,3,0,1:T(8,128)(2,1)S(1)} async-done(((bf16[16,4,128,128]{2,3,0,1:T(8,128)(2,1)}), bf16[16,4,128,128]{2,3,0,1:T(8,128)(2,1)S(1)}, u32[]{:S(2)}, u32[]{:S(2)}) %all-to-all-start.1) | async-done | bytes 2097184 | tf_op jit(solution)/shard_map/all_to_all | solution.py:27
  118.1 3.3 %fusion.2 = bf16[4,256,128]{1,2,0:T(8,128)(2,1)} fusion(bf16[16,4,128,128]{2,3,0,1:T(8,128)(2,1)} %all-to-all-done, bf16[16,256,128]{2,1,0:T(8,128)(2,1)} %bitcast.131), kind=kOutput, calls=%fused_computation.5 | convolution fusion | flops 537001984 | bytes 3407872 | tf_op jit(solution)/shard_map/ztf,zxfc->xtc/dot_general | solution.py:49
  121.4 3.4 %all-to-all-start.2 = ((bf16[4,256,128]{1,2,0:T(8,128)(2,1)}), bf16[4,256,128]{1,2,0:T(8,128)(2,1)S(1)}, u32[]{:S(2)}, u32[]{:S(2)}) async-start(bf16[4,256,128]{1,2,0:T(8,128)(2,1)} %fusion.2), calls=%async_computation.2 | async-start | bytes 524288 | tf_op jit(solution)/shard_map/all_to_all | solution.py:31
  126.7 4.7 %all-to-all-done.2 = bf16[4,256,128]{1,2,0:T(8,128)(2,1)S(1)} async-done(((bf16[4,256,128]{1,2,0:T(8,128)(2,1)}), bf16[4,256,128]{1,2,0:T(8,128)(2,1)S(1)}, u32[]{:S(2)}, u32[]{:S(2)}) %all-to-all-start.2) | async-done | bytes 262176 | tf_op jit(solution)/shard_map/all_to_all | solution.py:31
  131.5 8.0 %collective-permute-done.7 = bf16[8,256,128]{2,1,0:T(8,128)(2,1)} collective-permute-done((bf16[8,256,128]{2,1,0:T(8,128)(2,1)S(1)}, bf16[8,256,128]{2,1,0:T(8,128)(2,1)}, u32[]{:S(2)}, u32[]{:S(2)}) %collective-permute-start.7) | collective-permute-done | bytes 524320 | tf_op jit(solution)/shard_map/ppermute | solution.py:14
  144.8 4.5 %all-to-all-start.3 = ((bf16[4,128,256]{2,1,0:T(8,128)(2,1)}), bf16[4,128,256]{2,1,0:T(8,128)(2,1)S(1)}, u32[]{:S(2)}, u32[]{:S(2)}) async-start(bf16[4,128,256]{2,1,0:T(8,128)(2,1)} %fusion.1), calls=%async_computation.3 | async-start | bytes 524288 | tf_op jit(solution)/shard_map/all_to_all | solution.py:31
  149.2 6.9 %collective-permute-done.8 = bf16[1,256,128]{1,2,0:T(8,128)(2,1)S(1)} collective-permute-done((bf16[1,256,128]{1,2,0:T(8,128)(2,1)S(1)}, bf16[1,256,128]{1,2,0:T(8,128)(2,1)S(1)}, u32[]{:S(2)}, u32[]{:S(2)}) %collective-permute-start.8) | collective-permute-done | bytes 65568 | tf_op jit(solution)/shard_map/ppermute | solution.py:14
  156.2 4.5 %collective-permute-start.9 = (bf16[2,256,128]{1,2,0:T(8,128)(2,1)S(1)}, bf16[2,256,128]{1,2,0:T(8,128)(2,1)S(1)}, u32[]{:S(2)}, u32[]{:S(2)}) collective-permute-start(bf16[2,256,128]{1,2,0:T(8,128)(2,1)S(1)} %maximum_bitcast_fusion.2), channel_id=1, source_target_pairs={{0,16},{16,0},{1,17},{17,1},{2,18},{18,2},{3,19},{19,3},{4,20},{20... | collective-permute-start | bytes 393224 | tf_op jit(solution)/shard_map/ppermute | solution.py:14
  160.7 12.8 %all-gather = bf16[512,256]{1,0:T(8,128)(2,1)S(1)} all-gather(bf16[128,256]{1,0:T(8,128)(2,1)S(1)} %multiply_convert_fusion), channel_id=2, replica_groups=mesh['y'=4,'zh'=2,'c'=2,'z8'=2,'z4'=2,'z2'=2,'z1'=2,'x'=4] {'x'}, dimensions={0}, use_global_device_ids=true | all-gather | bytes 327680 | tf_op jit(solution)/shard_map/all_gather | solution.py:62
  176.9 25.1 %all-to-all-start.4 = ((bf16[16,8,512]{2,1,0:T(8,128)(2,1)}), bf16[16,8,512]{2,1,0:T(8,128)(2,1)S(1)}, u32[]{:S(2)}, u32[]{:S(2)}) async-start(bf16[16,8,512]{2,1,0:T(8,128)(2,1)} %bitcast.51), calls=%async_computation.4 | async-start | bytes 262144 | tf_op jit(solution)/shard_map/all_to_all | solution.py:68
  202.1 3.9 %collective-permute-start.11 = (bf16[8,256,128]{2,1,0:T(8,128)(2,1)S(1)}, bf16[8,256,128]{2,1,0:T(8,128)(2,1)S(1)}, u32[]{:S(2)}, u32[]{:S(2)}) collective-permute-start(bf16[8,256,128]{2,1,0:T(8,128)(2,1)S(1)} %bitcast.126), channel_id=1, source_target_pairs={{0,4},{4,0},{1,5},{5,1},{2,6},{6,2},{3,7},{7,3},{8,12},{12,8},{9,1... | collective-permute-start | bytes 1572872 | tf_op jit(solution)/shard_map/ppermute | solution.py:14
  206.1 19.7 %collective-permute-done.11 = bf16[8,256,128]{2,1,0:T(8,128)(2,1)S(1)} collective-permute-done((bf16[8,256,128]{2,1,0:T(8,128)(2,1)S(1)}, bf16[8,256,128]{2,1,0:T(8,128)(2,1)S(1)}, u32[]{:S(2)}, u32[]{:S(2)}) %collective-permute-start.11) | collective-permute-done | bytes 524320 | tf_op jit(solution)/shard_map/ppermute | solution.py:14
  231.7 6.6 %all_to_all.40 = bf16[2,256,2048]{2,1,0:T(8,128)(2,1)S(1)} all-to-all(bf16[2,256,2048]{2,1,0:T(8,128)(2,1)} %convert_element_type.69), channel_id=1, replica_groups=mesh['y'=4,'zh'=2,'c'=2,'z8'=2,'z4'=2,'z2'=2,'z1'=2,'x'=4] {'c'}, dimensions={0} | all-to-all | bytes 4194304 | tf_op jit(solution)/shard_map/all_to_all | solution.py:31
  240.1 7.3 %all-to-all-start.6 = ((bf16[4,64,2048]{2,1,0:T(8,128)(2,1)}), bf16[4,64,2048]{2,1,0:T(8,128)(2,1)S(1)}, u32[]{:S(2)}, u32[]{:S(2)}) async-start(bf16[4,64,2048]{2,1,0:T(8,128)(2,1)} %bitcast.55), calls=%async_computation.6 | async-start | bytes 2097152 | tf_op jit(solution)/shard_map/all_to_all | solution.py:31
  247.4 15.4 %all-to-all-done.6 = bf16[4,64,2048]{2,1,0:T(8,128)(2,1)S(1)} async-done(((bf16[4,64,2048]{2,1,0:T(8,128)(2,1)}), bf16[4,64,2048]{2,1,0:T(8,128)(2,1)S(1)}, u32[]{:S(2)}, u32[]{:S(2)}) %all-to-all-start.6) | async-done | bytes 1048608 | tf_op jit(solution)/shard_map/all_to_all | solution.py:31
  263.0 14.5 %collective-permute-start.12 = (bf16[32,2048]{1,0:T(8,128)(2,1)S(1)}, bf16[32,2048]{1,0:T(8,128)(2,1)S(1)}, u32[]{:S(2)}, u32[]{:S(2)}) collective-permute-start(bf16[32,2048]{1,0:T(8,128)(2,1)S(1)} %broadcast_select_fusion), channel_id=1, source_target_pairs={{0,128},{128,0},{1,129},{129,1},{2,130},{130,2},{3,131},{131,3},{4... | collective-permute-start | bytes 393224 | tf_op jit(solution)/shard_map/ppermute | solution.py:14
  277.6 29.5 %collective-permute-done.12 = bf16[32,2048]{1,0:T(8,128)(2,1)S(1)} collective-permute-done((bf16[32,2048]{1,0:T(8,128)(2,1)S(1)}, bf16[32,2048]{1,0:T(8,128)(2,1)S(1)}, u32[]{:S(2)}, u32[]{:S(2)}) %collective-permute-start.12) | collective-permute-done | bytes 131104 | tf_op jit(solution)/shard_map/ppermute | solution.py:14
  307.8 3.3 %all-to-all-start.7 = ((bf16[4,8,2048]{2,1,0:T(8,128)(2,1)}), bf16[4,8,2048]{2,1,0:T(8,128)(2,1)S(1)}, u32[]{:S(2)}, u32[]{:S(2)}) async-start(bf16[4,8,2048]{2,1,0:T(8,128)(2,1)} %fusion.6), calls=%async_computation.7 | async-start | bytes 262144 | tf_op jit(solution)/shard_map/all_to_all | solution.py:81
  311.2 5.9 %all-to-all-done.7 = bf16[4,8,2048]{2,1,0:T(8,128)(2,1)S(1)} async-done(((bf16[4,8,2048]{2,1,0:T(8,128)(2,1)}), bf16[4,8,2048]{2,1,0:T(8,128)(2,1)S(1)}, u32[]{:S(2)}, u32[]{:S(2)}) %all-to-all-start.7) | async-done | bytes 131104 | tf_op jit(solution)/shard_map/all_to_all | solution.py:81
  (69 shorter events, 34.0 us)
Async XLA Ops:
  0.9 21.9 %collective-permute-start = (bf16[1,256,128]{1,2,0:T(8,128)(2,1)S(1)}, bf16[1,256,128]{1,2,0:T(8,128)(2,1)S(1)}, u32[]{:S(2)}, u32[]{:S(2)}) collective-permute-start(bf16[1,256,128]{1,2,0:T(8,128)(2,1)S(1)} %bitcast.144), channel_id=1, source_target_pairs={{0,32},{32,0},{1,33},{33,1},{2,34},{34,2},{3,35},{35,3},{4,36},{36... | collective-permute-start | bytes 196616 | tf_op jit(solution)/shard_map/ppermute | solution.py:14
  22.9 23.6 %collective-permute-start.2 = (bf16[1,256,128]{1,2,0:T(8,128)(2,1)S(1)}, bf16[1,256,128]{1,2,0:T(8,128)(2,1)S(1)}, u32[]{:S(2)}, u32[]{:S(2)}) collective-permute-start(bf16[1,256,128]{1,2,0:T(8,128)(2,1)S(1)} %bitcast.142), channel_id=1, source_target_pairs={{0,32},{32,0},{1,33},{33,1},{2,34},{34,2},{3,35},{35,3},{4,36},{36... | collective-permute-start | bytes 196616 | tf_op jit(solution)/shard_map/ppermute | solution.py:14
  40.0 44.6 %all-to-all-start = ((bf16[16,4,128,128]{2,3,0,1:T(8,128)(2,1)}), bf16[16,4,128,128]{2,3,0,1:T(8,128)(2,1)}, u32[]{:S(2)}, u32[]{:S(2)}) async-start(bf16[16,4,128,128]{2,3,0,1:T(8,128)(2,1)} %copy.69), calls=%async_computation | async-start | bytes 4194304 | tf_op jit(solution)/shard_map/all_to_all | solution.py:27
  44.5 12.5 %collective-permute-start.1 = (bf16[2,256,128]{1,2,0:T(8,128)(2,1)S(1)}, bf16[2,256,128]{1,2,0:T(8,128)(2,1)S(1)}, u32[]{:S(2)}, u32[]{:S(2)}) collective-permute-start(bf16[2,256,128]{1,2,0:T(8,128)(2,1)S(1)} %maximum_bitcast_fusion), channel_id=1, source_target_pairs={{0,16},{16,0},{1,17},{17,1},{2,18},{18,2},{3,19},{19,3},{4,20},{20... | collective-permute-start | bytes 393224 | tf_op jit(solution)/shard_map/ppermute | solution.py:14
  57.2 15.2 %collective-permute-start.4 = (bf16[2,256,128]{1,2,0:T(8,128)(2,1)S(1)}, bf16[2,256,128]{1,2,0:T(8,128)(2,1)S(1)}, u32[]{:S(2)}, u32[]{:S(2)}) collective-permute-start(bf16[2,256,128]{1,2,0:T(8,128)(2,1)S(1)} %maximum_bitcast_fusion.1), channel_id=1, source_target_pairs={{0,16},{16,0},{1,17},{17,1},{2,18},{18,2},{3,19},{19,3},{4,20},{20... | collective-permute-start | bytes 393224 | tf_op jit(solution)/shard_map/ppermute | solution.py:14
  63.5 21.0 %collective-permute-start.3 = (bf16[4,256,128]{2,1,0:T(8,128)(2,1)S(1)}, bf16[4,256,128]{2,1,0:T(8,128)(2,1)S(1)}, u32[]{:S(2)}, u32[]{:S(2)}) collective-permute-start(bf16[4,256,128]{2,1,0:T(8,128)(2,1)S(1)} %bitcast.137), channel_id=1, source_target_pairs={{0,8},{8,0},{1,9},{9,1},{2,10},{10,2},{3,11},{11,3},{4,12},{12,4},... | collective-permute-start | bytes 786440 | tf_op jit(solution)/shard_map/ppermute | solution.py:14
  72.5 12.2 %copy-start = (bf16[8192,128]{1,0:T(8,128)(2,1)S(1)}, bf16[8192,128]{1,0:T(8,128)(2,1)}, u32[]{:S(2)}) copy-start(bf16[8192,128]{1,0:T(8,128)(2,1)} %param.7) | copy-start | bytes 6291460
  87.3 30.8 %all-to-all-start.1 = ((bf16[16,4,128,128]{2,3,0,1:T(8,128)(2,1)}), bf16[16,4,128,128]{2,3,0,1:T(8,128)(2,1)S(1)}, u32[]{:S(2)}, u32[]{:S(2)}) async-start(bf16[16,4,128,128]{2,3,0,1:T(8,128)(2,1)} %copy.72), calls=%async_computation.1 | async-start | bytes 4194304 | tf_op jit(solution)/shard_map/all_to_all | solution.py:27
  91.5 12.4 %collective-permute-start.6 = (bf16[4,256,128]{2,1,0:T(8,128)(2,1)S(1)}, bf16[4,256,128]{2,1,0:T(8,128)(2,1)S(1)}, u32[]{:S(2)}, u32[]{:S(2)}) collective-permute-start(bf16[4,256,128]{2,1,0:T(8,128)(2,1)S(1)} %bitcast.135), channel_id=1, source_target_pairs={{0,8},{8,0},{1,9},{9,1},{2,10},{10,2},{3,11},{11,3},{4,12},{12,4},... | collective-permute-start | bytes 786440 | tf_op jit(solution)/shard_map/ppermute | solution.py:14
  96.8 15.3 %collective-permute-start.5 = (bf16[8,256,128]{2,1,0:T(8,128)(2,1)S(1)}, bf16[8,256,128]{2,1,0:T(8,128)(2,1)}, u32[]{:S(2)}, u32[]{:S(2)}) collective-permute-start(bf16[8,256,128]{2,1,0:T(8,128)(2,1)S(1)} %bitcast.122), channel_id=1, source_target_pairs={{0,4},{4,0},{1,5},{5,1},{2,6},{6,2},{3,7},{7,3},{8,12},{12,8},{9,1... | collective-permute-start | bytes 1572872 | tf_op jit(solution)/shard_map/ppermute | solution.py:14
  121.4 10.1 %all-to-all-start.2 = ((bf16[4,256,128]{1,2,0:T(8,128)(2,1)}), bf16[4,256,128]{1,2,0:T(8,128)(2,1)S(1)}, u32[]{:S(2)}, u32[]{:S(2)}) async-start(bf16[4,256,128]{1,2,0:T(8,128)(2,1)} %fusion.2), calls=%async_computation.2 | async-start | bytes 524288 | tf_op jit(solution)/shard_map/all_to_all | solution.py:31
  124.8 14.7 %collective-permute-start.7 = (bf16[8,256,128]{2,1,0:T(8,128)(2,1)S(1)}, bf16[8,256,128]{2,1,0:T(8,128)(2,1)}, u32[]{:S(2)}, u32[]{:S(2)}) collective-permute-start(bf16[8,256,128]{2,1,0:T(8,128)(2,1)S(1)} %bitcast.124), channel_id=1, source_target_pairs={{0,4},{4,0},{1,5},{5,1},{2,6},{6,2},{3,7},{7,3},{8,12},{12,8},{9,1... | collective-permute-start | bytes 1572872 | tf_op jit(solution)/shard_map/ppermute | solution.py:14
  140.8 15.4 %collective-permute-start.8 = (bf16[1,256,128]{1,2,0:T(8,128)(2,1)S(1)}, bf16[1,256,128]{1,2,0:T(8,128)(2,1)S(1)}, u32[]{:S(2)}, u32[]{:S(2)}) collective-permute-start(bf16[1,256,128]{1,2,0:T(8,128)(2,1)S(1)} %bitcast.141), channel_id=1, source_target_pairs={{0,32},{32,0},{1,33},{33,1},{2,34},{34,2},{3,35},{35,3},{4,36},{36... | collective-permute-start | bytes 196616 | tf_op jit(solution)/shard_map/ppermute | solution.py:14
  144.8 11.4 %all-to-all-start.3 = ((bf16[4,128,256]{2,1,0:T(8,128)(2,1)}), bf16[4,128,256]{2,1,0:T(8,128)(2,1)S(1)}, u32[]{:S(2)}, u32[]{:S(2)}) async-start(bf16[4,128,256]{2,1,0:T(8,128)(2,1)} %fusion.1), calls=%async_computation.3 | async-start | bytes 524288 | tf_op jit(solution)/shard_map/all_to_all | solution.py:31
  156.2 17.3 %collective-permute-start.9 = (bf16[2,256,128]{1,2,0:T(8,128)(2,1)S(1)}, bf16[2,256,128]{1,2,0:T(8,128)(2,1)S(1)}, u32[]{:S(2)}, u32[]{:S(2)}) collective-permute-start(bf16[2,256,128]{1,2,0:T(8,128)(2,1)S(1)} %maximum_bitcast_fusion.2), channel_id=1, source_target_pairs={{0,16},{16,0},{1,17},{17,1},{2,18},{18,2},{3,19},{19,3},{4,20},{20... | collective-permute-start | bytes 393224 | tf_op jit(solution)/shard_map/ppermute | solution.py:14
  173.8 28.2 %collective-permute-start.10 = (bf16[4,256,128]{2,1,0:T(8,128)(2,1)S(1)}, bf16[4,256,128]{2,1,0:T(8,128)(2,1)S(1)}, u32[]{:S(2)}, u32[]{:S(2)}) collective-permute-start(bf16[4,256,128]{2,1,0:T(8,128)(2,1)S(1)} %bitcast.139), channel_id=1, source_target_pairs={{0,8},{8,0},{1,9},{9,1},{2,10},{10,2},{3,11},{11,3},{4,12},{12,4},... | collective-permute-start | bytes 786440 | tf_op jit(solution)/shard_map/ppermute | solution.py:14
  176.9 50.4 %all-to-all-start.4 = ((bf16[16,8,512]{2,1,0:T(8,128)(2,1)}), bf16[16,8,512]{2,1,0:T(8,128)(2,1)S(1)}, u32[]{:S(2)}, u32[]{:S(2)}) async-start(bf16[16,8,512]{2,1,0:T(8,128)(2,1)} %bitcast.51), calls=%async_computation.4 | async-start | bytes 262144 | tf_op jit(solution)/shard_map/all_to_all | solution.py:68
  202.1 23.7 %collective-permute-start.11 = (bf16[8,256,128]{2,1,0:T(8,128)(2,1)S(1)}, bf16[8,256,128]{2,1,0:T(8,128)(2,1)S(1)}, u32[]{:S(2)}, u32[]{:S(2)}) collective-permute-start(bf16[8,256,128]{2,1,0:T(8,128)(2,1)S(1)} %bitcast.126), channel_id=1, source_target_pairs={{0,4},{4,0},{1,5},{5,1},{2,6},{6,2},{3,7},{7,3},{8,12},{12,8},{9,1... | collective-permute-start | bytes 1572872 | tf_op jit(solution)/shard_map/ppermute | solution.py:14
  240.1 22.7 %all-to-all-start.6 = ((bf16[4,64,2048]{2,1,0:T(8,128)(2,1)}), bf16[4,64,2048]{2,1,0:T(8,128)(2,1)S(1)}, u32[]{:S(2)}, u32[]{:S(2)}) async-start(bf16[4,64,2048]{2,1,0:T(8,128)(2,1)} %bitcast.55), calls=%async_computation.6 | async-start | bytes 2097152 | tf_op jit(solution)/shard_map/all_to_all | solution.py:31
  263.0 44.1 %collective-permute-start.12 = (bf16[32,2048]{1,0:T(8,128)(2,1)S(1)}, bf16[32,2048]{1,0:T(8,128)(2,1)S(1)}, u32[]{:S(2)}, u32[]{:S(2)}) collective-permute-start(bf16[32,2048]{1,0:T(8,128)(2,1)S(1)} %broadcast_select_fusion), channel_id=1, source_target_pairs={{0,128},{128,0},{1,129},{129,1},{2,130},{130,2},{3,131},{131,3},{4... | collective-permute-start | bytes 393224 | tf_op jit(solution)/shard_map/ppermute | solution.py:14
  307.8 9.3 %all-to-all-start.7 = ((bf16[4,8,2048]{2,1,0:T(8,128)(2,1)}), bf16[4,8,2048]{2,1,0:T(8,128)(2,1)S(1)}, u32[]{:S(2)}, u32[]{:S(2)}) async-start(bf16[4,8,2048]{2,1,0:T(8,128)(2,1)} %fusion.6), calls=%async_computation.7 | async-start | bytes 262144 | tf_op jit(solution)/shard_map/all_to_all | solution.py:81

commit v3 on v1

v3 whole, which is shorter than its diff:
```python
import jax
import jax.numpy as jnp
from jax import lax
from jax.experimental import pallas as pl
from jax.experimental.pallas import tpu as pltpu
from jax.sharding import Mesh, PartitionSpec as P

damping = 0.1
Y, ZH, C, X = 4, 2, 2, 4
Z_BITS = ("z8", "z4", "z2", "z1")
RING = ("zh",) + Z_BITS
AXES = ("y", "zh", "c") + Z_BITS + ("x",)
f32, bf16 = jnp.float32, jnp.bfloat16
PARAMS = pltpu.CompilerParams(vmem_limit_bytes=16 * 2**20)
SCALAR = pl.BlockSpec(memory_space=pltpu.SMEM)
WHOLE = pl.BlockSpec(memory_space=pltpu.VMEM)
ARRIVAL = [0, 8, 4, 12, 2, 10, 6, 14, 1, 9, 5, 13, 3, 11, 7, 15]


def together(*values):
    return lax.optimization_barrier(values)


def swap(value, axis):
    return lax.ppermute(value, axis, [(0, 1), (1, 0)])


def around(value, hops):
    return lax.ppermute(value, RING, [(i, (i + hops) % 32) for i in range(32)])


def double_z(have, axis):
    return jnp.concatenate([have, swap(have, axis)], axis=0)


def project_kernel(z_ref, near_ref, far_ref, basis_ref, out_ref):
    z = z_ref[0]
    for pair in range(2):
        total = jnp.zeros((256, 256), f32)
        for step in range(8):
            source = near_ref if step < 4 else far_ref
            at = 2 * step if step < 4 else 2 * step - 8
            left = jnp.concatenate([source[at], source[at + 1]], axis=1)
            z0 = z ^ ARRIVAL[2 * step]
            z1 = z ^ ARRIVAL[2 * step + 1]
            columns = [
                jnp.concatenate([basis_ref[2 * pair + i, z0], basis_ref[2 * pair + i, z1]], axis=0) for i in range(2)
            ]
            right = jnp.concatenate(columns, axis=1)
            total = total + jnp.dot(left, right, preferred_element_type=f32)
        out_ref[2 * pair] = total[:, :128].astype(bf16)
        out_ref[2 * pair + 1] = total[:, 128:].astype(bf16)


def project(z, near, far, basis):
    return pl.pallas_call(
        project_kernel,
        out_shape=jax.ShapeDtypeStruct((X, 256, 128), bf16),
        in_specs=[SCALAR, WHOLE, WHOLE, WHOLE],
        out_specs=WHOLE,
        compiler_params=PARAMS,
        cost_estimate=pl.CostEstimate(flops=2 * 256 * 2048 * 512, bytes_accessed=3400000, transcendentals=0),
        name="project",
    )(z, near, far, basis)


def place_kernel(a_ref, *refs):
    *blocks, half_low, half_high, out_ref = refs
    for k, block in zip((0, 1, 2, 3, 5, 6, 7), blocks):
        out_ref[lax.rem(a_ref[0] + k, 8)] = block[...]
    far = lax.rem(a_ref[0] + 4, 8)
    out_ref[far, :128] = half_low[...]
    out_ref[far, 128:] = half_high[...]


def place(a, blocks, halves):
    return pl.pallas_call(
        place_kernel,
        out_shape=jax.ShapeDtypeStruct((8, 256, 128), bf16),
        in_specs=[SCALAR] + [WHOLE] * 9,
        out_specs=WHOLE,
        compiler_params=PARAMS,
        cost_estimate=pl.CostEstimate(flops=0, bytes_accessed=1100000, transcendentals=0),
        name="place",
    )(a, *blocks, *halves)


def scale_kernel(rows_ref, p0, p1, p2a, p2b, p3, out_ref):
    def block(j, at):
        if j == 2:
            return p2a[at] if at < 4 else p2b[at - 4]
        return {0: p0, 1: p1, 3: p3}[j][at]

    for j in range(4):
        for a in (0, 2):
            total = jnp.zeros((256, 256), f32)
            for h in range(2):
                right = jnp.concatenate([block(j, 4 * h + a), block(j, 4 * h + a + 1)], axis=1)
                total = total + jnp.dot(rows_ref[h], right, preferred_element_type=f32)
            total = total.astype(bf16)
            at = (4 * j + a) * 128
            out_ref[0, :, at : at + 256] = total[:128]
            out_ref[1, :, at : at + 256] = total[128:]


def scale_part(rows, p0, p1, p2a, p2b, p3):
    return pl.pallas_call(
        scale_kernel,
        out_shape=jax.ShapeDtypeStruct((C, 128, 2048), bf16),
        in_specs=[WHOLE] * 6,
        out_specs=WHOLE,
        compiler_params=PARAMS,
        cost_estimate=pl.CostEstimate(flops=2 * 256 * 512 * 2048, bytes_accessed=3300000, transcendentals=0),
        name="scale",
    )(rows, p0, p1, p2a, p2b, p3)


def exchange(value, axis):
    return lax.all_to_all(value, axis, split_axis=0, concat_axis=0, tiled=True)


def add_over(value, axis):
    return jnp.sum(exchange(value, axis).astype(f32), axis=0)


def squares(part):
    projected = add_over(part, "x")
    return (projected * projected).astype(bf16)


def per_device(activations, out_grads, basis_in, basis_out, grad_eigen):
    tokens = activations.shape[0]
    ring = lax.axis_index(RING)
    z = (ring % 16).astype(jnp.int32).reshape(1)
    high = lax.axis_index("zh") == 1

    def both(mine):
        kept = jnp.where(high, mine[1], mine[0])
        other = swap(jnp.where(high, mine[0], mine[1]), "zh")
        return jnp.stack([jnp.where(high, other, kept), jnp.where(high, kept, other)])

    basis_out = basis_out.reshape(16, X, 128, 128).transpose(1, 0, 2, 3)
    basis_in = basis_in.reshape(16, X, 128, 128).transpose(1, 0, 2, 3)

    z_out = double_z(out_grads[None], "z8")
    z_out, basis_out = together(z_out, basis_out)
    b_out = exchange(basis_out, "x")
    z_out = double_z(z_out, "z4")
    z_out, z_in = together(z_out, activations[None])
    z_out, z_in, b_out = together(double_z(z_out, "z2"), double_z(z_in, "z8"), b_out)
    z_out, basis_in = together(z_out, basis_in)
    b_in = exchange(basis_in, "x")
    far_out, z_out, z_in = together(swap(z_out, "z1"), z_out, double_z(z_in, "z4"))

    part_out = project(z, z_out, far_out, b_out)
    squares_out = squares(part_out)
    squares_out, z_in, b_in = together(squares_out, double_z(z_in, "z2"), b_in)

    up1, down1, far_in = around(squares_out, 4), around(squares_out, -4), swap(z_in, "z1")
    up1, down1, far_in, z_in = together(up1, down1, far_in, z_in)
    part_in = project(z, z_in, far_in, b_in)
    up2, down2 = around(up1, 4), around(down1, -4)
    squares_in = squares(part_in).T.reshape(Y, ZH, C * 8, tokens).transpose(1, 0, 2, 3)
    up2, down2, squares_in = together(up2, down2, squares_in)
    up3, down3 = around(up2, 4), around(down2, -4)
    rows_in = both(squares_in.reshape(ZH, 64, tokens))
    up3, down3, rows_in = together(up3, down3, rows_in)
    half_low, half_high = around(up3[:128], 4), around(down3[128:], -4)
    half_low, half_high, grad = together(half_low, half_high, grad_eigen)
    p0 = place(
        (ring // 4).astype(jnp.int32).reshape(1), (squares_out, down1, down2, down3, up3, up2, up1), (half_low, half_high)
    )
    p3, p1 = around(p0, 1), around(p0, -1)
    rows_in = lax.all_gather(rows_in, "x", axis=0, tiled=False)
    rows_in = rows_in.reshape(X, ZH, Y, C, 8, tokens).transpose(1, 3, 2, 0, 4, 5).reshape(ZH, 256, tokens)
    grad = both(grad.reshape(Y, ZH, C * 8, 512).transpose(1, 0, 2, 3))
    p3, p1, rows_in, grad = together(p3, p1, rows_in, grad)
    p2a, p2b = around(p1[:4], -1), around(p3[4:], 1)
    grad = grad.reshape(ZH, Y, C, 8, 512).transpose(1, 2, 0, 3, 4).reshape(Y * C, ZH, 8, 512)
    grad = exchange(grad, ("y", "c"))
    p2a, p2b, grad = together(p2a, p2b, grad)
    grad = grad.reshape(Y, C, ZH, 8, 512).transpose(3, 0, 2, 1, 4).reshape(8, 8192)

    partial = scale_part(rows_in, p0, p1, p2a, p2b, p3)
    partial = add_over(partial, "c").astype(bf16)
    summed = add_over(partial.reshape(Y, X * 8, 2048), "y").astype(bf16)
    rows = exchange(summed.reshape(X, 8, 2048), "x").reshape(X, 8, 4, 4, 128)
    rows = rows.transpose(1, 3, 2, 0, 4)
    odd, two = (ring % 2) == 1, ((ring // 2) % 2) == 1
    rows = jnp.where(odd, jnp.roll(rows, 1, axis=2), rows)
    rows = jnp.where(two, jnp.roll(rows, 2, axis=2), rows)
    rows = rows.reshape(8, 8192)

    scaling = rows.astype(f32) / (tokens * Y * ZH * C)
    return (grad.astype(f32) / (scaling + damping)).astype(bf16)


def solution(mesh):
    fine = Mesh(mesh.devices.reshape(Y, ZH, C, 2, 2, 2, 2, X), AXES)
    dp, mp = ("y", "zh", "c"), Z_BITS + ("x",)
    placed = (P(dp, mp), P(dp, mp), P(None, mp), P(None, mp), P(mp, dp))
    return jax.shard_map(
        per_device, mesh=fine, in_specs=placed, out_specs=P(mp + dp, None), check_vma=False
    )
```

time: 334 us -> 311 us (0.931)
  the two profiles are of different devices: /device:TPU:32 before, /device:TPU:1 now
where the time goes in v3:
time: 311 us; the launch traced here: 309 us
  starting transfers between devices  195 us (63%)
  waiting for transfers between devices  56.5 us (18%)
  blocking collectives  43.2 us (14%)
  local copies, waits for them, and re-layouts  7.01 us (2%)
  other arithmetic  3.93 us (1%)
    ppermute x10, starting transfers between devices, swap(): return lax.ppermute(value, axis, [(0, 1), (1, 0)])  123 us
    ppermute x12, starting transfers between devices, around(): return lax.ppermute(value, RING, [(i, (i + hops) % 32) for i in range(32)])  52.4 us
    all_to_all x3, blocking collectives, exchange(): return lax.all_to_all(value, axis, split_axis=0, concat_axis=0, tiled=True)  33.8 us
    all_to_all x5, waiting for transfers between devices, exchange(): return lax.all_to_all(value, axis, split_axis=0, concat_axis=0, tiled=True)  24.2 us
    ppermute x12, waiting for transfers between devices, around(): return lax.ppermute(value, RING, [(i, (i + hops) % 32) for i in range(32)])  22.5 us
    all_to_all x5, starting transfers between devices, exchange(): return lax.all_to_all(value, axis, split_axis=0, concat_axis=0, tiled=True)  19.3 us
    ppermute x10, waiting for transfers between devices, swap(): return lax.ppermute(value, axis, [(0, 1), (1, 0)])  9.9 us
    all_gather x1, blocking collectives, per_device(): rows_in = lax.all_gather(rows_in, 'x', axis=0, tiled=False)  9.39 us
  transfers between devices with their start and end apart: 27, of which 13 were waited for; matrix products, arithmetic and copies ran while one was open for 3% of the time, Pallas kernels for 0%

profile of v3, /device:TPU:1, one launch (start us, length us, event | category | flops | bytes accessed | tf_op | source)
XLA Modules:
  0.0 309.3 jit_solution(2822385959498897814)
XLA Ops:
  0.0 16.3 %collective-permute-start = (bf16[1,256,128]{2,1,0:T(8,128)(2,1)}, bf16[1,256,128]{2,1,0:T(8,128)(2,1)S(1)}, u32[]{:S(2)}, u32[]{:S(2)}) collective-permute-start(bf16[1,256,128]{2,1,0:T(8,128)(2,1)} %bitcast.90), channel_id=1, source_target_pairs={{0,32},{32,0},{1,33},{33,1},{2,34},{34,2},{3,35},{35,3},{4,36},{36... | collective-permute-start | bytes 196616 | tf_op jit(solution)/shard_map/ppermute | solution.py:25
  19.5 4.2 %all-to-all-start = ((bf16[4,16,128,128]{3,2,1,0:T(8,128)(2,1)}), bf16[4,16,128,128]{3,2,1,0:T(8,128)(2,1)S(1)}, u32[]{:S(2)}, u32[]{:S(2)}) async-start(bf16[4,16,128,128]{3,2,1,0:T(8,128)(2,1)} %bitcast.75), calls=%async_computation | async-start | bytes 4194304 | tf_op jit(solution)/shard_map/all_to_all | solution.py:119
  23.6 11.7 %collective-permute-start.1 = (bf16[2,256,128]{2,1,0:T(8,128)(2,1)S(1)}, bf16[2,256,128]{2,1,0:T(8,128)(2,1)S(1)}, u32[]{:S(2)}, u32[]{:S(2)}) collective-permute-start(bf16[2,256,128]{2,1,0:T(8,128)(2,1)S(1)} %pad_maximum_fusion.4), channel_id=1, source_target_pairs={{0,16},{16,0},{1,17},{17,1},{2,18},{18,2},{3,19},{19,3},{4,20},{20... | collective-permute-start | bytes 393224 | tf_op jit(solution)/shard_map/ppermute | solution.py:25
  37.7 10.5 %collective-permute-start.2 = (bf16[4,256,128]{2,1,0:T(8,128)(2,1)S(1)}, bf16[4,256,128]{2,1,0:T(8,128)(2,1)S(1)}, u32[]{:S(2)}, u32[]{:S(2)}) collective-permute-start(bf16[4,256,128]{2,1,0:T(8,128)(2,1)S(1)} %pad_maximum_fusion.2), channel_id=1, source_target_pairs={{0,8},{8,0},{1,9},{9,1},{2,10},{10,2},{3,11},{11,3},{4,12},{12,4},... | collective-permute-start | bytes 786440 | tf_op jit(solution)/shard_map/ppermute | solution.py:25
  48.2 12.7 %collective-permute-start.3 = (bf16[1,256,128]{2,1,0:T(8,128)(2,1)S(1)}, bf16[1,256,128]{2,1,0:T(8,128)(2,1)S(1)}, u32[]{:S(2)}, u32[]{:S(2)}) collective-permute-start(bf16[1,256,128]{2,1,0:T(8,128)(2,1)S(1)} %bitcast.92), channel_id=1, source_target_pairs={{0,32},{32,0},{1,33},{33,1},{2,34},{34,2},{3,35},{35,3},{4,36},{36... | collective-permute-start | bytes 196616 | tf_op jit(solution)/shard_map/ppermute | solution.py:25
  64.2 5.9 %collective-permute-start.4 = (bf16[8,256,128]{2,1,0:T(8,128)(2,1)S(1)}, bf16[8,256,128]{2,1,0:T(8,128)(2,1)S(1)}, u32[]{:S(2)}, u32[]{:S(2)}) collective-permute-start(bf16[8,256,128]{2,1,0:T(8,128)(2,1)S(1)} %pad_maximum_fusion.near_ref), channel_id=1, source_target_pairs={{0,4},{4,0},{1,5},{5,1},{2,6},{6,2},{3,7},{7,3},{8,12},{12,8},{9,1... | collective-permute-start | bytes 1572872 | tf_op jit(solution)/shard_map/ppermute | solution.py:25
  70.1 9.5 %collective-permute-start.5 = (bf16[2,256,128]{2,1,0:T(8,128)(2,1)S(1)}, bf16[2,256,128]{2,1,0:T(8,128)(2,1)}, u32[]{:S(2)}, u32[]{:S(2)}) collective-permute-start(bf16[2,256,128]{2,1,0:T(8,128)(2,1)S(1)} %pad_maximum_fusion.5), channel_id=1, source_target_pairs={{0,16},{16,0},{1,17},{17,1},{2,18},{18,2},{3,19},{19,3},{4,20},{20... | collective-permute-start | bytes 393224 | tf_op jit(solution)/shard_map/ppermute | solution.py:25
  84.8 9.6 %all_to_all.40 = bf16[4,256,128]{2,1,0:T(8,128)(2,1)S(1)} all-to-all(bf16[4,256,128]{2,1,0:T(8,128)(2,1)S(1)} %project.2), channel_id=1, replica_groups=mesh['y'=4,'zh'=2,'c'=2,'z8'=2,'z4'=2,'z2'=2,'z1'=2,'x'=4] {'x'}, dimensions={0} | all-to-all | bytes 524288 | tf_op jit(solution)/shard_map/all_to_all | solution.py:119
  94.4 3.6 %all-to-all-start.2 = ((bf16[4,16,128,128]{3,2,1,0:T(8,128)(2,1)}), bf16[4,16,128,128]{3,2,1,0:T(8,128)(2,1)S(1)}, u32[]{:S(2)}, u32[]{:S(2)}) async-start(bf16[4,16,128,128]{3,2,1,0:T(8,128)(2,1)} %bitcast.74), calls=%async_computation.2 | async-start | bytes 4194304 | tf_op jit(solution)/shard_map/all_to_all | solution.py:119
  98.0 8.3 %collective-permute-start.6 = (bf16[4,256,128]{2,1,0:T(8,128)(2,1)S(1)}, bf16[4,256,128]{2,1,0:T(8,128)(2,1)S(1)}, u32[]{:S(2)}, u32[]{:S(2)}) collective-permute-start(bf16[4,256,128]{2,1,0:T(8,128)(2,1)S(1)} %pad_maximum_fusion.3), channel_id=1, source_target_pairs={{0,8},{8,0},{1,9},{9,1},{2,10},{10,2},{3,11},{11,3},{4,12},{12,4},... | collective-permute-start | bytes 786440 | tf_op jit(solution)/shard_map/ppermute | solution.py:25
  106.3 4.0 %collective-permute-done.6 = bf16[4,256,128]{2,1,0:T(8,128)(2,1)S(1)} collective-permute-done((bf16[4,256,128]{2,1,0:T(8,128)(2,1)S(1)}, bf16[4,256,128]{2,1,0:T(8,128)(2,1)S(1)}, u32[]{:S(2)}, u32[]{:S(2)}) %collective-permute-start.6) | collective-permute-done | bytes 262176 | tf_op jit(solution)/shard_map/ppermute | solution.py:25
  110.4 10.6 %all-to-all-done.2.basis_ref = bf16[4,16,128,128]{3,2,1,0:T(8,128)(2,1)S(1)} async-done(((bf16[4,16,128,128]{3,2,1,0:T(8,128)(2,1)}), bf16[4,16,128,128]{3,2,1,0:T(8,128)(2,1)S(1)}, u32[]{:S(2)}, u32[]{:S(2)}) %all-to-all-start.2) | async-done | bytes 2097184 | tf_op jit(solution)/shard_map/all_to_all | solution.py:119
  121.0 14.0 %collective-permute-start.9 = (bf16[8,256,128]{2,1,0:T(8,128)(2,1)S(1)}, bf16[8,256,128]{2,1,0:T(8,128)(2,1)S(1)}, u32[]{:S(2)}, u32[]{:S(2)}) collective-permute-start(bf16[8,256,128]{2,1,0:T(8,128)(2,1)S(1)} %pad_maximum_fusion.1.near_ref), channel_id=1, source_target_pairs={{0,4},{4,0},{1,5},{5,1},{2,6},{6,2},{3,7},{7,3},{8,12},{12,8},{9,1... | collective-permute-start | bytes 1572872 | tf_op jit(solution)/shard_map/ppermute | solution.py:25
  138.5 6.9 %collective-permute-start.8 = (bf16[256,128]{1,0:T(8,128)(2,1)S(1)}, bf16[256,128]{1,0:T(8,128)(2,1)S(1)}, u32[]{:S(2)}, u32[]{:S(2)}) collective-permute-start(bf16[256,128]{1,0:T(8,128)(2,1)S(1)} %multiply_convert_fusion.1.refs_0_), channel_id=1, source_target_pairs={{0,176},{4,180},{8,184},{12,188},{16,0},{20,4},{24,8},{28,12},{32,... | collective-permute-start | bytes 196616 | tf_op jit(solution)/shard_map/ppermute | solution.py:29
  145.5 4.3 %collective-permute-done.7.refs_6_ = bf16[256,128]{1,0:T(8,128)(2,1)S(1)} collective-permute-done((bf16[256,128]{1,0:T(8,128)(2,1)S(1)}, bf16[256,128]{1,0:T(8,128)(2,1)S(1)}, u32[]{:S(2)}, u32[]{:S(2)}) %collective-permute-start.7) | collective-permute-done | bytes 65568 | tf_op jit(solution)/shard_map/ppermute | solution.py:29
  149.7 5.8 %collective-permute-done.8.refs_1_ = bf16[256,128]{1,0:T(8,128)(2,1)S(1)} collective-permute-done((bf16[256,128]{1,0:T(8,128)(2,1)S(1)}, bf16[256,128]{1,0:T(8,128)(2,1)S(1)}, u32[]{:S(2)}, u32[]{:S(2)}) %collective-permute-start.8) | collective-permute-done | bytes 65568 | tf_op jit(solution)/shard_map/ppermute | solution.py:29
  157.0 3.5 %all-to-all-start.3 = ((bf16[4,256,128]{2,1,0:T(8,128)(2,1)}), bf16[4,256,128]{2,1,0:T(8,128)(2,1)S(1)}, u32[]{:S(2)}, u32[]{:S(2)}) async-start(bf16[4,256,128]{2,1,0:T(8,128)(2,1)} %project.3), calls=%async_computation.3 | async-start | bytes 524288 | tf_op jit(solution)/shard_map/all_to_all | solution.py:119
  160.5 7.4 %collective-permute-start.10 = (bf16[256,128]{1,0:T(8,128)(2,1)S(1)}, bf16[256,128]{1,0:T(8,128)(2,1)S(1)}, u32[]{:S(2)}, u32[]{:S(2)}) collective-permute-start(bf16[256,128]{1,0:T(8,128)(2,1)S(1)} %collective-permute-done.7.refs_6_), channel_id=1, source_target_pairs={{0,16},{4,20},{8,24},{12,28},{16,32},{20,36},{24,40},{28,44},{32,4... | collective-permute-start | bytes 196616 | tf_op jit(solution)/shard_map/ppermute | solution.py:29
  170.0 8.4 %collective-permute-done.11.refs_2_ = bf16[256,128]{1,0:T(8,128)(2,1)S(1)} collective-permute-done((bf16[256,128]{1,0:T(8,128)(2,1)S(1)}, bf16[256,128]{1,0:T(8,128)(2,1)S(1)}, u32[]{:S(2)}, u32[]{:S(2)}) %collective-permute-start.11) | collective-permute-done | bytes 65568 | tf_op jit(solution)/shard_map/ppermute | solution.py:29
  178.4 18.6 %collective-permute-start.14 = (bf16[64,256]{1,0:T(8,128)(2,1)S(1)}, bf16[64,256]{1,0:T(8,128)(2,1)S(1)}, u32[]{:S(2)}, u32[]{:S(2)}) collective-permute-start(bf16[64,256]{1,0:T(8,128)(2,1)S(1)} %bitcast.94), channel_id=1, source_target_pairs={{0,128},{128,0},{1,129},{129,1},{2,130},{130,2},{3,131},{131,3},{4... | collective-permute-start | bytes 98312 | tf_op jit(solution)/shard_map/ppermute | solution.py:25
  198.9 7.3 %collective-permute-start.13 = (bf16[256,128]{1,0:T(8,128)(2,1)S(1)}, bf16[256,128]{1,0:T(8,128)(2,1)S(1)}, u32[]{:S(2)}, u32[]{:S(2)}) collective-permute-start(bf16[256,128]{1,0:T(8,128)(2,1)S(1)} %collective-permute-done.11.refs_2_), channel_id=1, source_target_pairs={{0,176},{4,180},{8,184},{12,188},{16,0},{20,4},{24,8},{28,12},{32,... | collective-permute-start | bytes 196616 | tf_op jit(solution)/shard_map/ppermute | solution.py:29
  210.9 7.0 %collective-permute-start.16 = (bf16[128,128]{1,0:T(8,128)(2,1)S(1)}, bf16[128,128]{1,0:T(8,128)(2,1)S(1)}, u32[]{:S(2)}, u32[]{:S(2)}) collective-permute-start(bf16[128,128]{1,0:T(8,128)(2,1)S(1)} %slice.49), channel_id=1, source_target_pairs={{0,176},{4,180},{8,184},{12,188},{16,0},{20,4},{24,8},{28,12},{32,... | collective-permute-start | bytes 98312 | tf_op jit(solution)/shard_map/ppermute | solution.py:29
  221.5 4.6 %collective-permute-start.18 = (bf16[8,256,128]{2,1,0:T(8,128)(2,1)S(1)}, bf16[8,256,128]{2,1,0:T(8,128)(2,1)S(1)}, u32[]{:S(2)}, u32[]{:S(2)}) collective-permute-start(bf16[8,256,128]{2,1,0:T(8,128)(2,1)S(1)} %place.1.p0), channel_id=1, source_target_pairs={{0,188},{4,0},{8,4},{12,8},{16,12},{20,16},{24,20},{28,24},{32,28}... | collective-permute-start | bytes 1572872 | tf_op jit(solution)/shard_map/ppermute | solution.py:29
  226.1 16.0 %collective-permute-start.19 = (bf16[4,16,512]{2,1,0:T(8,128)(2,1)S(1)}, bf16[4,16,512]{2,1,0:T(8,128)(2,1)S(1)}, u32[]{:S(2)}, u32[]{:S(2)}) collective-permute-start(bf16[4,16,512]{2,1,0:T(8,128)(2,1)S(1)} %fusion.2), channel_id=1, source_target_pairs={{0,128},{128,0},{1,129},{129,1},{2,130},{130,2},{3,131},{131,3},{4... | collective-permute-start | bytes 196616 | tf_op jit(solution)/shard_map/ppermute | solution.py:25
  242.1 9.4 %all-gather = bf16[8,64,256]{2,1,0:T(8,128)(2,1)S(1)} all-gather(bf16[2,64,256]{2,1,0:T(8,128)(2,1)S(1)} %pad_maximum_fusion.7), channel_id=2, replica_groups=mesh['y'=4,'zh'=2,'c'=2,'z8'=2,'z4'=2,'z2'=2,'z1'=2,'x'=4] {'x'}, dimensions={0}, use_global_device_ids=true | all-gather | bytes 327680 | tf_op jit(solution)/shard_map/all_gather | solution.py:174
  251.6 5.9 %collective-permute-start.20 = (bf16[4,256,128]{2,1,0:T(8,128)(2,1)S(1)}, bf16[4,256,128]{2,1,0:T(8,128)(2,1)S(1)}, u32[]{:S(2)}, u32[]{:S(2)}) collective-permute-start(bf16[4,256,128]{2,1,0:T(8,128)(2,1)S(1)} %slice.52), channel_id=1, source_target_pairs={{0,188},{4,0},{8,4},{12,8},{16,12},{20,16},{24,20},{28,24},{32,28}... | collective-permute-start | bytes 786440 | tf_op jit(solution)/shard_map/ppermute | solution.py:29
  259.5 19.2 %all_to_all.41 = bf16[8,2,8,512]{3,2,1,0:T(8,128)(2,1)S(1)} all-to-all(bf16[8,2,8,512]{3,2,1,0:T(8,128)(2,1)S(1)} %copy.52), channel_id=1, replica_groups=mesh['y'=4,'zh'=2,'c'=2,'z8'=2,'z4'=2,'z2'=2,'z1'=2,'x'=4] {'y','c'}, dimensions={0} | all-to-all | bytes 262144 | tf_op jit(solution)/shard_map/all_to_all | solution.py:119
  279.4 5.1 %all_to_all.42 = bf16[2,128,2048]{2,1,0:T(8,128)(2,1)S(1)} all-to-all(bf16[2,128,2048]{2,1,0:T(8,128)(2,1)S(1)} %scale.1), channel_id=1, replica_groups=mesh['y'=4,'zh'=2,'c'=2,'z8'=2,'z4'=2,'z2'=2,'z1'=2,'x'=4] {'c'}, dimensions={0} | all-to-all | bytes 2097152 | tf_op jit(solution)/shard_map/all_to_all | solution.py:119
  285.6 3.5 %all-to-all-start.6 = ((bf16[4,32,2048]{2,1,0:T(8,128)(2,1)}), bf16[4,32,2048]{2,1,0:T(8,128)(2,1)S(1)}, u32[]{:S(2)}, u32[]{:S(2)}) async-start(bf16[4,32,2048]{2,1,0:T(8,128)(2,1)} %bitcast.33), calls=%async_computation.6 | async-start | bytes 1048576 | tf_op jit(solution)/shard_map/all_to_all | solution.py:119
  289.1 9.2 %all-to-all-done.6 = bf16[4,32,2048]{2,1,0:T(8,128)(2,1)S(1)} async-done(((bf16[4,32,2048]{2,1,0:T(8,128)(2,1)}), bf16[4,32,2048]{2,1,0:T(8,128)(2,1)S(1)}, u32[]{:S(2)}, u32[]{:S(2)}) %all-to-all-start.6) | async-done | bytes 524320 | tf_op jit(solution)/shard_map/all_to_all | solution.py:119
  299.0 4.6 %all-to-all-start.7 = ((bf16[4,8,2048]{2,1,0:T(8,128)(2,1)}), bf16[4,8,2048]{2,1,0:T(8,128)(2,1)S(1)}, u32[]{:S(2)}, u32[]{:S(2)}) async-start(bf16[4,8,2048]{2,1,0:T(8,128)(2,1)} %bitcast.34), calls=%async_computation.7 | async-start | bytes 262144 | tf_op jit(solution)/shard_map/all_to_all | solution.py:119
  304.0 4.4 %all-to-all-done.7 = bf16[4,8,2048]{2,1,0:T(8,128)(2,1)S(1)} async-done(((bf16[4,8,2048]{2,1,0:T(8,128)(2,1)}), bf16[4,8,2048]{2,1,0:T(8,128)(2,1)S(1)}, u32[]{:S(2)}, u32[]{:S(2)}) %all-to-all-start.7) | async-done | bytes 131104 | tf_op jit(solution)/shard_map/all_to_all | solution.py:119
  (73 shorter events, 37.0 us)
Async XLA Ops:
  0.0 19.4 %collective-permute-start = (bf16[1,256,128]{2,1,0:T(8,128)(2,1)}, bf16[1,256,128]{2,1,0:T(8,128)(2,1)S(1)}, u32[]{:S(2)}, u32[]{:S(2)}) collective-permute-start(bf16[1,256,128]{2,1,0:T(8,128)(2,1)} %bitcast.90), channel_id=1, source_target_pairs={{0,32},{32,0},{1,33},{33,1},{2,34},{34,2},{3,35},{35,3},{4,36},{36... | collective-permute-start | bytes 196616 | tf_op jit(solution)/shard_map/ppermute | solution.py:25
  16.3 3.2 %copy-start.1 = (bf16[256,128]{1,0:T(8,128)(2,1)S(1)}, bf16[256,128]{1,0:T(8,128)(2,1)}, u32[]{:S(2)}) copy-start(bf16[256,128]{1,0:T(8,128)(2,1)} %param.6) | copy-start | bytes 196612
  19.5 28.7 %copy-start.2 = (bf16[256,128]{1,0:T(8,128)(2,1)S(1)}, bf16[256,128]{1,0:T(8,128)(2,1)}, u32[]{:S(2)}) copy-start(bf16[256,128]{1,0:T(8,128)(2,1)} %param.5) | copy-start | bytes 196612
  19.5 44.7 %all-to-all-start = ((bf16[4,16,128,128]{3,2,1,0:T(8,128)(2,1)}), bf16[4,16,128,128]{3,2,1,0:T(8,128)(2,1)S(1)}, u32[]{:S(2)}, u32[]{:S(2)}) async-start(bf16[4,16,128,128]{3,2,1,0:T(8,128)(2,1)} %bitcast.75), calls=%async_computation | async-start | bytes 4194304 | tf_op jit(solution)/shard_map/all_to_all | solution.py:119
  23.6 14.0 %collective-permute-start.1 = (bf16[2,256,128]{2,1,0:T(8,128)(2,1)S(1)}, bf16[2,256,128]{2,1,0:T(8,128)(2,1)S(1)}, u32[]{:S(2)}, u32[]{:S(2)}) collective-permute-start(bf16[2,256,128]{2,1,0:T(8,128)(2,1)S(1)} %pad_maximum_fusion.4), channel_id=1, source_target_pairs={{0,16},{16,0},{1,17},{17,1},{2,18},{18,2},{3,19},{19,3},{4,20},{20... | collective-permute-start | bytes 393224 | tf_op jit(solution)/shard_map/ppermute | solution.py:25
  37.7 26.4 %collective-permute-start.2 = (bf16[4,256,128]{2,1,0:T(8,128)(2,1)S(1)}, bf16[4,256,128]{2,1,0:T(8,128)(2,1)S(1)}, u32[]{:S(2)}, u32[]{:S(2)}) collective-permute-start(bf16[4,256,128]{2,1,0:T(8,128)(2,1)S(1)} %pad_maximum_fusion.2), channel_id=1, source_target_pairs={{0,8},{8,0},{1,9},{9,1},{2,10},{10,2},{3,11},{11,3},{4,12},{12,4},... | collective-permute-start | bytes 786440 | tf_op jit(solution)/shard_map/ppermute | solution.py:25
  48.2 15.9 %collective-permute-start.3 = (bf16[1,256,128]{2,1,0:T(8,128)(2,1)S(1)}, bf16[1,256,128]{2,1,0:T(8,128)(2,1)S(1)}, u32[]{:S(2)}, u32[]{:S(2)}) collective-permute-start(bf16[1,256,128]{2,1,0:T(8,128)(2,1)S(1)} %bitcast.92), channel_id=1, source_target_pairs={{0,32},{32,0},{1,33},{33,1},{2,34},{34,2},{3,35},{35,3},{4,36},{36... | collective-permute-start | bytes 196616 | tf_op jit(solution)/shard_map/ppermute | solution.py:25
  64.2 19.9 %collective-permute-start.4 = (bf16[8,256,128]{2,1,0:T(8,128)(2,1)S(1)}, bf16[8,256,128]{2,1,0:T(8,128)(2,1)S(1)}, u32[]{:S(2)}, u32[]{:S(2)}) collective-permute-start(bf16[8,256,128]{2,1,0:T(8,128)(2,1)S(1)} %pad_maximum_fusion.near_ref), channel_id=1, source_target_pairs={{0,4},{4,0},{1,5},{5,1},{2,6},{6,2},{3,7},{7,3},{8,12},{12,8},{9,1... | collective-permute-start | bytes 1572872 | tf_op jit(solution)/shard_map/ppermute | solution.py:25
  70.1 13.0 %collective-permute-start.5 = (bf16[2,256,128]{2,1,0:T(8,128)(2,1)S(1)}, bf16[2,256,128]{2,1,0:T(8,128)(2,1)}, u32[]{:S(2)}, u32[]{:S(2)}) collective-permute-start(bf16[2,256,128]{2,1,0:T(8,128)(2,1)S(1)} %pad_maximum_fusion.5), channel_id=1, source_target_pairs={{0,16},{16,0},{1,17},{17,1},{2,18},{18,2},{3,19},{19,3},{4,20},{20... | collective-permute-start | bytes 393224 | tf_op jit(solution)/shard_map/ppermute | solution.py:25
  94.4 26.7 %all-to-all-start.2 = ((bf16[4,16,128,128]{3,2,1,0:T(8,128)(2,1)}), bf16[4,16,128,128]{3,2,1,0:T(8,128)(2,1)S(1)}, u32[]{:S(2)}, u32[]{:S(2)}) async-start(bf16[4,16,128,128]{3,2,1,0:T(8,128)(2,1)} %bitcast.74), calls=%async_computation.2 | async-start | bytes 4194304 | tf_op jit(solution)/shard_map/all_to_all | solution.py:119
  98.0 12.3 %collective-permute-start.6 = (bf16[4,256,128]{2,1,0:T(8,128)(2,1)S(1)}, bf16[4,256,128]{2,1,0:T(8,128)(2,1)S(1)}, u32[]{:S(2)}, u32[]{:S(2)}) collective-permute-start(bf16[4,256,128]{2,1,0:T(8,128)(2,1)S(1)} %pad_maximum_fusion.3), channel_id=1, source_target_pairs={{0,8},{8,0},{1,9},{9,1},{2,10},{10,2},{3,11},{11,3},{4,12},{12,4},... | collective-permute-start | bytes 786440 | tf_op jit(solution)/shard_map/ppermute | solution.py:25
  121.0 34.6 %collective-permute-start.9 = (bf16[8,256,128]{2,1,0:T(8,128)(2,1)S(1)}, bf16[8,256,128]{2,1,0:T(8,128)(2,1)S(1)}, u32[]{:S(2)}, u32[]{:S(2)}) collective-permute-start(bf16[8,256,128]{2,1,0:T(8,128)(2,1)S(1)} %pad_maximum_fusion.1.near_ref), channel_id=1, source_target_pairs={{0,4},{4,0},{1,5},{5,1},{2,6},{6,2},{3,7},{7,3},{8,12},{12,8},{9,1... | collective-permute-start | bytes 1572872 | tf_op jit(solution)/shard_map/ppermute | solution.py:25
  135.0 14.7 %collective-permute-start.7 = (bf16[256,128]{1,0:T(8,128)(2,1)S(1)}, bf16[256,128]{1,0:T(8,128)(2,1)S(1)}, u32[]{:S(2)}, u32[]{:S(2)}) collective-permute-start(bf16[256,128]{1,0:T(8,128)(2,1)S(1)} %multiply_convert_fusion.1.refs_0_), channel_id=1, source_target_pairs={{0,16},{4,20},{8,24},{12,28},{16,32},{20,36},{24,40},{28,44},{32,4... | collective-permute-start | bytes 196616 | tf_op jit(solution)/shard_map/ppermute | solution.py:29
  138.5 17.0 %collective-permute-start.8 = (bf16[256,128]{1,0:T(8,128)(2,1)S(1)}, bf16[256,128]{1,0:T(8,128)(2,1)S(1)}, u32[]{:S(2)}, u32[]{:S(2)}) collective-permute-start(bf16[256,128]{1,0:T(8,128)(2,1)S(1)} %multiply_convert_fusion.1.refs_0_), channel_id=1, source_target_pairs={{0,176},{4,180},{8,184},{12,188},{16,0},{20,4},{24,8},{28,12},{32,... | collective-permute-start | bytes 196616 | tf_op jit(solution)/shard_map/ppermute | solution.py:29
  157.0 69.1 %copy-start = (bf16[128,512]{1,0:T(8,128)(2,1)S(1)}, bf16[128,512]{1,0:T(8,128)(2,1)}, u32[]{:S(2)}) copy-start(bf16[128,512]{1,0:T(8,128)(2,1)} %param.9) | copy-start | bytes 393220
  157.0 12.9 %all-to-all-start.3 = ((bf16[4,256,128]{2,1,0:T(8,128)(2,1)}), bf16[4,256,128]{2,1,0:T(8,128)(2,1)S(1)}, u32[]{:S(2)}, u32[]{:S(2)}) async-start(bf16[4,256,128]{2,1,0:T(8,128)(2,1)} %project.3), calls=%async_computation.3 | async-start | bytes 524288 | tf_op jit(solution)/shard_map/all_to_all | solution.py:119
  160.5 9.5 %collective-permute-start.10 = (bf16[256,128]{1,0:T(8,128)(2,1)S(1)}, bf16[256,128]{1,0:T(8,128)(2,1)S(1)}, u32[]{:S(2)}, u32[]{:S(2)}) collective-permute-start(bf16[256,128]{1,0:T(8,128)(2,1)S(1)} %collective-permute-done.7.refs_6_), channel_id=1, source_target_pairs={{0,16},{4,20},{8,24},{12,28},{16,32},{20,36},{24,40},{28,44},{32,4... | collective-permute-start | bytes 196616 | tf_op jit(solution)/shard_map/ppermute | solution.py:29
  167.9 10.5 %collective-permute-start.11 = (bf16[256,128]{1,0:T(8,128)(2,1)S(1)}, bf16[256,128]{1,0:T(8,128)(2,1)S(1)}, u32[]{:S(2)}, u32[]{:S(2)}) collective-permute-start(bf16[256,128]{1,0:T(8,128)(2,1)S(1)} %collective-permute-done.8.refs_1_), channel_id=1, source_target_pairs={{0,176},{4,180},{8,184},{12,188},{16,0},{20,4},{24,8},{28,12},{32,... | collective-permute-start | bytes 196616 | tf_op jit(solution)/shard_map/ppermute | solution.py:29
  178.4 27.8 %collective-permute-start.14 = (bf16[64,256]{1,0:T(8,128)(2,1)S(1)}, bf16[64,256]{1,0:T(8,128)(2,1)S(1)}, u32[]{:S(2)}, u32[]{:S(2)}) collective-permute-start(bf16[64,256]{1,0:T(8,128)(2,1)S(1)} %bitcast.94), channel_id=1, source_target_pairs={{0,128},{128,0},{1,129},{129,1},{2,130},{130,2},{3,131},{131,3},{4... | collective-permute-start | bytes 98312 | tf_op jit(solution)/shard_map/ppermute | solution.py:25
  197.0 11.0 %collective-permute-start.12 = (bf16[256,128]{1,0:T(8,128)(2,1)S(1)}, bf16[256,128]{1,0:T(8,128)(2,1)S(1)}, u32[]{:S(2)}, u32[]{:S(2)}) collective-permute-start(bf16[256,128]{1,0:T(8,128)(2,1)S(1)} %collective-permute-done.10.refs_5_), channel_id=1, source_target_pairs={{0,16},{4,20},{8,24},{12,28},{16,32},{20,36},{24,40},{28,44},{32,4... | collective-permute-start | bytes 196616 | tf_op jit(solution)/shard_map/ppermute | solution.py:29
  198.9 9.8 %collective-permute-start.13 = (bf16[256,128]{1,0:T(8,128)(2,1)S(1)}, bf16[256,128]{1,0:T(8,128)(2,1)S(1)}, u32[]{:S(2)}, u32[]{:S(2)}) collective-permute-start(bf16[256,128]{1,0:T(8,128)(2,1)S(1)} %collective-permute-done.11.refs_2_), channel_id=1, source_target_pairs={{0,176},{4,180},{8,184},{12,188},{16,0},{20,4},{24,8},{28,12},{32,... | collective-permute-start | bytes 196616 | tf_op jit(solution)/shard_map/ppermute | solution.py:29
  208.7 9.2 %collective-permute-start.15 = (bf16[128,128]{1,0:T(8,128)(2,1)S(1)}, bf16[128,128]{1,0:T(8,128)(2,1)S(1)}, u32[]{:S(2)}, u32[]{:S(2)}) collective-permute-start(bf16[128,128]{1,0:T(8,128)(2,1)S(1)} %slice.48), channel_id=1, source_target_pairs={{0,16},{4,20},{8,24},{12,28},{16,32},{20,36},{24,40},{28,44},{32,4... | collective-permute-start | bytes 98312 | tf_op jit(solution)/shard_map/ppermute | solution.py:29
  210.9 8.6 %collective-permute-start.16 = (bf16[128,128]{1,0:T(8,128)(2,1)S(1)}, bf16[128,128]{1,0:T(8,128)(2,1)S(1)}, u32[]{:S(2)}, u32[]{:S(2)}) collective-permute-start(bf16[128,128]{1,0:T(8,128)(2,1)S(1)} %slice.49), channel_id=1, source_target_pairs={{0,176},{4,180},{8,184},{12,188},{16,0},{20,4},{24,8},{28,12},{32,... | collective-permute-start | bytes 98312 | tf_op jit(solution)/shard_map/ppermute | solution.py:29
  219.5 32.0 %collective-permute-start.17 = (bf16[8,256,128]{2,1,0:T(8,128)(2,1)S(1)}, bf16[8,256,128]{2,1,0:T(8,128)(2,1)S(1)}, u32[]{:S(2)}, u32[]{:S(2)}) collective-permute-start(bf16[8,256,128]{2,1,0:T(8,128)(2,1)S(1)} %place.1.p0), channel_id=1, source_target_pairs={{0,4},{4,8},{8,12},{12,16},{16,20},{20,24},{24,28},{28,32},{32,36}... | collective-permute-start | bytes 1572872 | tf_op jit(solution)/shard_map/ppermute | solution.py:29
  221.5 30.1 %collective-permute-start.18 = (bf16[8,256,128]{2,1,0:T(8,128)(2,1)S(1)}, bf16[8,256,128]{2,1,0:T(8,128)(2,1)S(1)}, u32[]{:S(2)}, u32[]{:S(2)}) collective-permute-start(bf16[8,256,128]{2,1,0:T(8,128)(2,1)S(1)} %place.1.p0), channel_id=1, source_target_pairs={{0,188},{4,0},{8,4},{12,8},{16,12},{20,16},{24,20},{28,24},{32,28}... | collective-permute-start | bytes 1572872 | tf_op jit(solution)/shard_map/ppermute | solution.py:29
  226.1 25.4 %collective-permute-start.19 = (bf16[4,16,512]{2,1,0:T(8,128)(2,1)S(1)}, bf16[4,16,512]{2,1,0:T(8,128)(2,1)S(1)}, u32[]{:S(2)}, u32[]{:S(2)}) collective-permute-start(bf16[4,16,512]{2,1,0:T(8,128)(2,1)S(1)} %fusion.2), channel_id=1, source_target_pairs={{0,128},{128,0},{1,129},{129,1},{2,130},{130,2},{3,131},{131,3},{4... | collective-permute-start | bytes 196616 | tf_op jit(solution)/shard_map/ppermute | solution.py:25
  251.6 27.1 %collective-permute-start.20 = (bf16[4,256,128]{2,1,0:T(8,128)(2,1)S(1)}, bf16[4,256,128]{2,1,0:T(8,128)(2,1)S(1)}, u32[]{:S(2)}, u32[]{:S(2)}) collective-permute-start(bf16[4,256,128]{2,1,0:T(8,128)(2,1)S(1)} %slice.52), channel_id=1, source_target_pairs={{0,188},{4,0},{8,4},{12,8},{16,12},{20,16},{24,20},{28,24},{32,28}... | collective-permute-start | bytes 786440 | tf_op jit(solution)/shard_map/ppermute | solution.py:29
  257.6 21.1 %collective-permute-start.21 = (bf16[4,256,128]{2,1,0:T(8,128)(2,1)S(1)}, bf16[4,256,128]{2,1,0:T(8,128)(2,1)S(1)}, u32[]{:S(2)}, u32[]{:S(2)}) collective-permute-start(bf16[4,256,128]{2,1,0:T(8,128)(2,1)S(1)} %slice.53), channel_id=1, source_target_pairs={{0,4},{4,8},{8,12},{12,16},{16,20},{20,24},{24,28},{28,32},{32,36}... | collective-permute-start | bytes 786440 | tf_op jit(solution)/shard_map/ppermute | solution.py:29
  285.6 12.7 %all-to-all-start.6 = ((bf16[4,32,2048]{2,1,0:T(8,128)(2,1)}), bf16[4,32,2048]{2,1,0:T(8,128)(2,1)S(1)}, u32[]{:S(2)}, u32[]{:S(2)}) async-start(bf16[4,32,2048]{2,1,0:T(8,128)(2,1)} %bitcast.33), calls=%async_computation.6 | async-start | bytes 1048576 | tf_op jit(solution)/shard_map/all_to_all | solution.py:119
  299.0 9.4 %all-to-all-start.7 = ((bf16[4,8,2048]{2,1,0:T(8,128)(2,1)}), bf16[4,8,2048]{2,1,0:T(8,128)(2,1)S(1)}, u32[]{:S(2)}, u32[]{:S(2)}) async-start(bf16[4,8,2048]{2,1,0:T(8,128)(2,1)} %bitcast.34), calls=%async_computation.7 | async-start | bytes 262144 | tf_op jit(solution)/shard_map/all_to_all | solution.py:119

commit v4 on v3

v4 whole, which is shorter than its diff:
```python
import jax
import jax.numpy as jnp
from jax import lax
from jax.experimental import pallas as pl
from jax.experimental.pallas import tpu as pltpu
from jax.sharding import Mesh, PartitionSpec as P

damping = 0.1
Y, ZH, C, X = 4, 2, 2, 4
Z_BITS = ("z8", "z4", "z2", "z1")
RING = ("zh",) + Z_BITS
AXES = ("y", "zh", "c") + Z_BITS + ("x",)
f32, bf16 = jnp.float32, jnp.bfloat16
PARAMS = pltpu.CompilerParams(vmem_limit_bytes=16 * 2**20)
SCALAR = pl.BlockSpec(memory_space=pltpu.SMEM)
WHOLE = pl.BlockSpec(memory_space=pltpu.VMEM)
ARRIVAL = [0, 8, 4, 12, 2, 10, 6, 14, 1, 9, 5, 13, 3, 11, 7, 15]


def together(*values):
    return lax.optimization_barrier(values)


def swap(value, axis):
    return lax.ppermute(value, axis, [(0, 1), (1, 0)])


def around(value, hops):
    return lax.ppermute(value, RING, [(i, (i + hops) % 32) for i in range(32)])


def double_z(have, axis):
    return jnp.concatenate([have, swap(have, axis)], axis=0)


def project_kernel(z_ref, near_ref, far_ref, basis_out_ref, basis_in_ref, out_ref):
    z = z_ref[0]
    for m, basis_ref in enumerate((basis_out_ref, basis_in_ref)):
        for pair in range(2):
            total = jnp.zeros((256, 256), f32)
            for step in range(8):
                source = near_ref if step < 4 else far_ref
                at = 2 * step if step < 4 else 2 * step - 8
                left = jnp.concatenate([source[at, m], source[at + 1, m]], axis=1)
                z0 = z ^ ARRIVAL[2 * step]
                z1 = z ^ ARRIVAL[2 * step + 1]
                columns = [
                    jnp.concatenate([basis_ref[2 * pair + i, z0], basis_ref[2 * pair + i, z1]], axis=0) for i in range(2)
                ]
                right = jnp.concatenate(columns, axis=1)
                total = total + jnp.dot(left, right, preferred_element_type=f32)
            out_ref[2 * pair, m] = total[:, :128].astype(bf16)
            out_ref[2 * pair + 1, m] = total[:, 128:].astype(bf16)


def project(z, near, far, basis_out, basis_in):
    return pl.pallas_call(
        project_kernel,
        out_shape=jax.ShapeDtypeStruct((X, 2, 256, 128), bf16),
        in_specs=[SCALAR] + [WHOLE] * 4,
        out_specs=WHOLE,
        compiler_params=PARAMS,
        cost_estimate=pl.CostEstimate(flops=4 * 256 * 2048 * 512, bytes_accessed=6800000, transcendentals=0),
        name="project",
    )(z, near, far, basis_out, basis_in)


def place_kernel(a_ref, own, *refs):
    *blocks, half_low, half_high, out_ref = refs
    out_ref[a_ref[0]] = own[...]
    for k, block in zip((1, 2, 3, 5, 6, 7), blocks):
        at = lax.rem(a_ref[0] + k, 8)
        out_ref[at, :128] = block[:128]
        out_ref[at, 128:] = block[192:]
    far = lax.rem(a_ref[0] + 4, 8)
    out_ref[far, :128] = half_low[:128]
    out_ref[far, 128:] = half_high[64:]


def place(a, own, blocks, halves):
    return pl.pallas_call(
        place_kernel,
        out_shape=jax.ShapeDtypeStruct((8, 256, 128), bf16),
        in_specs=[SCALAR] + [WHOLE] * 9,
        out_specs=WHOLE,
        compiler_params=PARAMS,
        cost_estimate=pl.CostEstimate(flops=0, bytes_accessed=1100000, transcendentals=0),
        name="place",
    )(a, own, *blocks, *halves)


def scale_kernel(rows_ref, p0, p1, p2a, p2b, p3, out_ref):
    def block(j, at):
        if j == 2:
            return p2a[at] if at < 4 else p2b[at - 4]
        return {0: p0, 1: p1, 3: p3}[j][at]

    for j in range(4):
        for a in (0, 2):
            total = jnp.zeros((256, 256), f32)
            for h in range(2):
                right = jnp.concatenate([block(j, 4 * h + a), block(j, 4 * h + a + 1)], axis=1)
                total = total + jnp.dot(rows_ref[h], right, preferred_element_type=f32)
            at = (4 * j + a) * 128
            out_ref[:, :, at : at + 256] = total.reshape(32, 8, 256).astype(bf16)


def scale_part(rows, p0, p1, p2a, p2b, p3):
    return pl.pallas_call(
        scale_kernel,
        out_shape=jax.ShapeDtypeStruct((X * Y * C, 8, 2048), bf16),
        in_specs=[WHOLE] * 6,
        out_specs=WHOLE,
        compiler_params=PARAMS,
        cost_estimate=pl.CostEstimate(flops=2 * 256 * 512 * 2048, bytes_accessed=3300000, transcendentals=0),
        name="scale",
    )(rows, p0, p1, p2a, p2b, p3)


def exchange(value, axis):
    return lax.all_to_all(value, axis, split_axis=0, concat_axis=0, tiled=True)


def per_device(activations, out_grads, basis_in, basis_out, grad_eigen):
    tokens = activations.shape[0]
    ring = lax.axis_index(RING)
    z = (ring % 16).astype(jnp.int32).reshape(1)
    high = lax.axis_index("zh") == 1

    def mine(halves):
        return jnp.where(high, halves[1], halves[0])

    def theirs(halves):
        return jnp.where(high, halves[0], halves[1])

    def in_order(own, other):
        return jnp.stack([jnp.where(high, other, own), jnp.where(high, own, other)])

    basis_out = basis_out.reshape(16, X, 128, 128).transpose(1, 0, 2, 3)
    basis_in = basis_in.reshape(16, X, 128, 128).transpose(1, 0, 2, 3)

    grad = grad_eigen.reshape(Y, ZH, C * 8, 512).transpose(1, 0, 2, 3)
    grad_own = mine(grad)
    have, grad_other, basis_out = together(
        double_z(jnp.stack([out_grads, activations])[None], "z8"), swap(theirs(grad), "zh"), basis_out
    )
    b_out = exchange(basis_out, "x")
    have, basis_in = together(double_z(have, "z4"), basis_in)
    have, b_out = together(double_z(have, "z2"), b_out)
    b_in = exchange(basis_in, "x")
    far, have, b_in = together(swap(have, "z1"), have, b_in)

    part = project(z, have, far, b_out, b_in)
    projected = jnp.sum(exchange(part, "x").astype(f32), axis=0)
    squares = (projected * projected).astype(bf16)
    squares_out = squares[0]
    squares_in = squares[1].T.reshape(Y, ZH, C * 8, tokens).transpose(1, 0, 2, 3).reshape(ZH, 64, tokens)
    rows_own, rows_sent = mine(squares_in), theirs(squares_in)

    up = jnp.concatenate([squares_out[:128], rows_sent[:, :128], squares_out[128:]], axis=0)
    down = jnp.concatenate([squares_out[:128], rows_sent[:, 128:], squares_out[128:]], axis=0)
    up1, down1 = together(around(up, 4), around(down, -4))
    up2, down2, grad_own, grad_other = together(around(up1, 4), around(down1, -4), grad_own, grad_other)
    grad = in_order(grad_own, grad_other).reshape(ZH, Y, C, 8, 512).transpose(1, 2, 0, 3, 4)
    grad = exchange(grad.reshape(Y * C, ZH, 8, 512), ("y", "c"))
    up3, down3 = together(around(up2, 4), around(down2, -4))
    half_low, half_high, grad = together(around(up3[:192], 4), around(down3[128:], -4), grad)
    p0 = place(
        (ring // 4).astype(jnp.int32).reshape(1),
        squares_out,
        (down1, down2, down3, up3, up2, up1),
        (half_low, half_high),
    )
    rows_other = jnp.concatenate([half_low[128:], half_high[:64]], axis=1)
    rows_in = lax.all_gather(in_order(rows_own, rows_other), "x", axis=0, tiled=False)
    rows_in = rows_in.reshape(X, ZH, Y * C, 8, tokens).transpose(1, 2, 0, 3, 4).reshape(ZH, 256, tokens)
    p3, p1, rows_in = together(around(p0, 1), around(p0, -1), rows_in)
    p2a, p2b = around(p1[:4], -1), around(p3[4:], 1)
    grad = grad.reshape(Y, C, ZH, 8, 512).transpose(3, 0, 2, 1, 4).reshape(8, 8192)
    p2a, p2b, grad = together(p2a, p2b, grad)

    partial = exchange(scale_part(rows_in, p0, p1, p2a, p2b, p3), ("y", "c", "x"))
    rows = jnp.sum(partial.reshape(Y * C, X, 8, 2048).astype(f32), axis=0).reshape(X, 8, 4, 4, 128)
    rows = rows.transpose(1, 3, 2, 0, 4)
    odd, two = (ring % 2) == 1, ((ring // 2) % 2) == 1
    rows = jnp.where(odd, jnp.roll(rows, 1, axis=2), rows)
    rows = jnp.where(two, jnp.roll(rows, 2, axis=2), rows)
    rows = rows.reshape(8, 8192)

    scaling = rows / (tokens * Y * ZH * C)
    return (grad.astype(f32) / (scaling + damping)).astype(bf16)


def solution(mesh):
    fine = Mesh(mesh.devices.reshape(Y, ZH, C, 2, 2, 2, 2, X), AXES)
    dp, mp = ("y", "zh", "c"), Z_BITS + ("x",)
    placed = (P(dp, mp), P(dp, mp), P(None, mp), P(None, mp), P(mp, dp))
    return jax.shard_map(
        per_device, mesh=fine, in_specs=placed, out_specs=P(mp + dp, None), check_vma=False
    )
```

time: 311 us -> 282 us (0.907)
  starting transfers between devices: 195 us -> 163 us
  waiting for transfers between devices: 56.5 us -> 79.9 us
  blocking collectives: 43.2 us -> 20.8 us
    ppermute x10 -> x5, starting transfers between devices: 123 us -> 71.8 us  [swap(): return lax.ppermute(value, axis, [(0, 1), (1, 0)])]
    ppermute x10 -> x5, waiting for transfers between devices: 9.9 us -> 40.9 us  [swap(): return lax.ppermute(value, axis, [(0, 1), (1, 0)])]
    all_to_all x3 -> x1, blocking collectives: 33.8 us -> 10.8 us  [exchange(): return lax.all_to_all(value, axis, split_axis=0, concat_axis=0, tiled=True)]
    all_to_all x5 -> x4, starting transfers between devices: 19.3 us -> 34.3 us  [exchange(): return lax.all_to_all(value, axis, split_axis=0, concat_axis=0, tiled=True)]
    all_to_all x5 -> x4, waiting for transfers between devices: 24.2 us -> 17.6 us  [exchange(): return lax.all_to_all(value, axis, split_axis=0, concat_axis=0, tiled=True)]
    ppermute x12, starting transfers between devices: 52.4 us -> 56.4 us  [around(): return lax.ppermute(value, RING, [(i, (i + hops) % 32) for i in range(32)])]
  transfers between devices with their start and end apart: 27 -> 21, of which waited for: 13 -> 14; matrix products, arithmetic and copies ran while one was open for 3% -> 3% of each run, Pallas kernels for 0% -> 0%
where the time goes in v4:
time: 282 us; the launch traced here: 280 us
  starting transfers between devices  163 us (58%)
  waiting for transfers between devices  79.9 us (28%)
  blocking collectives  20.8 us (7%)
  local copies, waits for them, and re-layouts  6.82 us (2%)
  other arithmetic  4.92 us (2%)
  Pallas kernels  4.9 us (2%)
    ppermute x5, starting transfers between devices, swap(): return lax.ppermute(value, axis, [(0, 1), (1, 0)])  71.8 us
    ppermute x12, starting transfers between devices, around(): return lax.ppermute(value, RING, [(i, (i + hops) % 32) for i in range(32)])  56.4 us
    ppermute x5, waiting for transfers between devices, swap(): return lax.ppermute(value, axis, [(0, 1), (1, 0)])  40.9 us
    all_to_all x4, starting transfers between devices, exchange(): return lax.all_to_all(value, axis, split_axis=0, concat_axis=0, tiled=True)  34.3 us
    ppermute x12, waiting for transfers between devices, around(): return lax.ppermute(value, RING, [(i, (i + hops) % 32) for i in range(32)])  21.4 us
    all_to_all x4, waiting for transfers between devices, exchange(): return lax.all_to_all(value, axis, split_axis=0, concat_axis=0, tiled=True)  17.6 us
    all_to_all x1, blocking collectives, exchange(): return lax.all_to_all(value, axis, split_axis=0, concat_axis=0, tiled=True)  10.8 us
    all_gather x1, blocking collectives, per_device(): lax.all_gather(in_order(rows_own, rows_other), 'x', axis=0, tiled=False)  9.96 us
  transfers between devices with their start and end apart: 21, of which 14 were waited for; matrix products, arithmetic and copies ran while one was open for 3% of the time, Pallas kernels for 0%

profile of v4, /device:TPU:1, one launch (start us, length us, event | category | flops | bytes accessed | tf_op | source)
XLA Modules:
  0.0 280.5 jit_solution(4753831907376568335)
XLA Ops:
  0.9 16.3 %collective-permute-start = (bf16[1,2,256,128]{3,2,1,0:T(8,128)(2,1)S(1)}, bf16[1,2,256,128]{3,2,1,0:T(8,128)(2,1)S(1)}, u32[]{:S(2)}, u32[]{:S(2)}) collective-permute-start(bf16[1,2,256,128]{3,2,1,0:T(8,128)(2,1)S(1)} %maximum_bitcast_fusion), channel_id=1, source_target_pairs={{0,32},{32,0},{1,33},{33,1},{2,34},{34,2},{3,35},{35,3},{4,36},{36... | collective-permute-start | bytes 393224 | tf_op jit(solution)/shard_map/ppermute | solution.py:25
  18.1 19.1 %collective-permute-start.1 = (bf16[4,16,512]{2,1,0:T(8,128)(2,1)S(1)}, bf16[4,16,512]{2,1,0:T(8,128)(2,1)S(1)}, u32[]{:S(2)}, u32[]{:S(2)}) collective-permute-start(bf16[4,16,512]{2,1,0:T(8,128)(2,1)S(1)} %fusion.3), channel_id=1, source_target_pairs={{0,128},{128,0},{1,129},{129,1},{2,130},{130,2},{3,131},{131,3},{4... | collective-permute-start | bytes 196616 | tf_op jit(solution)/shard_map/ppermute | solution.py:25
  37.2 3.1 %copy.44 = bf16[16,4,128,128]{3,2,0,1:T(8,128)(2,1)} copy(bf16[16,4,128,128]{3,2,1,0:T(8,128)(2,1)} %bitcast.79) | data formatting | bytes 4194304 | tf_op jit(solution)/shard_map/reshape | solution.py:139
  41.7 4.0 %all-to-all-start = ((bf16[4,16,128,128]{3,2,1,0:T(8,128)(2,1)}), bf16[4,16,128,128]{3,2,1,0:T(8,128)(2,1)S(1)}, u32[]{:S(2)}, u32[]{:S(2)}) async-start(bf16[4,16,128,128]{3,2,1,0:T(8,128)(2,1)} %bitcast.74), calls=%async_computation | async-start | bytes 4194304 | tf_op jit(solution)/shard_map/all_to_all | solution.py:121
  45.7 15.0 %collective-permute-start.2 = (bf16[2,2,256,128]{3,2,1,0:T(8,128)(2,1)S(1)}, bf16[2,2,256,128]{3,2,1,0:T(8,128)(2,1)S(1)}, u32[]{:S(2)}, u32[]{:S(2)}) collective-permute-start(bf16[2,2,256,128]{3,2,1,0:T(8,128)(2,1)S(1)} %pad_maximum_fusion.2), channel_id=1, source_target_pairs={{0,16},{16,0},{1,17},{17,1},{2,18},{18,2},{3,19},{19,3},{4,20},{20... | collective-permute-start | bytes 786440 | tf_op jit(solution)/shard_map/ppermute | solution.py:25
  60.7 3.2 %copy.43 = bf16[16,4,128,128]{3,2,0,1:T(8,128)(2,1)} copy(bf16[16,4,128,128]{3,2,1,0:T(8,128)(2,1)} %bitcast.80) | data formatting | bytes 4194304 | tf_op jit(solution)/shard_map/reshape | solution.py:140
  65.7 17.4 %collective-permute-start.3 = (bf16[4,2,256,128]{3,2,1,0:T(8,128)(2,1)S(1)}, bf16[4,2,256,128]{3,2,1,0:T(8,128)(2,1)}, u32[]{:S(2)}, u32[]{:S(2)}) collective-permute-start(bf16[4,2,256,128]{3,2,1,0:T(8,128)(2,1)S(1)} %pad_maximum_fusion.1), channel_id=1, source_target_pairs={{0,8},{8,0},{1,9},{9,1},{2,10},{10,2},{3,11},{11,3},{4,12},{12,4},... | collective-permute-start | bytes 1572872 | tf_op jit(solution)/shard_map/ppermute | solution.py:25
  83.2 4.5 %all-to-all-start.1 = ((bf16[4,16,128,128]{3,2,1,0:T(8,128)(2,1)}), bf16[4,16,128,128]{3,2,1,0:T(8,128)(2,1)}, u32[]{:S(2)}, u32[]{:S(2)}) async-start(bf16[4,16,128,128]{3,2,1,0:T(8,128)(2,1)} %bitcast.73), calls=%async_computation.1 | async-start | bytes 4194304 | tf_op jit(solution)/shard_map/all_to_all | solution.py:121
  87.6 17.4 %collective-permute-done.3 = bf16[4,2,256,128]{3,2,1,0:T(8,128)(2,1)} collective-permute-done((bf16[4,2,256,128]{3,2,1,0:T(8,128)(2,1)S(1)}, bf16[4,2,256,128]{3,2,1,0:T(8,128)(2,1)}, u32[]{:S(2)}, u32[]{:S(2)}) %collective-permute-start.3) | collective-permute-done | bytes 524320 | tf_op jit(solution)/shard_map/ppermute | solution.py:25
  106.4 4.0 %collective-permute-start.4 = (bf16[8,2,256,128]{3,2,1,0:T(8,128)(2,1)S(1)}, bf16[8,2,256,128]{3,2,1,0:T(8,128)(2,1)}, u32[]{:S(2)}, u32[]{:S(2)}) collective-permute-start(bf16[8,2,256,128]{3,2,1,0:T(8,128)(2,1)S(1)} %pad_maximum_fusion.near_ref), channel_id=1, source_target_pairs={{0,4},{4,0},{1,5},{5,1},{2,6},{6,2},{3,7},{7,3},{8,12},{12,8},{9,1... | collective-permute-start | bytes 3145736 | tf_op jit(solution)/shard_map/ppermute | solution.py:25
  112.1 20.4 %collective-permute-done.4.far_ref = bf16[8,2,256,128]{3,2,1,0:T(8,128)(2,1)} collective-permute-done((bf16[8,2,256,128]{3,2,1,0:T(8,128)(2,1)S(1)}, bf16[8,2,256,128]{3,2,1,0:T(8,128)(2,1)}, u32[]{:S(2)}, u32[]{:S(2)}) %collective-permute-start.4) | collective-permute-done | bytes 1048608 | tf_op jit(solution)/shard_map/ppermute | solution.py:25
  132.4 3.2 %project.1 = bf16[4,2,256,128]{3,2,1,0:T(8,128)(2,1)S(1)} custom-call(s32[1]{0:T(128)} %bitcast.1.z_ref, bf16[8,2,256,128]{3,2,1,0:T(8,128)(2,1)S(1)} %pad_maximum_fusion.near_ref, bf16[8,2,256,128]{3,2,1,0:T(8,128)(2,1)} %collective-permute-done.4.far_ref, bf16[4,16,128,128]{3,2,1,0:T(8,128)(2,1)S(1)} %all-to-all-done.basis_out_ref, ...), custom_call_target="tpu_custom_call" | custom-call | flops 1073741824 | bytes 6800000 | tf_op jit(solution)/shard_map/project/pallas_call | solution.py:57
  135.6 10.8 %all_to_all.25 = bf16[4,2,256,128]{3,2,1,0:T(8,128)(2,1)S(1)} all-to-all(bf16[4,2,256,128]{3,2,1,0:T(8,128)(2,1)S(1)} %project.1), channel_id=1, replica_groups=mesh['y'=4,'zh'=2,'c'=2,'z8'=2,'z4'=2,'z2'=2,'z1'=2,'x'=4] {'x'}, dimensions={0} | all-to-all | bytes 1048576 | tf_op jit(solution)/shard_map/all_to_all | solution.py:121
  146.7 15.1 %collective-permute-start.6 = (bf16[320,128]{1,0:T(8,128)(2,1)S(1)}, bf16[320,128]{1,0:T(8,128)(2,1)S(1)}, u32[]{:S(2)}, u32[]{:S(2)}) collective-permute-start(bf16[320,128]{1,0:T(8,128)(2,1)S(1)} %get-tuple-element.71), channel_id=1, source_target_pairs={{0,176},{4,180},{8,184},{12,188},{16,0},{20,4},{24,8},{28,12},{32,... | collective-permute-start | bytes 245768 | tf_op jit(solution)/shard_map/ppermute | solution.py:29
  161.9 1.9 collective-permute-start.5
  164.1 6.9 %collective-permute-done.5.refs_5_ = bf16[320,128]{1,0:T(8,128)(2,1)S(1)} collective-permute-done((bf16[320,128]{1,0:T(8,128)(2,1)S(1)}, bf16[320,128]{1,0:T(8,128)(2,1)S(1)}, u32[]{:S(2)}, u32[]{:S(2)}) %collective-permute-start.5) | collective-permute-done | bytes 81952 | tf_op jit(solution)/shard_map/ppermute | solution.py:29
  171.1 6.7 %collective-permute-start.8 = (bf16[320,128]{1,0:T(8,128)(2,1)S(1)}, bf16[320,128]{1,0:T(8,128)(2,1)S(1)}, u32[]{:S(2)}, u32[]{:S(2)}) collective-permute-start(bf16[320,128]{1,0:T(8,128)(2,1)S(1)} %collective-permute-done.6.refs_0_), channel_id=1, source_target_pairs={{0,176},{4,180},{8,184},{12,188},{16,0},{20,4},{24,8},{28,12},{32,... | collective-permute-start | bytes 245768 | tf_op jit(solution)/shard_map/ppermute | solution.py:29
  177.8 2.4 collective-permute-start.7
  181.0 5.9 %collective-permute-done.7.refs_4_ = bf16[320,128]{1,0:T(8,128)(2,1)S(1)} collective-permute-done((bf16[320,128]{1,0:T(8,128)(2,1)S(1)}, bf16[320,128]{1,0:T(8,128)(2,1)S(1)}, u32[]{:S(2)}, u32[]{:S(2)}) %collective-permute-start.7) | collective-permute-done | bytes 81952 | tf_op jit(solution)/shard_map/ppermute | solution.py:29
  186.9 5.7 %collective-permute-start.10 = (bf16[320,128]{1,0:T(8,128)(2,1)S(1)}, bf16[320,128]{1,0:T(8,128)(2,1)S(1)}, u32[]{:S(2)}, u32[]{:S(2)}) collective-permute-start(bf16[320,128]{1,0:T(8,128)(2,1)S(1)} %collective-permute-done.8.refs_1_), channel_id=1, source_target_pairs={{0,176},{4,180},{8,184},{12,188},{16,0},{20,4},{24,8},{28,12},{32,... | collective-permute-start | bytes 245768 | tf_op jit(solution)/shard_map/ppermute | solution.py:29
  192.6 3.5 %collective-permute-start.9 = (bf16[320,128]{1,0:T(8,128)(2,1)S(1)}, bf16[320,128]{1,0:T(8,128)(2,1)S(1)}, u32[]{:S(2)}, u32[]{:S(2)}) collective-permute-start(bf16[320,128]{1,0:T(8,128)(2,1)S(1)} %collective-permute-done.7.refs_4_), channel_id=1, source_target_pairs={{0,16},{4,20},{8,24},{12,28},{16,32},{20,36},{24,40},{28,44},{32,4... | collective-permute-start | bytes 245768 | tf_op jit(solution)/shard_map/ppermute | solution.py:29
  196.8 13.1 %all-to-all-start.3 = ((bf16[8,2,8,512]{3,2,1,0:T(8,128)(2,1)}), bf16[8,2,8,512]{3,2,1,0:T(8,128)(2,1)S(1)}, u32[]{:S(2)}, u32[]{:S(2)}) async-start(bf16[8,2,8,512]{3,2,1,0:T(8,128)(2,1)} %bitcast.29), calls=%async_computation.3 | async-start | bytes 262144 | tf_op jit(solution)/shard_map/all_to_all | solution.py:121
  209.9 3.7 %collective-permute-start.11 = (bf16[192,128]{1,0:T(8,128)(2,1)S(1)}, bf16[192,128]{1,0:T(8,128)(2,1)S(1)}, u32[]{:S(2)}, u32[]{:S(2)}) collective-permute-start(bf16[192,128]{1,0:T(8,128)(2,1)S(1)} %slice.92), channel_id=1, source_target_pairs={{0,16},{4,20},{8,24},{12,28},{16,32},{20,36},{24,40},{28,44},{32,4... | collective-permute-start | bytes 147464 | tf_op jit(solution)/shard_map/ppermute | solution.py:29
  213.6 5.5 %collective-permute-start.12 = (bf16[192,128]{1,0:T(8,128)(2,1)S(1)}, bf16[192,128]{1,0:T(8,128)(2,1)S(1)}, u32[]{:S(2)}, u32[]{:S(2)}) collective-permute-start(bf16[192,128]{1,0:T(8,128)(2,1)S(1)} %slice.93), channel_id=1, source_target_pairs={{0,176},{4,180},{8,184},{12,188},{16,0},{20,4},{24,8},{28,12},{32,... | collective-permute-start | bytes 147464 | tf_op jit(solution)/shard_map/ppermute | solution.py:29
  219.1 1.9 collective-permute-done.11.refs_6_
  221.0 2.6 collective-permute-done.12.refs_7_
  225.6 3.4 %collective-permute-start.13 = (bf16[8,256,128]{2,1,0:T(8,128)(2,1)S(1)}, bf16[8,256,128]{2,1,0:T(8,128)(2,1)S(1)}, u32[]{:S(2)}, u32[]{:S(2)}) collective-permute-start(bf16[8,256,128]{2,1,0:T(8,128)(2,1)S(1)} %place.1.p0), channel_id=1, source_target_pairs={{0,4},{4,8},{8,12},{12,16},{16,20},{20,24},{24,28},{28,32},{32,36}... | collective-permute-start | bytes 1572872 | tf_op jit(solution)/shard_map/ppermute | solution.py:29
  229.0 10.0 %all-gather = bf16[8,64,256]{2,1,0:T(8,128)(2,1)S(1)} all-gather(bf16[2,64,256]{2,1,0:T(8,128)(2,1)S(1)} %pad_maximum_fusion.8), channel_id=2, replica_groups=mesh['y'=4,'zh'=2,'c'=2,'z8'=2,'z4'=2,'z2'=2,'z1'=2,'x'=4] {'x'}, dimensions={0}, use_global_device_ids=true | all-gather | bytes 327680 | tf_op jit(solution)/shard_map/all_gather | solution.py:175
  239.1 2.4 collective-permute-start.16
  241.5 4.1 %collective-permute-start.15 = (bf16[4,256,128]{2,1,0:T(8,128)(2,1)S(1)}, bf16[4,256,128]{2,1,0:T(8,128)(2,1)S(1)}, u32[]{:S(2)}, u32[]{:S(2)}) collective-permute-start(bf16[4,256,128]{2,1,0:T(8,128)(2,1)S(1)} %slice.96), channel_id=1, source_target_pairs={{0,188},{4,0},{8,4},{12,8},{16,12},{20,16},{24,20},{28,24},{32,28}... | collective-permute-start | bytes 786440 | tf_op jit(solution)/shard_map/ppermute | solution.py:29
  250.6 12.8 %all-to-all-start.4 = ((bf16[32,8,2048]{2,1,0:T(8,128)(2,1)}), bf16[32,8,2048]{2,1,0:T(8,128)(2,1)S(1)}, u32[]{:S(2)}, u32[]{:S(2)}) async-start(bf16[32,8,2048]{2,1,0:T(8,128)(2,1)} %scale.1), calls=%async_computation.4 | async-start | bytes 2097152 | tf_op jit(solution)/shard_map/all_to_all | solution.py:121
  263.4 16.0 %all-to-all-done.4 = bf16[32,8,2048]{2,1,0:T(8,128)(2,1)S(1)} async-done(((bf16[32,8,2048]{2,1,0:T(8,128)(2,1)}), bf16[32,8,2048]{2,1,0:T(8,128)(2,1)S(1)}, u32[]{:S(2)}, u32[]{:S(2)}) %all-to-all-start.4) | async-done | bytes 1048608 | tf_op jit(solution)/shard_map/all_to_all | solution.py:121
  (55 shorter events, 17.9 us)
Async XLA Ops:
  0.9 39.4 %collective-permute-start = (bf16[1,2,256,128]{3,2,1,0:T(8,128)(2,1)S(1)}, bf16[1,2,256,128]{3,2,1,0:T(8,128)(2,1)S(1)}, u32[]{:S(2)}, u32[]{:S(2)}) collective-permute-start(bf16[1,2,256,128]{3,2,1,0:T(8,128)(2,1)S(1)} %maximum_bitcast_fusion), channel_id=1, source_target_pairs={{0,32},{32,0},{1,33},{33,1},{2,34},{34,2},{3,35},{35,3},{4,36},{36... | collective-permute-start | bytes 393224 | tf_op jit(solution)/shard_map/ppermute | solution.py:25
  18.1 23.6 %collective-permute-start.1 = (bf16[4,16,512]{2,1,0:T(8,128)(2,1)S(1)}, bf16[4,16,512]{2,1,0:T(8,128)(2,1)S(1)}, u32[]{:S(2)}, u32[]{:S(2)}) collective-permute-start(bf16[4,16,512]{2,1,0:T(8,128)(2,1)S(1)} %fusion.3), channel_id=1, source_target_pairs={{0,128},{128,0},{1,129},{129,1},{2,130},{130,2},{3,131},{131,3},{4... | collective-permute-start | bytes 196616 | tf_op jit(solution)/shard_map/ppermute | solution.py:25
  41.7 41.4 %all-to-all-start = ((bf16[4,16,128,128]{3,2,1,0:T(8,128)(2,1)}), bf16[4,16,128,128]{3,2,1,0:T(8,128)(2,1)S(1)}, u32[]{:S(2)}, u32[]{:S(2)}) async-start(bf16[4,16,128,128]{3,2,1,0:T(8,128)(2,1)} %bitcast.74), calls=%async_computation | async-start | bytes 4194304 | tf_op jit(solution)/shard_map/all_to_all | solution.py:121
  45.7 20.0 %collective-permute-start.2 = (bf16[2,2,256,128]{3,2,1,0:T(8,128)(2,1)S(1)}, bf16[2,2,256,128]{3,2,1,0:T(8,128)(2,1)S(1)}, u32[]{:S(2)}, u32[]{:S(2)}) collective-permute-start(bf16[2,2,256,128]{3,2,1,0:T(8,128)(2,1)S(1)} %pad_maximum_fusion.2), channel_id=1, source_target_pairs={{0,16},{16,0},{1,17},{17,1},{2,18},{18,2},{3,19},{19,3},{4,20},{20... | collective-permute-start | bytes 786440 | tf_op jit(solution)/shard_map/ppermute | solution.py:25
  65.7 17.5 %copy-start = (bf16[4,2,256,128]{3,2,1,0:T(8,128)(2,1)}, bf16[4,2,256,128]{3,2,1,0:T(8,128)(2,1)S(1)}, u32[]{:S(2)}) copy-start(bf16[4,2,256,128]{3,2,1,0:T(8,128)(2,1)S(1)} %pad_maximum_fusion.1) | copy-start | bytes 1572868
  65.7 39.4 %collective-permute-start.3 = (bf16[4,2,256,128]{3,2,1,0:T(8,128)(2,1)S(1)}, bf16[4,2,256,128]{3,2,1,0:T(8,128)(2,1)}, u32[]{:S(2)}, u32[]{:S(2)}) collective-permute-start(bf16[4,2,256,128]{3,2,1,0:T(8,128)(2,1)S(1)} %pad_maximum_fusion.1), channel_id=1, source_target_pairs={{0,8},{8,0},{1,9},{9,1},{2,10},{10,2},{3,11},{11,3},{4,12},{12,4},... | collective-permute-start | bytes 1572872 | tf_op jit(solution)/shard_map/ppermute | solution.py:25
  83.2 28.9 %all-to-all-start.1 = ((bf16[4,16,128,128]{3,2,1,0:T(8,128)(2,1)}), bf16[4,16,128,128]{3,2,1,0:T(8,128)(2,1)}, u32[]{:S(2)}, u32[]{:S(2)}) async-start(bf16[4,16,128,128]{3,2,1,0:T(8,128)(2,1)} %bitcast.73), calls=%async_computation.1 | async-start | bytes 4194304 | tf_op jit(solution)/shard_map/all_to_all | solution.py:121
  106.4 26.0 %collective-permute-start.4 = (bf16[8,2,256,128]{3,2,1,0:T(8,128)(2,1)S(1)}, bf16[8,2,256,128]{3,2,1,0:T(8,128)(2,1)}, u32[]{:S(2)}, u32[]{:S(2)}) collective-permute-start(bf16[8,2,256,128]{3,2,1,0:T(8,128)(2,1)S(1)} %pad_maximum_fusion.near_ref), channel_id=1, source_target_pairs={{0,4},{4,0},{1,5},{5,1},{2,6},{6,2},{3,7},{7,3},{8,12},{12,8},{9,1... | collective-permute-start | bytes 3145736 | tf_op jit(solution)/shard_map/ppermute | solution.py:25
  135.6 44.7 %copy-start.1 = (bf16[128,512]{1,0:T(8,128)(2,1)S(1)}, bf16[128,512]{1,0:T(8,128)(2,1)}, u32[]{:S(2)}) copy-start(bf16[128,512]{1,0:T(8,128)(2,1)} %param.9) | copy-start | bytes 393220
  146.7 17.4 %collective-permute-start.6 = (bf16[320,128]{1,0:T(8,128)(2,1)S(1)}, bf16[320,128]{1,0:T(8,128)(2,1)S(1)}, u32[]{:S(2)}, u32[]{:S(2)}) collective-permute-start(bf16[320,128]{1,0:T(8,128)(2,1)S(1)} %get-tuple-element.71), channel_id=1, source_target_pairs={{0,176},{4,180},{8,184},{12,188},{16,0},{20,4},{24,8},{28,12},{32,... | collective-permute-start | bytes 245768 | tf_op jit(solution)/shard_map/ppermute | solution.py:29
  161.9 9.1 %collective-permute-start.5 = (bf16[320,128]{1,0:T(8,128)(2,1)S(1)}, bf16[320,128]{1,0:T(8,128)(2,1)S(1)}, u32[]{:S(2)}, u32[]{:S(2)}) collective-permute-start(bf16[320,128]{1,0:T(8,128)(2,1)S(1)} %get-tuple-element.72), channel_id=1, source_target_pairs={{0,16},{4,20},{8,24},{12,28},{16,32},{20,36},{24,40},{28,44},{32,4... | collective-permute-start | bytes 245768 | tf_op jit(solution)/shard_map/ppermute | solution.py:29
  171.1 9.9 %collective-permute-start.8 = (bf16[320,128]{1,0:T(8,128)(2,1)S(1)}, bf16[320,128]{1,0:T(8,128)(2,1)S(1)}, u32[]{:S(2)}, u32[]{:S(2)}) collective-permute-start(bf16[320,128]{1,0:T(8,128)(2,1)S(1)} %collective-permute-done.6.refs_0_), channel_id=1, source_target_pairs={{0,176},{4,180},{8,184},{12,188},{16,0},{20,4},{24,8},{28,12},{32,... | collective-permute-start | bytes 245768 | tf_op jit(solution)/shard_map/ppermute | solution.py:29
  177.8 9.1 %collective-permute-start.7 = (bf16[320,128]{1,0:T(8,128)(2,1)S(1)}, bf16[320,128]{1,0:T(8,128)(2,1)S(1)}, u32[]{:S(2)}, u32[]{:S(2)}) collective-permute-start(bf16[320,128]{1,0:T(8,128)(2,1)S(1)} %collective-permute-done.5.refs_5_), channel_id=1, source_target_pairs={{0,16},{4,20},{8,24},{12,28},{16,32},{20,36},{24,40},{28,44},{32,4... | collective-permute-start | bytes 245768 | tf_op jit(solution)/shard_map/ppermute | solution.py:29
  186.9 23.0 %collective-permute-start.10 = (bf16[320,128]{1,0:T(8,128)(2,1)S(1)}, bf16[320,128]{1,0:T(8,128)(2,1)S(1)}, u32[]{:S(2)}, u32[]{:S(2)}) collective-permute-start(bf16[320,128]{1,0:T(8,128)(2,1)S(1)} %collective-permute-done.8.refs_1_), channel_id=1, source_target_pairs={{0,176},{4,180},{8,184},{12,188},{16,0},{20,4},{24,8},{28,12},{32,... | collective-permute-start | bytes 245768 | tf_op jit(solution)/shard_map/ppermute | solution.py:29
  192.6 17.3 %collective-permute-start.9 = (bf16[320,128]{1,0:T(8,128)(2,1)S(1)}, bf16[320,128]{1,0:T(8,128)(2,1)S(1)}, u32[]{:S(2)}, u32[]{:S(2)}) collective-permute-start(bf16[320,128]{1,0:T(8,128)(2,1)S(1)} %collective-permute-done.7.refs_4_), channel_id=1, source_target_pairs={{0,16},{4,20},{8,24},{12,28},{16,32},{20,36},{24,40},{28,44},{32,4... | collective-permute-start | bytes 245768 | tf_op jit(solution)/shard_map/ppermute | solution.py:29
  196.8 22.3 %all-to-all-start.3 = ((bf16[8,2,8,512]{3,2,1,0:T(8,128)(2,1)}), bf16[8,2,8,512]{3,2,1,0:T(8,128)(2,1)S(1)}, u32[]{:S(2)}, u32[]{:S(2)}) async-start(bf16[8,2,8,512]{3,2,1,0:T(8,128)(2,1)} %bitcast.29), calls=%async_computation.3 | async-start | bytes 262144 | tf_op jit(solution)/shard_map/all_to_all | solution.py:121
  209.9 11.2 %collective-permute-start.11 = (bf16[192,128]{1,0:T(8,128)(2,1)S(1)}, bf16[192,128]{1,0:T(8,128)(2,1)S(1)}, u32[]{:S(2)}, u32[]{:S(2)}) collective-permute-start(bf16[192,128]{1,0:T(8,128)(2,1)S(1)} %slice.92), channel_id=1, source_target_pairs={{0,16},{4,20},{8,24},{12,28},{16,32},{20,36},{24,40},{28,44},{32,4... | collective-permute-start | bytes 147464 | tf_op jit(solution)/shard_map/ppermute | solution.py:29
  213.6 10.0 %collective-permute-start.12 = (bf16[192,128]{1,0:T(8,128)(2,1)S(1)}, bf16[192,128]{1,0:T(8,128)(2,1)S(1)}, u32[]{:S(2)}, u32[]{:S(2)}) collective-permute-start(bf16[192,128]{1,0:T(8,128)(2,1)S(1)} %slice.93), channel_id=1, source_target_pairs={{0,176},{4,180},{8,184},{12,188},{16,0},{20,4},{24,8},{28,12},{32,... | collective-permute-start | bytes 147464 | tf_op jit(solution)/shard_map/ppermute | solution.py:29
  223.7 15.3 %collective-permute-start.14 = (bf16[8,256,128]{2,1,0:T(8,128)(2,1)S(1)}, bf16[8,256,128]{2,1,0:T(8,128)(2,1)S(1)}, u32[]{:S(2)}, u32[]{:S(2)}) collective-permute-start(bf16[8,256,128]{2,1,0:T(8,128)(2,1)S(1)} %place.1.p0), channel_id=1, source_target_pairs={{0,188},{4,0},{8,4},{12,8},{16,12},{20,16},{24,20},{28,24},{32,28}... | collective-permute-start | bytes 1572872 | tf_op jit(solution)/shard_map/ppermute | solution.py:29
  225.6 13.4 %collective-permute-start.13 = (bf16[8,256,128]{2,1,0:T(8,128)(2,1)S(1)}, bf16[8,256,128]{2,1,0:T(8,128)(2,1)S(1)}, u32[]{:S(2)}, u32[]{:S(2)}) collective-permute-start(bf16[8,256,128]{2,1,0:T(8,128)(2,1)S(1)} %place.1.p0), channel_id=1, source_target_pairs={{0,4},{4,8},{8,12},{12,16},{16,20},{20,24},{24,28},{28,32},{32,36}... | collective-permute-start | bytes 1572872 | tf_op jit(solution)/shard_map/ppermute | solution.py:29
  239.1 8.3 %collective-permute-start.16 = (bf16[4,256,128]{2,1,0:T(8,128)(2,1)S(1)}, bf16[4,256,128]{2,1,0:T(8,128)(2,1)S(1)}, u32[]{:S(2)}, u32[]{:S(2)}) collective-permute-start(bf16[4,256,128]{2,1,0:T(8,128)(2,1)S(1)} %slice.97), channel_id=1, source_target_pairs={{0,4},{4,8},{8,12},{12,16},{16,20},{20,24},{24,28},{28,32},{32,36}... | collective-permute-start | bytes 786440 | tf_op jit(solution)/shard_map/ppermute | solution.py:29
  241.5 7.4 %collective-permute-start.15 = (bf16[4,256,128]{2,1,0:T(8,128)(2,1)S(1)}, bf16[4,256,128]{2,1,0:T(8,128)(2,1)S(1)}, u32[]{:S(2)}, u32[]{:S(2)}) collective-permute-start(bf16[4,256,128]{2,1,0:T(8,128)(2,1)S(1)} %slice.96), channel_id=1, source_target_pairs={{0,188},{4,0},{8,4},{12,8},{16,12},{20,16},{24,20},{28,24},{32,28}... | collective-permute-start | bytes 786440 | tf_op jit(solution)/shard_map/ppermute | solution.py:29
  250.6 28.8 %all-to-all-start.4 = ((bf16[32,8,2048]{2,1,0:T(8,128)(2,1)}), bf16[32,8,2048]{2,1,0:T(8,128)(2,1)S(1)}, u32[]{:S(2)}, u32[]{:S(2)}) async-start(bf16[32,8,2048]{2,1,0:T(8,128)(2,1)} %scale.1), calls=%async_computation.4 | async-start | bytes 2097152 | tf_op jit(solution)/shard_map/all_to_all | solution.py:121

commit v5 on v4

--- a/solution.py
+++ b/solution.py
@@ -33,36 +33,35 @@
     return jnp.concatenate([have, swap(have, axis)], axis=0)
 
 
-def project_kernel(z_ref, near_ref, far_ref, basis_out_ref, basis_in_ref, out_ref):
+def project_kernel(z_ref, near_ref, far_ref, basis_ref, out_ref):
     z = z_ref[0]
-    for m, basis_ref in enumerate((basis_out_ref, basis_in_ref)):
-        for pair in range(2):
-            total = jnp.zeros((256, 256), f32)
-            for step in range(8):
-                source = near_ref if step < 4 else far_ref
-                at = 2 * step if step < 4 else 2 * step - 8
-                left = jnp.concatenate([source[at, m], source[at + 1, m]], axis=1)
-                z0 = z ^ ARRIVAL[2 * step]
-                z1 = z ^ ARRIVAL[2 * step + 1]
-                columns = [
-                    jnp.concatenate([basis_ref[2 * pair + i, z0], basis_ref[2 * pair + i, z1]], axis=0) for i in range(2)
-                ]
-                right = jnp.concatenate(columns, axis=1)
-                total = total + jnp.dot(left, right, preferred_element_type=f32)
-            out_ref[2 * pair, m] = total[:, :128].astype(bf16)
-            out_ref[2 * pair + 1, m] = total[:, 128:].astype(bf16)
-
-
-def project(z, near, far, basis_out, basis_in):
+    for pair in range(2):
+        total = jnp.zeros((256, 256), f32)
+        for step in range(8):
+            source = near_ref if step < 4 else far_ref
+            at = 2 * step if step < 4 else 2 * step - 8
+            left = jnp.concatenate([source[at], source[at + 1]], axis=1)
+            z0 = z ^ ARRIVAL[2 * step]
+            z1 = z ^ ARRIVAL[2 * step + 1]
+            columns = [
+                jnp.concatenate([basis_ref[2 * pair + i, z0], basis_ref[2 * pair + i, z1]], axis=0) for i in range(2)
+            ]
+            right = jnp.concatenate(columns, axis=1)
+            total = total + jnp.dot(left, right, preferred_element_type=f32)
+        out_ref[2 * pair] = total[:, :128].astype(bf16)
+        out_ref[2 * pair + 1] = total[:, 128:].astype(bf16)
+
+
+def project(z, near, far, basis):
     return pl.pallas_call(
         project_kernel,
-        out_shape=jax.ShapeDtypeStruct((X, 2, 256, 128), bf16),
-        in_specs=[SCALAR] + [WHOLE] * 4,
+        out_shape=jax.ShapeDtypeStruct((X, 256, 128), bf16),
+        in_specs=[SCALAR] + [WHOLE] * 3,
         out_specs=WHOLE,
         compiler_params=PARAMS,
-        cost_estimate=pl.CostEstimate(flops=4 * 256 * 2048 * 512, bytes_accessed=6800000, transcendentals=0),
+        cost_estimate=pl.CostEstimate(flops=20 * 2**30, bytes_accessed=3400000, transcendentals=0),
         name="project",
-    )(z, near, far, basis_out, basis_in)
+    )(z, near, far, basis)
 
 
 def place_kernel(a_ref, own, *refs):
@@ -71,10 +70,10 @@
     for k, block in zip((1, 2, 3, 5, 6, 7), blocks):
         at = lax.rem(a_ref[0] + k, 8)
         out_ref[at, :128] = block[:128]
-        out_ref[at, 128:] = block[192:]
+        out_ref[at, 128:] = block[128:]
     far = lax.rem(a_ref[0] + 4, 8)
-    out_ref[far, :128] = half_low[:128]
-    out_ref[far, 128:] = half_high[64:]
+    out_ref[far, :128] = half_low[...]
+    out_ref[far, 128:] = half_high[...]
 
 
 def place(a, own, blocks, halves):
@@ -136,48 +135,50 @@
     def in_order(own, other):
         return jnp.stack([jnp.where(high, other, own), jnp.where(high, own, other)])
 
+    def squares(part):
+        projected = jnp.sum(part.astype(f32), axis=0)
+        return (projected * projected).astype(bf16)
+
     basis_out = basis_out.reshape(16, X, 128, 128).transpose(1, 0, 2, 3)
     basis_in = basis_in.reshape(16, X, 128, 128).transpose(1, 0, 2, 3)
 
-    grad = grad_eigen.reshape(Y, ZH, C * 8, 512).transpose(1, 0, 2, 3)
-    grad_own = mine(grad)
-    have, grad_other, basis_out = together(
-        double_z(jnp.stack([out_grads, activations])[None], "z8"), swap(theirs(grad), "zh"), basis_out
-    )
+    b_in = exchange(basis_in, "x")
+    z_in, z_out, grad_eigen = together(double_z(activations[None], "z8"), out_grads[None], grad_eigen)
+    z_in, z_out, b_in, basis_out = together(double_z(z_in, "z4"), double_z(z_out, "z8"), b_in, basis_out)
+    grad = grad_eigen.reshape(Y, ZH, C, 8, 512).transpose(0, 2, 1, 3, 4).reshape(Y * C, ZH, 8, 512)
+    grad = exchange(grad, ("y", "c"))
+    z_in, z_out, grad, basis_out = together(double_z(z_in, "z2"), double_z(z_out, "z4"), grad, basis_out)
     b_out = exchange(basis_out, "x")
-    have, basis_in = together(double_z(have, "z4"), basis_in)
-    have, b_out = together(double_z(have, "z2"), b_out)
-    b_in = exchange(basis_in, "x")
-    far, have, b_in = together(swap(have, "z1"), have, b_in)
-
-    part = project(z, have, far, b_out, b_in)
-    projected = jnp.sum(exchange(part, "x").astype(f32), axis=0)
-    squares = (projected * projected).astype(bf16)
-    squares_out = squares[0]
-    squares_in = squares[1].T.reshape(Y, ZH, C * 8, tokens).transpose(1, 0, 2, 3).reshape(ZH, 64, tokens)
-    rows_own, rows_sent = mine(squares_in), theirs(squares_in)
-
-    up = jnp.concatenate([squares_out[:128], rows_sent[:, :128], squares_out[128:]], axis=0)
-    down = jnp.concatenate([squares_out[:128], rows_sent[:, 128:], squares_out[128:]], axis=0)
-    up1, down1 = together(around(up, 4), around(down, -4))
-    up2, down2, grad_own, grad_other = together(around(up1, 4), around(down1, -4), grad_own, grad_other)
-    grad = in_order(grad_own, grad_other).reshape(ZH, Y, C, 8, 512).transpose(1, 2, 0, 3, 4)
-    grad = exchange(grad.reshape(Y * C, ZH, 8, 512), ("y", "c"))
+    far_in, z_in, z_out, b_out = together(swap(z_in, "z1"), z_in, double_z(z_out, "z2"), b_out)
+
+    far_out = swap(z_out, "z1")
+    squares_in = squares(exchange(project(z, z_in, far_in, b_in), "x"))
+    squares_in = squares_in.T.reshape(Y, ZH, C * 8, tokens).transpose(1, 0, 2, 3).reshape(ZH, 64, tokens)
+    far_out, z_out, b_out, squares_in, grad = together(far_out, z_out, b_out, squares_in, grad)
+    grad = grad.transpose(1, 0, 2, 3)
+
+    sent = jnp.concatenate([theirs(squares_in), theirs(grad).reshape(64, 512)], axis=1)
+    got = swap(sent, "zh")
+    part_out, got = together(exchange(project(z, z_out, far_out, b_out), "x"), got)
+    squares_out = squares(part_out)
+    rows_in = in_order(mine(squares_in), got[:, :tokens])
+    grad = in_order(mine(grad), got[:, tokens:].reshape(Y * C, 8, 512))
+    grad = grad.reshape(ZH, Y, C, 8, 512).transpose(3, 1, 0, 2, 4).reshape(8, 8192)
+
+    up1, down1 = together(around(squares_out, 4), around(squares_out, -4))
+    up2, down2 = together(around(up1, 4), around(down1, -4))
     up3, down3 = together(around(up2, 4), around(down2, -4))
-    half_low, half_high, grad = together(around(up3[:192], 4), around(down3[128:], -4), grad)
+    half_low, half_high, grad, rows_in = together(around(up3[:128], 4), around(down3[128:], -4), grad, rows_in)
     p0 = place(
         (ring // 4).astype(jnp.int32).reshape(1),
         squares_out,
         (down1, down2, down3, up3, up2, up1),
         (half_low, half_high),
     )
-    rows_other = jnp.concatenate([half_low[128:], half_high[:64]], axis=1)
-    rows_in = lax.all_gather(in_order(rows_own, rows_other), "x", axis=0, tiled=False)
+    rows_in = lax.all_gather(rows_in, "x", axis=0, tiled=False)
     rows_in = rows_in.reshape(X, ZH, Y * C, 8, tokens).transpose(1, 2, 0, 3, 4).reshape(ZH, 256, tokens)
     p3, p1, rows_in = together(around(p0, 1), around(p0, -1), rows_in)
     p2a, p2b = around(p1[:4], -1), around(p3[4:], 1)
-    grad = grad.reshape(Y, C, ZH, 8, 512).transpose(3, 0, 2, 1, 4).reshape(8, 8192)
-    p2a, p2b, grad = together(p2a, p2b, grad)
 
     partial = exchange(scale_part(rows_in, p0, p1, p2a, p2b, p3), ("y", "c", "x"))
     rows = jnp.sum(partial.reshape(Y * C, X, 8, 2048).astype(f32), axis=0).reshape(X, 8, 4, 4, 128)

time: 282 us -> 303 us (1.074)
  starting transfers between devices: 163 us -> 188 us
  blocking collectives: 20.8 us -> 14.2 us
    ppermute x5 -> x9, starting transfers between devices: 71.8 us -> 92.8 us  [swap(): return lax.ppermute(value, axis, [(0, 1), (1, 0)])]
    ppermute x5 -> x9, waiting for transfers between devices: 40.9 us -> 29.6 us  [swap(): return lax.ppermute(value, axis, [(0, 1), (1, 0)])]
    all_to_all x1 -> x0, blocking collectives: 10.8 us -> none  [exchange(): return lax.all_to_all(value, axis, split_axis=0, concat_axis=0, tiled=True)]
    ppermute x12, waiting for transfers between devices: 21.4 us -> 28.7 us  [around(): return lax.ppermute(value, RING, [(i, (i + hops) % 32) for i in range(32)])]
    all_to_all x4 -> x6, waiting for transfers between devices: 17.6 us -> 22.7 us  [exchange(): return lax.all_to_all(value, axis, split_axis=0, concat_axis=0, tiled=True)]
    all_gather x1, blocking collectives: 9.96 us -> 14.2 us  [per_device(): rows_in = lax.all_gather(rows_in, 'x', axis=0, tiled=False)]
    all_to_all x4 -> x6, starting transfers between devices: 34.3 us -> 37.5 us  [exchange(): return lax.all_to_all(value, axis, split_axis=0, concat_axis=0, tiled=True)]
  transfers between devices with their start and end apart: 21 -> 27, of which waited for: 14 -> 15; matrix products, arithmetic and copies ran while one was open for 3% -> 2% of each run, Pallas kernels for 0% -> 0%
where the time goes in v5:
time: 303 us; the launch traced here: 301 us
  starting transfers between devices  188 us (62%)
  waiting for transfers between devices  81 us (27%)
  blocking collectives  14.2 us (5%)
  local copies, waits for them, and re-layouts  7.29 us (2%)
  Pallas kernels  7.2 us (2%)
  other arithmetic  3.18 us (1%)
    ppermute x9, starting transfers between devices, swap(): return lax.ppermute(value, axis, [(0, 1), (1, 0)])  92.8 us
    ppermute x12, starting transfers between devices, around(): return lax.ppermute(value, RING, [(i, (i + hops) % 32) for i in range(32)])  57.7 us
    all_to_all x6, starting transfers between devices, exchange(): return lax.all_to_all(value, axis, split_axis=0, concat_axis=0, tiled=True)  37.5 us
    ppermute x9, waiting for transfers between devices, swap(): return lax.ppermute(value, axis, [(0, 1), (1, 0)])  29.6 us
    ppermute x12, waiting for transfers between devices, around(): return lax.ppermute(value, RING, [(i, (i + hops) % 32) for i in range(32)])  28.7 us
    all_to_all x6, waiting for transfers between devices, exchange(): return lax.all_to_all(value, axis, split_axis=0, concat_axis=0, tiled=True)  22.7 us
    all_gather x1, blocking collectives, per_device(): rows_in = lax.all_gather(rows_in, 'x', axis=0, tiled=False)  14.2 us
  transfers between devices with their start and end apart: 27, of which 15 were waited for; matrix products, arithmetic and copies ran while one was open for 2% of the time, Pallas kernels for 0%

profile of v5, /device:TPU:1, one launch (start us, length us, event | category | flops | bytes accessed | tf_op | source)
XLA Modules:
  0.0 301.3 jit_solution(18128544583328074416)
XLA Ops:
  0.0 3.2 %copy.28 = bf16[16,4,128,128]{3,2,0,1:T(8,128)(2,1)} copy(bf16[16,4,128,128]{3,2,1,0:T(8,128)(2,1)} %bitcast.63) | data formatting | bytes 4194304 | tf_op jit(solution)/shard_map/reshape | solution.py:143
  3.2 5.0 %all-to-all-start = ((bf16[4,16,128,128]{3,2,1,0:T(8,128)(2,1)}), bf16[4,16,128,128]{3,2,1,0:T(8,128)(2,1)S(1)}, u32[]{:S(2)}, u32[]{:S(2)}) async-start(bf16[4,16,128,128]{3,2,1,0:T(8,128)(2,1)} %bitcast.58), calls=%async_computation | async-start | bytes 4194304 | tf_op jit(solution)/shard_map/all_to_all | solution.py:120
  8.2 15.4 %collective-permute-start = (bf16[1,256,128]{2,1,0:T(8,128)(2,1)S(1)}, bf16[1,256,128]{2,1,0:T(8,128)(2,1)S(1)}, u32[]{:S(2)}, u32[]{:S(2)}) collective-permute-start(bf16[1,256,128]{2,1,0:T(8,128)(2,1)S(1)} %bitcast.76), channel_id=1, source_target_pairs={{0,32},{32,0},{1,33},{33,1},{2,34},{34,2},{3,35},{35,3},{4,36},{36... | collective-permute-start | bytes 196616 | tf_op jit(solution)/shard_map/ppermute | solution.py:25
  25.3 12.1 %collective-permute-start.2 = (bf16[1,256,128]{2,1,0:T(8,128)(2,1)S(1)}, bf16[1,256,128]{2,1,0:T(8,128)(2,1)S(1)}, u32[]{:S(2)}, u32[]{:S(2)}) collective-permute-start(bf16[1,256,128]{2,1,0:T(8,128)(2,1)S(1)} %bitcast.78), channel_id=1, source_target_pairs={{0,32},{32,0},{1,33},{33,1},{2,34},{34,2},{3,35},{35,3},{4,36},{36... | collective-permute-start | bytes 196616 | tf_op jit(solution)/shard_map/ppermute | solution.py:25
  37.4 13.6 %collective-permute-start.1 = (bf16[2,256,128]{2,1,0:T(8,128)(2,1)S(1)}, bf16[2,256,128]{2,1,0:T(8,128)(2,1)S(1)}, u32[]{:S(2)}, u32[]{:S(2)}) collective-permute-start(bf16[2,256,128]{2,1,0:T(8,128)(2,1)S(1)} %pad_maximum_fusion.4), channel_id=1, source_target_pairs={{0,16},{16,0},{1,17},{17,1},{2,18},{18,2},{3,19},{19,3},{4,20},{20... | collective-permute-start | bytes 393224 | tf_op jit(solution)/shard_map/ppermute | solution.py:25
  51.0 3.2 %copy.27 = bf16[16,4,128,128]{3,2,0,1:T(8,128)(2,1)} copy(bf16[16,4,128,128]{3,2,1,0:T(8,128)(2,1)} %bitcast.64) | data formatting | bytes 4194304 | tf_op jit(solution)/shard_map/reshape | solution.py:142
  54.3 9.6 %collective-permute-start.3 = (bf16[4,256,128]{2,1,0:T(8,128)(2,1)S(1)}, bf16[4,256,128]{2,1,0:T(8,128)(2,1)}, u32[]{:S(2)}, u32[]{:S(2)}) collective-permute-start(bf16[4,256,128]{2,1,0:T(8,128)(2,1)S(1)} %pad_maximum_fusion.2), channel_id=1, source_target_pairs={{0,8},{8,0},{1,9},{9,1},{2,10},{10,2},{3,11},{11,3},{4,12},{12,4},... | collective-permute-start | bytes 786440 | tf_op jit(solution)/shard_map/ppermute | solution.py:25
  63.9 8.0 %collective-permute-start.4 = (bf16[2,256,128]{2,1,0:T(8,128)(2,1)S(1)}, bf16[2,256,128]{2,1,0:T(8,128)(2,1)S(1)}, u32[]{:S(2)}, u32[]{:S(2)}) collective-permute-start(bf16[2,256,128]{2,1,0:T(8,128)(2,1)S(1)} %pad_maximum_fusion.5), channel_id=1, source_target_pairs={{0,16},{16,0},{1,17},{17,1},{2,18},{18,2},{3,19},{19,3},{4,20},{20... | collective-permute-start | bytes 393224 | tf_op jit(solution)/shard_map/ppermute | solution.py:25
  72.6 5.6 %all-to-all-start.1 = ((bf16[8,2,8,512]{3,2,1,0:T(8,128)(2,1)}), bf16[8,2,8,512]{3,2,1,0:T(8,128)(2,1)S(1)}, u32[]{:S(2)}, u32[]{:S(2)}) async-start(bf16[8,2,8,512]{3,2,1,0:T(8,128)(2,1)} %bitcast.9), calls=%async_computation.1 | async-start | bytes 262144 | tf_op jit(solution)/shard_map/all_to_all | solution.py:120
  79.2 4.2 %all-to-all-done.1 = bf16[8,2,8,512]{3,2,1,0:T(8,128)(2,1)S(1)} async-done(((bf16[8,2,8,512]{3,2,1,0:T(8,128)(2,1)}), bf16[8,2,8,512]{3,2,1,0:T(8,128)(2,1)S(1)}, u32[]{:S(2)}, u32[]{:S(2)}) %all-to-all-start.1) | async-done | bytes 131104 | tf_op jit(solution)/shard_map/all_to_all | solution.py:120
  83.5 4.5 %all-to-all-start.2 = ((bf16[4,16,128,128]{3,2,1,0:T(8,128)(2,1)}), bf16[4,16,128,128]{3,2,1,0:T(8,128)(2,1)}, u32[]{:S(2)}, u32[]{:S(2)}) async-start(bf16[4,16,128,128]{3,2,1,0:T(8,128)(2,1)} %bitcast.57), calls=%async_computation.2 | async-start | bytes 4194304 | tf_op jit(solution)/shard_map/all_to_all | solution.py:120
  87.9 5.8 %collective-permute-start.5 = (bf16[8,256,128]{2,1,0:T(8,128)(2,1)S(1)}, bf16[8,256,128]{2,1,0:T(8,128)(2,1)}, u32[]{:S(2)}, u32[]{:S(2)}) collective-permute-start(bf16[8,256,128]{2,1,0:T(8,128)(2,1)S(1)} %pad_maximum_fusion.near_ref), channel_id=1, source_target_pairs={{0,4},{4,0},{1,5},{5,1},{2,6},{6,2},{3,7},{7,3},{8,12},{12,8},{9,1... | collective-permute-start | bytes 1572872 | tf_op jit(solution)/shard_map/ppermute | solution.py:25
  96.3 13.4 %collective-permute-done.6 = bf16[4,256,128]{2,1,0:T(8,128)(2,1)} collective-permute-done((bf16[4,256,128]{2,1,0:T(8,128)(2,1)S(1)}, bf16[4,256,128]{2,1,0:T(8,128)(2,1)}, u32[]{:S(2)}, u32[]{:S(2)}) %collective-permute-start.6) | collective-permute-done | bytes 262176 | tf_op jit(solution)/shard_map/ppermute | solution.py:25
  115.8 3.4 %all-to-all-start.3 = ((bf16[4,256,128]{2,1,0:T(8,128)(2,1)}), bf16[4,256,128]{2,1,0:T(8,128)(2,1)S(1)}, u32[]{:S(2)}, u32[]{:S(2)}) async-start(bf16[4,256,128]{2,1,0:T(8,128)(2,1)} %project.2), calls=%async_computation.3 | async-start | bytes 524288 | tf_op jit(solution)/shard_map/all_to_all | solution.py:120
  119.3 5.8 %collective-permute-start.7 = (bf16[8,256,128]{2,1,0:T(8,128)(2,1)S(1)}, bf16[8,256,128]{2,1,0:T(8,128)(2,1)S(1)}, u32[]{:S(2)}, u32[]{:S(2)}) collective-permute-start(bf16[8,256,128]{2,1,0:T(8,128)(2,1)S(1)} %pad_maximum_fusion.1.near_ref), channel_id=1, source_target_pairs={{0,4},{4,0},{1,5},{5,1},{2,6},{6,2},{3,7},{7,3},{8,12},{12,8},{9,1... | collective-permute-start | bytes 1572872 | tf_op jit(solution)/shard_map/ppermute | solution.py:25
  125.3 10.2 %collective-permute-done.7.far_ref = bf16[8,256,128]{2,1,0:T(8,128)(2,1)S(1)} collective-permute-done((bf16[8,256,128]{2,1,0:T(8,128)(2,1)S(1)}, bf16[8,256,128]{2,1,0:T(8,128)(2,1)S(1)}, u32[]{:S(2)}, u32[]{:S(2)}) %collective-permute-start.7) | collective-permute-done | bytes 524320 | tf_op jit(solution)/shard_map/ppermute | solution.py:25
  135.5 3.0 project.3
  138.5 3.9 %all-to-all-start.4 = ((bf16[4,256,128]{2,1,0:T(8,128)(2,1)}), bf16[4,256,128]{2,1,0:T(8,128)(2,1)S(1)}, u32[]{:S(2)}, u32[]{:S(2)}) async-start(bf16[4,256,128]{2,1,0:T(8,128)(2,1)} %project.3), calls=%async_computation.4 | async-start | bytes 524288 | tf_op jit(solution)/shard_map/all_to_all | solution.py:120
  142.4 19.8 %collective-permute-start.8 = (bf16[64,768]{1,0:T(8,128)(2,1)S(1)}, bf16[64,768]{1,0:T(8,128)(2,1)S(1)}, u32[]{:S(2)}, u32[]{:S(2)}) collective-permute-start(bf16[64,768]{1,0:T(8,128)(2,1)S(1)} %pad_maximum_fusion.6), channel_id=1, source_target_pairs={{0,128},{128,0},{1,129},{129,1},{2,130},{130,2},{3,131},{131,3},{4... | collective-permute-start | bytes 294920 | tf_op jit(solution)/shard_map/ppermute | solution.py:25
  162.3 4.2 %collective-permute-done.8 = bf16[64,768]{1,0:T(8,128)(2,1)S(1)} collective-permute-done((bf16[64,768]{1,0:T(8,128)(2,1)S(1)}, bf16[64,768]{1,0:T(8,128)(2,1)S(1)}, u32[]{:S(2)}, u32[]{:S(2)}) %collective-permute-start.8) | collective-permute-done | bytes 98336 | tf_op jit(solution)/shard_map/ppermute | solution.py:25
  166.5 9.1 %collective-permute-start.10 = (bf16[256,128]{1,0:T(8,128)(2,1)S(1)}, bf16[256,128]{1,0:T(8,128)(2,1)S(1)}, u32[]{:S(2)}, u32[]{:S(2)}) collective-permute-start(bf16[256,128]{1,0:T(8,128)(2,1)S(1)} %multiply_convert_fusion.own), channel_id=1, source_target_pairs={{0,176},{4,180},{8,184},{12,188},{16,0},{20,4},{24,8},{28,12},{32,... | collective-permute-start | bytes 196616 | tf_op jit(solution)/shard_map/ppermute | solution.py:29
  177.6 9.5 %collective-permute-done.10.refs_0_ = bf16[256,128]{1,0:T(8,128)(2,1)S(1)} collective-permute-done((bf16[256,128]{1,0:T(8,128)(2,1)S(1)}, bf16[256,128]{1,0:T(8,128)(2,1)S(1)}, u32[]{:S(2)}, u32[]{:S(2)}) %collective-permute-start.10) | collective-permute-done | bytes 65568 | tf_op jit(solution)/shard_map/ppermute | solution.py:29
  187.1 6.3 %collective-permute-start.11 = (bf16[256,128]{1,0:T(8,128)(2,1)S(1)}, bf16[256,128]{1,0:T(8,128)(2,1)S(1)}, u32[]{:S(2)}, u32[]{:S(2)}) collective-permute-start(bf16[256,128]{1,0:T(8,128)(2,1)S(1)} %collective-permute-done.9.refs_5_), channel_id=1, source_target_pairs={{0,16},{4,20},{8,24},{12,28},{16,32},{20,36},{24,40},{28,44},{32,4... | collective-permute-start | bytes 196616 | tf_op jit(solution)/shard_map/ppermute | solution.py:29
  196.4 6.6 %collective-permute-done.12.refs_1_ = bf16[256,128]{1,0:T(8,128)(2,1)S(1)} collective-permute-done((bf16[256,128]{1,0:T(8,128)(2,1)S(1)}, bf16[256,128]{1,0:T(8,128)(2,1)S(1)}, u32[]{:S(2)}, u32[]{:S(2)}) %collective-permute-start.12) | collective-permute-done | bytes 65568 | tf_op jit(solution)/shard_map/ppermute | solution.py:29
  203.0 7.7 %collective-permute-start.13 = (bf16[256,128]{1,0:T(8,128)(2,1)S(1)}, bf16[256,128]{1,0:T(8,128)(2,1)S(1)}, u32[]{:S(2)}, u32[]{:S(2)}) collective-permute-start(bf16[256,128]{1,0:T(8,128)(2,1)S(1)} %collective-permute-done.11.refs_4_), channel_id=1, source_target_pairs={{0,16},{4,20},{8,24},{12,28},{16,32},{20,36},{24,40},{28,44},{32,4... | collective-permute-start | bytes 196616 | tf_op jit(solution)/shard_map/ppermute | solution.py:29
  212.7 7.7 %collective-permute-done.14.refs_2_ = bf16[256,128]{1,0:T(8,128)(2,1)S(1)} collective-permute-done((bf16[256,128]{1,0:T(8,128)(2,1)S(1)}, bf16[256,128]{1,0:T(8,128)(2,1)S(1)}, u32[]{:S(2)}, u32[]{:S(2)}) %collective-permute-start.14) | collective-permute-done | bytes 65568 | tf_op jit(solution)/shard_map/ppermute | solution.py:29
  222.3 7.3 %collective-permute-start.15 = (bf16[128,128]{1,0:T(8,128)(2,1)S(1)}, bf16[128,128]{1,0:T(8,128)(2,1)S(1)}, u32[]{:S(2)}, u32[]{:S(2)}) collective-permute-start(bf16[128,128]{1,0:T(8,128)(2,1)S(1)} %slice.54), channel_id=1, source_target_pairs={{0,16},{4,20},{8,24},{12,28},{16,32},{20,36},{24,40},{28,44},{32,4... | collective-permute-start | bytes 98312 | tf_op jit(solution)/shard_map/ppermute | solution.py:29
  231.2 9.5 %collective-permute-start.18 = (bf16[8,256,128]{2,1,0:T(8,128)(2,1)S(1)}, bf16[8,256,128]{2,1,0:T(8,128)(2,1)S(1)}, u32[]{:S(2)}, u32[]{:S(2)}) collective-permute-start(bf16[8,256,128]{2,1,0:T(8,128)(2,1)S(1)} %place.1.p0), channel_id=1, source_target_pairs={{0,188},{4,0},{8,4},{12,8},{16,12},{20,16},{24,20},{28,24},{32,28}... | collective-permute-start | bytes 1572872 | tf_op jit(solution)/shard_map/ppermute | solution.py:29
  242.6 14.2 %all-gather = bf16[8,64,256]{2,1,0:T(8,128)(2,1)S(1)} all-gather(bf16[2,64,256]{2,1,0:T(8,128)(2,1)S(1)} %pad_maximum_fusion.7), channel_id=2, replica_groups=mesh['y'=4,'zh'=2,'c'=2,'z8'=2,'z4'=2,'z2'=2,'z1'=2,'x'=4] {'x'}, dimensions={0}, use_global_device_ids=true | all-gather | bytes 327680 | tf_op jit(solution)/shard_map/all_gather | solution.py:178
  258.8 5.3 %collective-permute-start.19 = (bf16[4,256,128]{2,1,0:T(8,128)(2,1)S(1)}, bf16[4,256,128]{2,1,0:T(8,128)(2,1)S(1)}, u32[]{:S(2)}, u32[]{:S(2)}) collective-permute-start(bf16[4,256,128]{2,1,0:T(8,128)(2,1)S(1)} %slice.58), channel_id=1, source_target_pairs={{0,188},{4,0},{8,4},{12,8},{16,12},{20,16},{24,20},{28,24},{32,28}... | collective-permute-start | bytes 786440 | tf_op jit(solution)/shard_map/ppermute | solution.py:29
  269.1 15.1 %all-to-all-start.5 = ((bf16[32,8,2048]{2,1,0:T(8,128)(2,1)}), bf16[32,8,2048]{2,1,0:T(8,128)(2,1)S(1)}, u32[]{:S(2)}, u32[]{:S(2)}) async-start(bf16[32,8,2048]{2,1,0:T(8,128)(2,1)} %scale.1), calls=%async_computation.5 | async-start | bytes 2097152 | tf_op jit(solution)/shard_map/all_to_all | solution.py:120
  284.2 16.0 %all-to-all-done.5 = bf16[32,8,2048]{2,1,0:T(8,128)(2,1)S(1)} async-done(((bf16[32,8,2048]{2,1,0:T(8,128)(2,1)}), bf16[32,8,2048]{2,1,0:T(8,128)(2,1)S(1)}, u32[]{:S(2)}, u32[]{:S(2)}) %all-to-all-start.5) | async-done | bytes 1048608 | tf_op jit(solution)/shard_map/all_to_all | solution.py:120
  (69 shorter events, 32.5 us)
Async XLA Ops:
  3.2 5.0 %copy-start.1 = (bf16[256,128]{1,0:T(8,128)(2,1)S(1)}, bf16[256,128]{1,0:T(8,128)(2,1)}, u32[]{:S(2)}) copy-start(bf16[256,128]{1,0:T(8,128)(2,1)} %param.5) | copy-start | bytes 196612
  3.2 22.1 %copy-start.2 = (bf16[256,128]{1,0:T(8,128)(2,1)S(1)}, bf16[256,128]{1,0:T(8,128)(2,1)}, u32[]{:S(2)}) copy-start(bf16[256,128]{1,0:T(8,128)(2,1)} %param.6) | copy-start | bytes 196612
  3.2 51.1 %all-to-all-start = ((bf16[4,16,128,128]{3,2,1,0:T(8,128)(2,1)}), bf16[4,16,128,128]{3,2,1,0:T(8,128)(2,1)S(1)}, u32[]{:S(2)}, u32[]{:S(2)}) async-start(bf16[4,16,128,128]{3,2,1,0:T(8,128)(2,1)} %bitcast.58), calls=%async_computation | async-start | bytes 4194304 | tf_op jit(solution)/shard_map/all_to_all | solution.py:120
  8.2 17.1 %collective-permute-start = (bf16[1,256,128]{2,1,0:T(8,128)(2,1)S(1)}, bf16[1,256,128]{2,1,0:T(8,128)(2,1)S(1)}, u32[]{:S(2)}, u32[]{:S(2)}) collective-permute-start(bf16[1,256,128]{2,1,0:T(8,128)(2,1)S(1)} %bitcast.76), channel_id=1, source_target_pairs={{0,32},{32,0},{1,33},{33,1},{2,34},{34,2},{3,35},{35,3},{4,36},{36... | collective-permute-start | bytes 196616 | tf_op jit(solution)/shard_map/ppermute | solution.py:25
  25.3 28.9 %collective-permute-start.2 = (bf16[1,256,128]{2,1,0:T(8,128)(2,1)S(1)}, bf16[1,256,128]{2,1,0:T(8,128)(2,1)S(1)}, u32[]{:S(2)}, u32[]{:S(2)}) collective-permute-start(bf16[1,256,128]{2,1,0:T(8,128)(2,1)S(1)} %bitcast.78), channel_id=1, source_target_pairs={{0,32},{32,0},{1,33},{33,1},{2,34},{34,2},{3,35},{35,3},{4,36},{36... | collective-permute-start | bytes 196616 | tf_op jit(solution)/shard_map/ppermute | solution.py:25
  37.4 16.9 %collective-permute-start.1 = (bf16[2,256,128]{2,1,0:T(8,128)(2,1)S(1)}, bf16[2,256,128]{2,1,0:T(8,128)(2,1)S(1)}, u32[]{:S(2)}, u32[]{:S(2)}) collective-permute-start(bf16[2,256,128]{2,1,0:T(8,128)(2,1)S(1)} %pad_maximum_fusion.4), channel_id=1, source_target_pairs={{0,16},{16,0},{1,17},{17,1},{2,18},{18,2},{3,19},{19,3},{4,20},{20... | collective-permute-start | bytes 393224 | tf_op jit(solution)/shard_map/ppermute | solution.py:25
  51.0 20.9 %copy-start = (bf16[128,512]{1,0:T(8,128)(2,1)S(1)}, bf16[128,512]{1,0:T(8,128)(2,1)}, u32[]{:S(2)}) copy-start(bf16[128,512]{1,0:T(8,128)(2,1)} %param.9) | copy-start | bytes 393220
  54.3 23.9 %collective-permute-start.3 = (bf16[4,256,128]{2,1,0:T(8,128)(2,1)S(1)}, bf16[4,256,128]{2,1,0:T(8,128)(2,1)}, u32[]{:S(2)}, u32[]{:S(2)}) collective-permute-start(bf16[4,256,128]{2,1,0:T(8,128)(2,1)S(1)} %pad_maximum_fusion.2), channel_id=1, source_target_pairs={{0,8},{8,0},{1,9},{9,1},{2,10},{10,2},{3,11},{11,3},{4,12},{12,4},... | collective-permute-start | bytes 786440 | tf_op jit(solution)/shard_map/ppermute | solution.py:25
  63.9 14.3 %collective-permute-start.4 = (bf16[2,256,128]{2,1,0:T(8,128)(2,1)S(1)}, bf16[2,256,128]{2,1,0:T(8,128)(2,1)S(1)}, u32[]{:S(2)}, u32[]{:S(2)}) collective-permute-start(bf16[2,256,128]{2,1,0:T(8,128)(2,1)S(1)} %pad_maximum_fusion.5), channel_id=1, source_target_pairs={{0,16},{16,0},{1,17},{17,1},{2,18},{18,2},{3,19},{19,3},{4,20},{20... | collective-permute-start | bytes 393224 | tf_op jit(solution)/shard_map/ppermute | solution.py:25
  72.6 10.9 %all-to-all-start.1 = ((bf16[8,2,8,512]{3,2,1,0:T(8,128)(2,1)}), bf16[8,2,8,512]{3,2,1,0:T(8,128)(2,1)S(1)}, u32[]{:S(2)}, u32[]{:S(2)}) async-start(bf16[8,2,8,512]{3,2,1,0:T(8,128)(2,1)} %bitcast.9), calls=%async_computation.1 | async-start | bytes 262144 | tf_op jit(solution)/shard_map/all_to_all | solution.py:120
  83.5 29.9 %all-to-all-start.2 = ((bf16[4,16,128,128]{3,2,1,0:T(8,128)(2,1)}), bf16[4,16,128,128]{3,2,1,0:T(8,128)(2,1)}, u32[]{:S(2)}, u32[]{:S(2)}) async-start(bf16[4,16,128,128]{3,2,1,0:T(8,128)(2,1)} %bitcast.57), calls=%async_computation.2 | async-start | bytes 4194304 | tf_op jit(solution)/shard_map/all_to_all | solution.py:120
  87.9 22.9 %collective-permute-start.5 = (bf16[8,256,128]{2,1,0:T(8,128)(2,1)S(1)}, bf16[8,256,128]{2,1,0:T(8,128)(2,1)}, u32[]{:S(2)}, u32[]{:S(2)}) collective-permute-start(bf16[8,256,128]{2,1,0:T(8,128)(2,1)S(1)} %pad_maximum_fusion.near_ref), channel_id=1, source_target_pairs={{0,4},{4,0},{1,5},{5,1},{2,6},{6,2},{3,7},{7,3},{8,12},{12,8},{9,1... | collective-permute-start | bytes 1572872 | tf_op jit(solution)/shard_map/ppermute | solution.py:25
  93.8 15.9 %collective-permute-start.6 = (bf16[4,256,128]{2,1,0:T(8,128)(2,1)S(1)}, bf16[4,256,128]{2,1,0:T(8,128)(2,1)}, u32[]{:S(2)}, u32[]{:S(2)}) collective-permute-start(bf16[4,256,128]{2,1,0:T(8,128)(2,1)S(1)} %pad_maximum_fusion.3), channel_id=1, source_target_pairs={{0,8},{8,0},{1,9},{9,1},{2,10},{10,2},{3,11},{11,3},{4,12},{12,4},... | collective-permute-start | bytes 786440 | tf_op jit(solution)/shard_map/ppermute | solution.py:25
  115.8 9.3 %all-to-all-start.3 = ((bf16[4,256,128]{2,1,0:T(8,128)(2,1)}), bf16[4,256,128]{2,1,0:T(8,128)(2,1)S(1)}, u32[]{:S(2)}, u32[]{:S(2)}) async-start(bf16[4,256,128]{2,1,0:T(8,128)(2,1)} %project.2), calls=%async_computation.3 | async-start | bytes 524288 | tf_op jit(solution)/shard_map/all_to_all | solution.py:120
  119.3 16.2 %collective-permute-start.7 = (bf16[8,256,128]{2,1,0:T(8,128)(2,1)S(1)}, bf16[8,256,128]{2,1,0:T(8,128)(2,1)S(1)}, u32[]{:S(2)}, u32[]{:S(2)}) collective-permute-start(bf16[8,256,128]{2,1,0:T(8,128)(2,1)S(1)} %pad_maximum_fusion.1.near_ref), channel_id=1, source_target_pairs={{0,4},{4,0},{1,5},{5,1},{2,6},{6,2},{3,7},{7,3},{8,12},{12,8},{9,1... | collective-permute-start | bytes 1572872 | tf_op jit(solution)/shard_map/ppermute | solution.py:25
  138.5 28.0 %all-to-all-start.4 = ((bf16[4,256,128]{2,1,0:T(8,128)(2,1)}), bf16[4,256,128]{2,1,0:T(8,128)(2,1)S(1)}, u32[]{:S(2)}, u32[]{:S(2)}) async-start(bf16[4,256,128]{2,1,0:T(8,128)(2,1)} %project.3), calls=%async_computation.4 | async-start | bytes 524288 | tf_op jit(solution)/shard_map/all_to_all | solution.py:120
  142.4 24.0 %collective-permute-start.8 = (bf16[64,768]{1,0:T(8,128)(2,1)S(1)}, bf16[64,768]{1,0:T(8,128)(2,1)S(1)}, u32[]{:S(2)}, u32[]{:S(2)}) collective-permute-start(bf16[64,768]{1,0:T(8,128)(2,1)S(1)} %pad_maximum_fusion.6), channel_id=1, source_target_pairs={{0,128},{128,0},{1,129},{129,1},{2,130},{130,2},{3,131},{131,3},{4... | collective-permute-start | bytes 294920 | tf_op jit(solution)/shard_map/ppermute | solution.py:25
  166.5 20.6 %collective-permute-start.10 = (bf16[256,128]{1,0:T(8,128)(2,1)S(1)}, bf16[256,128]{1,0:T(8,128)(2,1)S(1)}, u32[]{:S(2)}, u32[]{:S(2)}) collective-permute-start(bf16[256,128]{1,0:T(8,128)(2,1)S(1)} %multiply_convert_fusion.own), channel_id=1, source_target_pairs={{0,176},{4,180},{8,184},{12,188},{16,0},{20,4},{24,8},{28,12},{32,... | collective-permute-start | bytes 196616 | tf_op jit(solution)/shard_map/ppermute | solution.py:29
  175.6 11.5 %collective-permute-start.9 = (bf16[256,128]{1,0:T(8,128)(2,1)S(1)}, bf16[256,128]{1,0:T(8,128)(2,1)S(1)}, u32[]{:S(2)}, u32[]{:S(2)}) collective-permute-start(bf16[256,128]{1,0:T(8,128)(2,1)S(1)} %multiply_convert_fusion.own), channel_id=1, source_target_pairs={{0,16},{4,20},{8,24},{12,28},{16,32},{20,36},{24,40},{28,44},{32,4... | collective-permute-start | bytes 196616 | tf_op jit(solution)/shard_map/ppermute | solution.py:29
  187.1 9.2 %collective-permute-start.11 = (bf16[256,128]{1,0:T(8,128)(2,1)S(1)}, bf16[256,128]{1,0:T(8,128)(2,1)S(1)}, u32[]{:S(2)}, u32[]{:S(2)}) collective-permute-start(bf16[256,128]{1,0:T(8,128)(2,1)S(1)} %collective-permute-done.9.refs_5_), channel_id=1, source_target_pairs={{0,16},{4,20},{8,24},{12,28},{16,32},{20,36},{24,40},{28,44},{32,4... | collective-permute-start | bytes 196616 | tf_op jit(solution)/shard_map/ppermute | solution.py:29
  193.5 9.5 %collective-permute-start.12 = (bf16[256,128]{1,0:T(8,128)(2,1)S(1)}, bf16[256,128]{1,0:T(8,128)(2,1)S(1)}, u32[]{:S(2)}, u32[]{:S(2)}) collective-permute-start(bf16[256,128]{1,0:T(8,128)(2,1)S(1)} %collective-permute-done.10.refs_0_), channel_id=1, source_target_pairs={{0,176},{4,180},{8,184},{12,188},{16,0},{20,4},{24,8},{28,12},{32,... | collective-permute-start | bytes 196616 | tf_op jit(solution)/shard_map/ppermute | solution.py:29
  203.0 9.7 %collective-permute-start.13 = (bf16[256,128]{1,0:T(8,128)(2,1)S(1)}, bf16[256,128]{1,0:T(8,128)(2,1)S(1)}, u32[]{:S(2)}, u32[]{:S(2)}) collective-permute-start(bf16[256,128]{1,0:T(8,128)(2,1)S(1)} %collective-permute-done.11.refs_4_), channel_id=1, source_target_pairs={{0,16},{4,20},{8,24},{12,28},{16,32},{20,36},{24,40},{28,44},{32,4... | collective-permute-start | bytes 196616 | tf_op jit(solution)/shard_map/ppermute | solution.py:29
  210.7 9.7 %collective-permute-start.14 = (bf16[256,128]{1,0:T(8,128)(2,1)S(1)}, bf16[256,128]{1,0:T(8,128)(2,1)S(1)}, u32[]{:S(2)}, u32[]{:S(2)}) collective-permute-start(bf16[256,128]{1,0:T(8,128)(2,1)S(1)} %collective-permute-done.12.refs_1_), channel_id=1, source_target_pairs={{0,176},{4,180},{8,184},{12,188},{16,0},{20,4},{24,8},{28,12},{32,... | collective-permute-start | bytes 196616 | tf_op jit(solution)/shard_map/ppermute | solution.py:29
  220.4 9.9 %collective-permute-start.16 = (bf16[128,128]{1,0:T(8,128)(2,1)S(1)}, bf16[128,128]{1,0:T(8,128)(2,1)S(1)}, u32[]{:S(2)}, u32[]{:S(2)}) collective-permute-start(bf16[128,128]{1,0:T(8,128)(2,1)S(1)} %slice.55), channel_id=1, source_target_pairs={{0,176},{4,180},{8,184},{12,188},{16,0},{20,4},{24,8},{28,12},{32,... | collective-permute-start | bytes 98312 | tf_op jit(solution)/shard_map/ppermute | solution.py:29
  222.3 8.8 %collective-permute-start.15 = (bf16[128,128]{1,0:T(8,128)(2,1)S(1)}, bf16[128,128]{1,0:T(8,128)(2,1)S(1)}, u32[]{:S(2)}, u32[]{:S(2)}) collective-permute-start(bf16[128,128]{1,0:T(8,128)(2,1)S(1)} %slice.54), channel_id=1, source_target_pairs={{0,16},{4,20},{8,24},{12,28},{16,32},{20,36},{24,40},{28,44},{32,4... | collective-permute-start | bytes 98312 | tf_op jit(solution)/shard_map/ppermute | solution.py:29
  231.2 25.6 %collective-permute-start.18 = (bf16[8,256,128]{2,1,0:T(8,128)(2,1)S(1)}, bf16[8,256,128]{2,1,0:T(8,128)(2,1)S(1)}, u32[]{:S(2)}, u32[]{:S(2)}) collective-permute-start(bf16[8,256,128]{2,1,0:T(8,128)(2,1)S(1)} %place.1.p0), channel_id=1, source_target_pairs={{0,188},{4,0},{8,4},{12,8},{16,12},{20,16},{24,20},{28,24},{32,28}... | collective-permute-start | bytes 1572872 | tf_op jit(solution)/shard_map/ppermute | solution.py:29
  240.7 16.1 %collective-permute-start.17 = (bf16[8,256,128]{2,1,0:T(8,128)(2,1)S(1)}, bf16[8,256,128]{2,1,0:T(8,128)(2,1)S(1)}, u32[]{:S(2)}, u32[]{:S(2)}) collective-permute-start(bf16[8,256,128]{2,1,0:T(8,128)(2,1)S(1)} %place.1.p0), channel_id=1, source_target_pairs={{0,4},{4,8},{8,12},{12,16},{16,20},{20,24},{24,28},{28,32},{32,36}... | collective-permute-start | bytes 1572872 | tf_op jit(solution)/shard_map/ppermute | solution.py:29
  256.9 9.0 %collective-permute-start.20 = (bf16[4,256,128]{2,1,0:T(8,128)(2,1)S(1)}, bf16[4,256,128]{2,1,0:T(8,128)(2,1)S(1)}, u32[]{:S(2)}, u32[]{:S(2)}) collective-permute-start(bf16[4,256,128]{2,1,0:T(8,128)(2,1)S(1)} %slice.59), channel_id=1, source_target_pairs={{0,4},{4,8},{8,12},{12,16},{16,20},{20,24},{24,28},{28,32},{32,36}... | collective-permute-start | bytes 786440 | tf_op jit(solution)/shard_map/ppermute | solution.py:29
  258.8 8.6 %collective-permute-start.19 = (bf16[4,256,128]{2,1,0:T(8,128)(2,1)S(1)}, bf16[4,256,128]{2,1,0:T(8,128)(2,1)S(1)}, u32[]{:S(2)}, u32[]{:S(2)}) collective-permute-start(bf16[4,256,128]{2,1,0:T(8,128)(2,1)S(1)} %slice.58), channel_id=1, source_target_pairs={{0,188},{4,0},{8,4},{12,8},{16,12},{20,16},{24,20},{28,24},{32,28}... | collective-permute-start | bytes 786440 | tf_op jit(solution)/shard_map/ppermute | solution.py:29
  269.1 31.1 %all-to-all-start.5 = ((bf16[32,8,2048]{2,1,0:T(8,128)(2,1)}), bf16[32,8,2048]{2,1,0:T(8,128)(2,1)S(1)}, u32[]{:S(2)}, u32[]{:S(2)}) async-start(bf16[32,8,2048]{2,1,0:T(8,128)(2,1)} %scale.1), calls=%async_computation.5 | async-start | bytes 2097152 | tf_op jit(solution)/shard_map/all_to_all | solution.py:120

commit v6 on v4

--- a/solution.py
+++ b/solution.py
@@ -14,9 +14,6 @@
 PARAMS = pltpu.CompilerParams(vmem_limit_bytes=16 * 2**20)
 SCALAR = pl.BlockSpec(memory_space=pltpu.SMEM)
 WHOLE = pl.BlockSpec(memory_space=pltpu.VMEM)
-ARRIVAL = [0, 8, 4, 12, 2, 10, 6, 14, 1, 9, 5, 13, 3, 11, 7, 15]
-
-
 def together(*values):
     return lax.optimization_barrier(values)
 
@@ -29,21 +26,17 @@
     return lax.ppermute(value, RING, [(i, (i + hops) % 32) for i in range(32)])
 
 
-def double_z(have, axis):
-    return jnp.concatenate([have, swap(have, axis)], axis=0)
-
-
 def project_kernel(z_ref, near_ref, far_ref, basis_out_ref, basis_in_ref, out_ref):
-    z = z_ref[0]
+    residue = lax.rem(z_ref[0], 4)
     for m, basis_ref in enumerate((basis_out_ref, basis_in_ref)):
         for pair in range(2):
             total = jnp.zeros((256, 256), f32)
             for step in range(8):
                 source = near_ref if step < 4 else far_ref
-                at = 2 * step if step < 4 else 2 * step - 8
+                at = 2 * (step % 4)
                 left = jnp.concatenate([source[at, m], source[at + 1, m]], axis=1)
-                z0 = z ^ ARRIVAL[2 * step]
-                z1 = z ^ ARRIVAL[2 * step + 1]
+                z0 = 4 * (at % 4) + (residue ^ (2 * (at // 4) + step // 4))
+                z1 = z0 + 4
                 columns = [
                     jnp.concatenate([basis_ref[2 * pair + i, z0], basis_ref[2 * pair + i, z1]], axis=0) for i in range(2)
                 ]
@@ -63,30 +56,6 @@
         cost_estimate=pl.CostEstimate(flops=4 * 256 * 2048 * 512, bytes_accessed=6800000, transcendentals=0),
         name="project",
     )(z, near, far, basis_out, basis_in)
-
-
-def place_kernel(a_ref, own, *refs):
-    *blocks, half_low, half_high, out_ref = refs
-    out_ref[a_ref[0]] = own[...]
-    for k, block in zip((1, 2, 3, 5, 6, 7), blocks):
-        at = lax.rem(a_ref[0] + k, 8)
-        out_ref[at, :128] = block[:128]
-        out_ref[at, 128:] = block[192:]
-    far = lax.rem(a_ref[0] + 4, 8)
-    out_ref[far, :128] = half_low[:128]
-    out_ref[far, 128:] = half_high[64:]
-
-
-def place(a, own, blocks, halves):
-    return pl.pallas_call(
-        place_kernel,
-        out_shape=jax.ShapeDtypeStruct((8, 256, 128), bf16),
-        in_specs=[SCALAR] + [WHOLE] * 9,
-        out_specs=WHOLE,
-        compiler_params=PARAMS,
-        cost_estimate=pl.CostEstimate(flops=0, bytes_accessed=1100000, transcendentals=0),
-        name="place",
-    )(a, own, *blocks, *halves)
 
 
 def scale_kernel(rows_ref, p0, p1, p2a, p2b, p3, out_ref):
@@ -137,47 +106,33 @@
         return jnp.stack([jnp.where(high, other, own), jnp.where(high, own, other)])
 
     basis_out = basis_out.reshape(16, X, 128, 128).transpose(1, 0, 2, 3)
-    basis_in = basis_in.reshape(16, X, 128, 128).transpose(1, 0, 2, 3)
 
-    grad = grad_eigen.reshape(Y, ZH, C * 8, 512).transpose(1, 0, 2, 3)
-    grad_own = mine(grad)
-    have, grad_other, basis_out = together(
-        double_z(jnp.stack([out_grads, activations])[None], "z8"), swap(theirs(grad), "zh"), basis_out
-    )
     b_out = exchange(basis_out, "x")
-    have, basis_in = together(double_z(have, "z4"), basis_in)
-    have, b_out = together(double_z(have, "z2"), b_out)
-    b_in = exchange(basis_in, "x")
-    far, have, b_in = together(swap(have, "z1"), have, b_in)
+    have = lax.all_gather(jnp.stack([out_grads, activations]), ("z8", "z4"), axis=0, tiled=False)
+    have, b_out, basis_in, grad_eigen = together(have, b_out, basis_in, grad_eigen)
+    b_in = exchange(basis_in.reshape(16, X, 128, 128).transpose(1, 0, 2, 3), "x")
+    have = jnp.concatenate([have, swap(have, "z2")], axis=0)
+    have, b_in, grad_eigen = together(have, b_in, grad_eigen)
+    grad = grad_eigen.reshape(Y, ZH, C, 8, 512).transpose(0, 2, 1, 3, 4).reshape(Y * C, ZH, 8, 512)
+    grad = exchange(grad, ("y", "c"))
+    far, have, grad = together(swap(have, "z1"), have, grad)
+    grad = grad.transpose(1, 0, 2, 3)
 
     part = project(z, have, far, b_out, b_in)
     projected = jnp.sum(exchange(part, "x").astype(f32), axis=0)
     squares = (projected * projected).astype(bf16)
-    squares_out = squares[0]
     squares_in = squares[1].T.reshape(Y, ZH, C * 8, tokens).transpose(1, 0, 2, 3).reshape(ZH, 64, tokens)
-    rows_own, rows_sent = mine(squares_in), theirs(squares_in)
 
-    up = jnp.concatenate([squares_out[:128], rows_sent[:, :128], squares_out[128:]], axis=0)
-    down = jnp.concatenate([squares_out[:128], rows_sent[:, 128:], squares_out[128:]], axis=0)
-    up1, down1 = together(around(up, 4), around(down, -4))
-    up2, down2, grad_own, grad_other = together(around(up1, 4), around(down1, -4), grad_own, grad_other)
-    grad = in_order(grad_own, grad_other).reshape(ZH, Y, C, 8, 512).transpose(1, 2, 0, 3, 4)
-    grad = exchange(grad.reshape(Y * C, ZH, 8, 512), ("y", "c"))
-    up3, down3 = together(around(up2, 4), around(down2, -4))
-    half_low, half_high, grad = together(around(up3[:192], 4), around(down3[128:], -4), grad)
-    p0 = place(
-        (ring // 4).astype(jnp.int32).reshape(1),
-        squares_out,
-        (down1, down2, down3, up3, up2, up1),
-        (half_low, half_high),
-    )
-    rows_other = jnp.concatenate([half_low[128:], half_high[:64]], axis=1)
-    rows_in = lax.all_gather(in_order(rows_own, rows_other), "x", axis=0, tiled=False)
+    sent = jnp.concatenate([theirs(squares_in), theirs(grad).reshape(64, 512)], axis=1)
+    p0 = lax.all_gather(squares[0], ("zh", "z8", "z4"), axis=0, tiled=False)
+    p0, got = together(p0, swap(sent, "zh"))
+    rows_in = in_order(mine(squares_in), got[:, :tokens])
+    rows_in = lax.all_gather(rows_in, "x", axis=0, tiled=False)
     rows_in = rows_in.reshape(X, ZH, Y * C, 8, tokens).transpose(1, 2, 0, 3, 4).reshape(ZH, 256, tokens)
+    grad = in_order(mine(grad), got[:, tokens:].reshape(Y * C, 8, 512))
+    grad = grad.reshape(ZH, Y, C, 8, 512).transpose(3, 1, 0, 2, 4).reshape(8, 8192)
     p3, p1, rows_in = together(around(p0, 1), around(p0, -1), rows_in)
-    p2a, p2b = around(p1[:4], -1), around(p3[4:], 1)
-    grad = grad.reshape(Y, C, ZH, 8, 512).transpose(3, 0, 2, 1, 4).reshape(8, 8192)
-    p2a, p2b, grad = together(p2a, p2b, grad)
+    p2a, p2b, grad = together(around(p1[:4], -1), around(p3[4:], 1), grad)
 
     partial = exchange(scale_part(rows_in, p0, p1, p2a, p2b, p3), ("y", "c", "x"))
     rows = jnp.sum(partial.reshape(Y * C, X, 8, 2048).astype(f32), axis=0).reshape(X, 8, 4, 4, 128)

time: 282 us -> 274 us (0.972)
  blocking collectives: 20.8 us -> 97.8 us
  starting transfers between devices: 163 us -> 107 us
  waiting for transfers between devices: 79.9 us -> 51.8 us
    all_gather x1 -> x3, blocking collectives: 9.96 us -> 97.8 us  [the longest x1 46 us: per_device(): p0 = lax.all_gather(squares[0], ('zh', 'z8', 'z4'), axis=0, tiled=False)]
    ppermute x12 -> x4, starting transfers between devices: 56.4 us -> 13.7 us  [around(): return lax.ppermute(value, RING, [(i, (i + hops) % 32) for i in range(32)])]
    ppermute x5 -> x3, waiting for transfers between devices: 40.9 us -> 19.4 us  [swap(): return lax.ppermute(value, axis, [(0, 1), (1, 0)])]
    ppermute x5 -> x3, starting transfers between devices: 71.8 us -> 54.1 us  [swap(): return lax.ppermute(value, axis, [(0, 1), (1, 0)])]
    ppermute x12 -> x4, waiting for transfers between devices: 21.4 us -> 4.21 us  [around(): return lax.ppermute(value, RING, [(i, (i + hops) % 32) for i in range(32)])]
    all_to_all x1 -> x0, blocking collectives: 10.8 us -> none  [exchange(): return lax.all_to_all(value, axis, split_axis=0, concat_axis=0, tiled=True)]
    all_to_all x4 -> x5, waiting for transfers between devices: 17.6 us -> 28.2 us  [exchange(): return lax.all_to_all(value, axis, split_axis=0, concat_axis=0, tiled=True)]
    all_to_all x4 -> x5, starting transfers between devices: 34.3 us -> 39.6 us  [exchange(): return lax.all_to_all(value, axis, split_axis=0, concat_axis=0, tiled=True)]
  transfers between devices with their start and end apart: 21 -> 12, of which waited for: 14 -> 7; matrix products, arithmetic and copies ran while one was open for 3% -> 1% of each run, Pallas kernels for 0% -> 0%
where the time goes in v6:
time: 274 us; the launch traced here: 273 us
  starting transfers between devices  107 us (39%)
  blocking collectives  97.8 us (36%)
  waiting for transfers between devices  51.8 us (19%)
  local copies, waits for them, and re-layouts  8.23 us (3%)
  Pallas kernels  4.87 us (2%)
    ppermute x3, starting transfers between devices, swap(): return lax.ppermute(value, axis, [(0, 1), (1, 0)])  54.1 us
    all_gather x1, blocking collectives, per_device(): p0 = lax.all_gather(squares[0], ('zh', 'z8', 'z4'), axis=0, tiled=False)  46 us
    all_gather x1, blocking collectives, per_device(): lax.all_gather(jnp.stack([out_grads, activations]), ('z8', 'z4'), axis=0,...  42.4 us
    all_to_all x5, starting transfers between devices, exchange(): return lax.all_to_all(value, axis, split_axis=0, concat_axis=0, tiled=True)  39.6 us
    all_to_all x5, waiting for transfers between devices, exchange(): return lax.all_to_all(value, axis, split_axis=0, concat_axis=0, tiled=True)  28.2 us
    ppermute x3, waiting for transfers between devices, swap(): return lax.ppermute(value, axis, [(0, 1), (1, 0)])  19.4 us
    ppermute x4, starting transfers between devices, around(): return lax.ppermute(value, RING, [(i, (i + hops) % 32) for i in range(32)])  13.7 us
    all_gather x1, blocking collectives, per_device(): rows_in = lax.all_gather(rows_in, 'x', axis=0, tiled=False)  9.37 us
  transfers between devices with their start and end apart: 12, of which 7 were waited for; matrix products, arithmetic and copies ran while one was open for 1% of the time, Pallas kernels for 0%

profile of v6, /device:TPU:1, one launch (start us, length us, event | category | flops | bytes accessed | tf_op | source)
XLA Modules:
  0.0 272.7 jit_solution(7221252865631718454)
XLA Ops:
  0.0 3.2 %copy.46 = bf16[16,4,128,128]{3,2,0,1:T(8,128)(2,1)} copy(bf16[16,4,128,128]{3,2,1,0:T(8,128)(2,1)} %bitcast.59) | data formatting | bytes 4194304 | tf_op jit(solution)/shard_map/reshape | solution.py:108
  3.2 5.0 %all-to-all-start = ((bf16[4,16,128,128]{3,2,1,0:T(8,128)(2,1)}), bf16[4,16,128,128]{3,2,1,0:T(8,128)(2,1)S(1)}, u32[]{:S(2)}, u32[]{:S(2)}) async-start(bf16[4,16,128,128]{3,2,1,0:T(8,128)(2,1)} %bitcast.54), calls=%async_computation | async-start | bytes 4194304 | tf_op jit(solution)/shard_map/all_to_all | solution.py:90
  8.2 42.4 %all-gather = bf16[8,256,128]{2,1,0:T(8,128)(2,1)S(1)} all-gather(bf16[2,256,128]{2,1,0:T(8,128)(2,1)S(1)} %pad_maximum_fusion.1), channel_id=2, replica_groups=mesh['y'=4,'zh'=2,'c'=2,'z8'=2,'z4'=2,'z2'=2,'z1'=2,'x'=4] {'z8','z4'}, dimensions={0}, use_global_device_ids=true | all-gather | bytes 655360 | tf_op jit(solution)/shard_map/all_gather | solution.py:111
  50.6 3.3 %copy.45 = bf16[16,4,128,128]{3,2,0,1:T(8,128)(2,1)} copy(bf16[16,4,128,128]{3,2,1,0:T(8,128)(2,1)} %bitcast.60) | data formatting | bytes 4194304 | tf_op jit(solution)/shard_map/reshape | solution.py:113
  53.9 4.5 %all-to-all-start.1 = ((bf16[4,16,128,128]{3,2,1,0:T(8,128)(2,1)}), bf16[4,16,128,128]{3,2,1,0:T(8,128)(2,1)}, u32[]{:S(2)}, u32[]{:S(2)}) async-start(bf16[4,16,128,128]{3,2,1,0:T(8,128)(2,1)} %bitcast.53), calls=%async_computation.1 | async-start | bytes 4194304 | tf_op jit(solution)/shard_map/all_to_all | solution.py:90
  58.4 17.0 %collective-permute-start = (bf16[4,2,256,128]{3,2,1,0:T(8,128)(2,1)S(1)}, bf16[4,2,256,128]{3,2,1,0:T(8,128)(2,1)S(1)}, u32[]{:S(2)}, u32[]{:S(2)}) collective-permute-start(bf16[4,2,256,128]{3,2,1,0:T(8,128)(2,1)S(1)} %bitcast.61), channel_id=1, source_target_pairs={{0,8},{8,0},{1,9},{9,1},{2,10},{10,2},{3,11},{11,3},{4,12},{12,4},... | collective-permute-start | bytes 1572872 | tf_op jit(solution)/shard_map/ppermute | solution.py:22
  75.4 11.1 %collective-permute-done = bf16[4,2,256,128]{3,2,1,0:T(8,128)(2,1)S(1)} collective-permute-done((bf16[4,2,256,128]{3,2,1,0:T(8,128)(2,1)S(1)}, bf16[4,2,256,128]{3,2,1,0:T(8,128)(2,1)S(1)}, u32[]{:S(2)}, u32[]{:S(2)}) %collective-permute-start) | collective-permute-done | bytes 524320 | tf_op jit(solution)/shard_map/ppermute | solution.py:22
  86.6 1.1 pad_maximum_fusion.near_ref
  87.7 14.1 %collective-permute-start.1 = (bf16[8,2,256,128]{3,2,1,0:T(8,128)(2,1)S(1)}, bf16[8,2,256,128]{3,2,1,0:T(8,128)(2,1)}, u32[]{:S(2)}, u32[]{:S(2)}) collective-permute-start(bf16[8,2,256,128]{3,2,1,0:T(8,128)(2,1)S(1)} %pad_maximum_fusion.near_ref), channel_id=1, source_target_pairs={{0,4},{4,0},{1,5},{5,1},{2,6},{6,2},{3,7},{7,3},{8,12},{12,8},{9,1... | collective-permute-start | bytes 3145736 | tf_op jit(solution)/shard_map/ppermute | solution.py:22
  101.8 0.7 copy.36
  102.5 7.1 %all-to-all-start.2 = ((bf16[8,2,8,512]{3,2,1,0:T(8,128)(2,1)}), bf16[8,2,8,512]{3,2,1,0:T(8,128)(2,1)S(1)}, u32[]{:S(2)}, u32[]{:S(2)}) async-start(bf16[8,2,8,512]{3,2,1,0:T(8,128)(2,1)} %bitcast.10), calls=%async_computation.2 | async-start | bytes 262144 | tf_op jit(solution)/shard_map/all_to_all | solution.py:90
  109.6 5.3 %all-to-all-done.2 = bf16[8,2,8,512]{3,2,1,0:T(8,128)(2,1)S(1)} async-done(((bf16[8,2,8,512]{3,2,1,0:T(8,128)(2,1)}), bf16[8,2,8,512]{3,2,1,0:T(8,128)(2,1)S(1)}, u32[]{:S(2)}, u32[]{:S(2)}) %all-to-all-start.2) | async-done | bytes 131104 | tf_op jit(solution)/shard_map/all_to_all | solution.py:90
  114.9 8.2 %collective-permute-done.1.far_ref = bf16[8,2,256,128]{3,2,1,0:T(8,128)(2,1)} collective-permute-done((bf16[8,2,256,128]{3,2,1,0:T(8,128)(2,1)S(1)}, bf16[8,2,256,128]{3,2,1,0:T(8,128)(2,1)}, u32[]{:S(2)}, u32[]{:S(2)}) %collective-permute-start.1) | collective-permute-done | bytes 1048608 | tf_op jit(solution)/shard_map/ppermute | solution.py:22
  123.1 3.2 %project.1 = bf16[4,2,256,128]{3,2,1,0:T(8,128)(2,1)S(1)} custom-call(s32[1]{0:T(128)} %bitcast.z_ref, bf16[8,2,256,128]{3,2,1,0:T(8,128)(2,1)S(1)} %pad_maximum_fusion.near_ref, bf16[8,2,256,128]{3,2,1,0:T(8,128)(2,1)} %collective-permute-done.1.far_ref, bf16[4,16,128,128]{3,2,1,0:T(8,128)(2,1)S(1)} %all-to-all-done.basis_out_ref, ...), custom_call_target="tpu_custom_call" | custom-call | flops 1073741824 | bytes 6800000 | tf_op jit(solution)/shard_map/project/pallas_call | solution.py:50
  126.3 0.8 copy-done
  127.1 3.6 %all-to-all-start.3 = ((bf16[4,2,256,128]{3,2,1,0:T(8,128)(2,1)}), bf16[4,2,256,128]{3,2,1,0:T(8,128)(2,1)S(1)}, u32[]{:S(2)}, u32[]{:S(2)}) async-start(bf16[4,2,256,128]{3,2,1,0:T(8,128)(2,1)} %copy-done), calls=%async_computation.3 | async-start | bytes 1048576 | tf_op jit(solution)/shard_map/all_to_all | solution.py:90
  130.7 6.9 %all-to-all-done.3 = bf16[4,2,256,128]{3,2,1,0:T(8,128)(2,1)S(1)} async-done(((bf16[4,2,256,128]{3,2,1,0:T(8,128)(2,1)}), bf16[4,2,256,128]{3,2,1,0:T(8,128)(2,1)S(1)}, u32[]{:S(2)}, u32[]{:S(2)}) %all-to-all-start.3) | async-done | bytes 524320 | tf_op jit(solution)/shard_map/all_to_all | solution.py:90
  137.7 0.1 copy.37
  137.9 23.0 %collective-permute-start.2 = (bf16[64,768]{1,0:T(8,128)(2,1)S(1)}, bf16[64,768]{1,0:T(8,128)(2,1)S(1)}, u32[]{:S(2)}, u32[]{:S(2)}) collective-permute-start(bf16[64,768]{1,0:T(8,128)(2,1)S(1)} %pad_maximum_fusion.2), channel_id=1, source_target_pairs={{0,128},{128,0},{1,129},{129,1},{2,130},{130,2},{3,131},{131,3},{4... | collective-permute-start | bytes 294920 | tf_op jit(solution)/shard_map/ppermute | solution.py:22
  160.9 46.0 %all_gather.17.p0 = bf16[8,256,128]{2,1,0:T(8,128)(2,1)S(1)} all-gather(bf16[1,256,128]{2,1,0:T(8,128)(2,1)S(1)} %get-tuple-element.48), channel_id=1, replica_groups=mesh['y'=4,'zh'=2,'c'=2,'z8'=2,'z4'=2,'z2'=2,'z1'=2,'x'=4] {'zh','z8','z4'}, dimensions={0}, use_global_device_ids=true | all-gather | bytes 589824 | tf_op jit(solution)/shard_map/all_gather | solution.py:127
  206.9 3.1 %collective-permute-start.4 = (bf16[8,256,128]{2,1,0:T(8,128)(2,1)S(1)}, bf16[8,256,128]{2,1,0:T(8,128)(2,1)S(1)}, u32[]{:S(2)}, u32[]{:S(2)}) collective-permute-start(bf16[8,256,128]{2,1,0:T(8,128)(2,1)S(1)} %all_gather.17.p0), channel_id=1, source_target_pairs={{0,188},{4,0},{8,4},{12,8},{16,12},{20,16},{24,20},{28,24},{32,28}... | collective-permute-start | bytes 1572872 | tf_op jit(solution)/shard_map/ppermute | solution.py:26
  210.1 4.1 %collective-permute-start.3 = (bf16[8,256,128]{2,1,0:T(8,128)(2,1)S(1)}, bf16[8,256,128]{2,1,0:T(8,128)(2,1)S(1)}, u32[]{:S(2)}, u32[]{:S(2)}) collective-permute-start(bf16[8,256,128]{2,1,0:T(8,128)(2,1)S(1)} %all_gather.17.p0), channel_id=1, source_target_pairs={{0,4},{4,8},{8,12},{12,16},{16,20},{20,24},{24,28},{28,32},{32,36}... | collective-permute-start | bytes 1572872 | tf_op jit(solution)/shard_map/ppermute | solution.py:26
  214.2 9.4 %all-gather.1 = bf16[8,64,256]{2,1,0:T(8,128)(2,1)S(1)} all-gather(bf16[2,64,256]{2,1,0:T(8,128)(2,1)S(1)} %pad_maximum_fusion.3), channel_id=3, replica_groups=mesh['y'=4,'zh'=2,'c'=2,'z8'=2,'z4'=2,'z2'=2,'z1'=2,'x'=4] {'x'}, dimensions={0}, use_global_device_ids=true | all-gather | bytes 327680 | tf_op jit(solution)/shard_map/all_gather | solution.py:130
  223.6 3.4 %collective-permute-start.6 = (bf16[4,256,128]{2,1,0:T(8,128)(2,1)S(1)}, bf16[4,256,128]{2,1,0:T(8,128)(2,1)S(1)}, u32[]{:S(2)}, u32[]{:S(2)}) collective-permute-start(bf16[4,256,128]{2,1,0:T(8,128)(2,1)S(1)} %slice.60), channel_id=1, source_target_pairs={{0,4},{4,8},{8,12},{12,16},{16,20},{20,24},{24,28},{28,32},{32,36}... | collective-permute-start | bytes 786440 | tf_op jit(solution)/shard_map/ppermute | solution.py:26
  227.0 3.1 %collective-permute-start.5 = (bf16[4,256,128]{2,1,0:T(8,128)(2,1)S(1)}, bf16[4,256,128]{2,1,0:T(8,128)(2,1)S(1)}, u32[]{:S(2)}, u32[]{:S(2)}) collective-permute-start(bf16[4,256,128]{2,1,0:T(8,128)(2,1)S(1)} %slice.59), channel_id=1, source_target_pairs={{0,188},{4,0},{8,4},{12,8},{16,12},{20,16},{24,20},{28,24},{32,28}... | collective-permute-start | bytes 786440 | tf_op jit(solution)/shard_map/ppermute | solution.py:26
  230.2 1.8 collective-permute-done.6.p2b
  232.1 2.4 collective-permute-done.5.p2a
  234.4 1.7 scale.1
  236.1 19.5 %all-to-all-start.4 = ((bf16[32,8,2048]{2,1,0:T(8,128)(2,1)}), bf16[32,8,2048]{2,1,0:T(8,128)(2,1)S(1)}, u32[]{:S(2)}, u32[]{:S(2)}) async-start(bf16[32,8,2048]{2,1,0:T(8,128)(2,1)} %scale.1), calls=%async_computation.4 | async-start | bytes 2097152 | tf_op jit(solution)/shard_map/all_to_all | solution.py:90
  255.7 16.0 %all-to-all-done.4 = bf16[32,8,2048]{2,1,0:T(8,128)(2,1)S(1)} async-done(((bf16[32,8,2048]{2,1,0:T(8,128)(2,1)}), bf16[32,8,2048]{2,1,0:T(8,128)(2,1)S(1)}, u32[]{:S(2)}, u32[]{:S(2)}) %all-to-all-start.4) | async-done | bytes 1048608 | tf_op jit(solution)/shard_map/all_to_all | solution.py:90
  271.6 0.1 convert_reduce_fusion
  272.0 0.7 divide_convert_fusion
  (35 shorter events, 0.5 us)
Async XLA Ops:
  3.2 5.0 %copy-start.3 = (bf16[256,128]{1,0:T(8,128)(2,1)S(1)}, bf16[256,128]{1,0:T(8,128)(2,1)}, u32[]{:S(2)}) copy-start(bf16[256,128]{1,0:T(8,128)(2,1)} %param.5) | copy-start | bytes 196612
  3.2 5.0 %copy-start.4 = (bf16[256,128]{1,0:T(8,128)(2,1)S(1)}, bf16[256,128]{1,0:T(8,128)(2,1)}, u32[]{:S(2)}) copy-start(bf16[256,128]{1,0:T(8,128)(2,1)} %param.6) | copy-start | bytes 196612
  3.2 47.4 %all-to-all-start = ((bf16[4,16,128,128]{3,2,1,0:T(8,128)(2,1)}), bf16[4,16,128,128]{3,2,1,0:T(8,128)(2,1)S(1)}, u32[]{:S(2)}, u32[]{:S(2)}) async-start(bf16[4,16,128,128]{3,2,1,0:T(8,128)(2,1)} %bitcast.54), calls=%async_computation | async-start | bytes 4194304 | tf_op jit(solution)/shard_map/all_to_all | solution.py:90
  50.6 7.8 %copy-start.1 = (bf16[8,256,128]{2,1,0:T(8,128)(2,1)}, bf16[8,256,128]{2,1,0:T(8,128)(2,1)S(1)}, u32[]{:S(2)}) copy-start(bf16[8,256,128]{2,1,0:T(8,128)(2,1)S(1)} %all-gather) | copy-start | bytes 1572868
  53.9 33.8 %all-to-all-start.1 = ((bf16[4,16,128,128]{3,2,1,0:T(8,128)(2,1)}), bf16[4,16,128,128]{3,2,1,0:T(8,128)(2,1)}, u32[]{:S(2)}, u32[]{:S(2)}) async-start(bf16[4,16,128,128]{3,2,1,0:T(8,128)(2,1)} %bitcast.53), calls=%async_computation.1 | async-start | bytes 4194304 | tf_op jit(solution)/shard_map/all_to_all | solution.py:90
  58.4 43.4 %copy-start.2 = (bf16[128,512]{1,0:T(8,128)(2,1)S(1)}, bf16[128,512]{1,0:T(8,128)(2,1)}, u32[]{:S(2)}) copy-start(bf16[128,512]{1,0:T(8,128)(2,1)} %param.9) | copy-start | bytes 393220
  58.4 28.2 %collective-permute-start = (bf16[4,2,256,128]{3,2,1,0:T(8,128)(2,1)S(1)}, bf16[4,2,256,128]{3,2,1,0:T(8,128)(2,1)S(1)}, u32[]{:S(2)}, u32[]{:S(2)}) collective-permute-start(bf16[4,2,256,128]{3,2,1,0:T(8,128)(2,1)S(1)} %bitcast.61), channel_id=1, source_target_pairs={{0,8},{8,0},{1,9},{9,1},{2,10},{10,2},{3,11},{11,3},{4,12},{12,4},... | collective-permute-start | bytes 1572872 | tf_op jit(solution)/shard_map/ppermute | solution.py:22
  87.7 35.4 %collective-permute-start.1 = (bf16[8,2,256,128]{3,2,1,0:T(8,128)(2,1)S(1)}, bf16[8,2,256,128]{3,2,1,0:T(8,128)(2,1)}, u32[]{:S(2)}, u32[]{:S(2)}) collective-permute-start(bf16[8,2,256,128]{3,2,1,0:T(8,128)(2,1)S(1)} %pad_maximum_fusion.near_ref), channel_id=1, source_target_pairs={{0,4},{4,0},{1,5},{5,1},{2,6},{6,2},{3,7},{7,3},{8,12},{12,8},{9,1... | collective-permute-start | bytes 3145736 | tf_op jit(solution)/shard_map/ppermute | solution.py:22
  102.5 12.3 %all-to-all-start.2 = ((bf16[8,2,8,512]{3,2,1,0:T(8,128)(2,1)}), bf16[8,2,8,512]{3,2,1,0:T(8,128)(2,1)S(1)}, u32[]{:S(2)}, u32[]{:S(2)}) async-start(bf16[8,2,8,512]{3,2,1,0:T(8,128)(2,1)} %bitcast.10), calls=%async_computation.2 | async-start | bytes 262144 | tf_op jit(solution)/shard_map/all_to_all | solution.py:90
  126.3 0.8 copy-start
  127.1 10.6 %all-to-all-start.3 = ((bf16[4,2,256,128]{3,2,1,0:T(8,128)(2,1)}), bf16[4,2,256,128]{3,2,1,0:T(8,128)(2,1)S(1)}, u32[]{:S(2)}, u32[]{:S(2)}) async-start(bf16[4,2,256,128]{3,2,1,0:T(8,128)(2,1)} %copy-done), calls=%async_computation.3 | async-start | bytes 1048576 | tf_op jit(solution)/shard_map/all_to_all | solution.py:90
  137.9 69.0 %collective-permute-start.2 = (bf16[64,768]{1,0:T(8,128)(2,1)S(1)}, bf16[64,768]{1,0:T(8,128)(2,1)S(1)}, u32[]{:S(2)}, u32[]{:S(2)}) collective-permute-start(bf16[64,768]{1,0:T(8,128)(2,1)S(1)} %pad_maximum_fusion.2), channel_id=1, source_target_pairs={{0,128},{128,0},{1,129},{129,1},{2,130},{130,2},{3,131},{131,3},{4... | collective-permute-start | bytes 294920 | tf_op jit(solution)/shard_map/ppermute | solution.py:22
  206.9 16.7 %collective-permute-start.4 = (bf16[8,256,128]{2,1,0:T(8,128)(2,1)S(1)}, bf16[8,256,128]{2,1,0:T(8,128)(2,1)S(1)}, u32[]{:S(2)}, u32[]{:S(2)}) collective-permute-start(bf16[8,256,128]{2,1,0:T(8,128)(2,1)S(1)} %all_gather.17.p0), channel_id=1, source_target_pairs={{0,188},{4,0},{8,4},{12,8},{16,12},{20,16},{24,20},{28,24},{32,28}... | collective-permute-start | bytes 1572872 | tf_op jit(solution)/shard_map/ppermute | solution.py:26
  210.1 13.5 %collective-permute-start.3 = (bf16[8,256,128]{2,1,0:T(8,128)(2,1)S(1)}, bf16[8,256,128]{2,1,0:T(8,128)(2,1)S(1)}, u32[]{:S(2)}, u32[]{:S(2)}) collective-permute-start(bf16[8,256,128]{2,1,0:T(8,128)(2,1)S(1)} %all_gather.17.p0), channel_id=1, source_target_pairs={{0,4},{4,8},{8,12},{12,16},{16,20},{20,24},{24,28},{28,32},{32,36}... | collective-permute-start | bytes 1572872 | tf_op jit(solution)/shard_map/ppermute | solution.py:26
  223.6 8.4 %collective-permute-start.6 = (bf16[4,256,128]{2,1,0:T(8,128)(2,1)S(1)}, bf16[4,256,128]{2,1,0:T(8,128)(2,1)S(1)}, u32[]{:S(2)}, u32[]{:S(2)}) collective-permute-start(bf16[4,256,128]{2,1,0:T(8,128)(2,1)S(1)} %slice.60), channel_id=1, source_target_pairs={{0,4},{4,8},{8,12},{12,16},{16,20},{20,24},{24,28},{28,32},{32,36}... | collective-permute-start | bytes 786440 | tf_op jit(solution)/shard_map/ppermute | solution.py:26
  227.0 7.4 %collective-permute-start.5 = (bf16[4,256,128]{2,1,0:T(8,128)(2,1)S(1)}, bf16[4,256,128]{2,1,0:T(8,128)(2,1)S(1)}, u32[]{:S(2)}, u32[]{:S(2)}) collective-permute-start(bf16[4,256,128]{2,1,0:T(8,128)(2,1)S(1)} %slice.59), channel_id=1, source_target_pairs={{0,188},{4,0},{8,4},{12,8},{16,12},{20,16},{24,20},{28,24},{32,28}... | collective-permute-start | bytes 786440 | tf_op jit(solution)/shard_map/ppermute | solution.py:26
  236.1 35.5 %all-to-all-start.4 = ((bf16[32,8,2048]{2,1,0:T(8,128)(2,1)}), bf16[32,8,2048]{2,1,0:T(8,128)(2,1)S(1)}, u32[]{:S(2)}, u32[]{:S(2)}) async-start(bf16[32,8,2048]{2,1,0:T(8,128)(2,1)} %scale.1), calls=%async_computation.4 | async-start | bytes 2097152 | tf_op jit(solution)/shard_map/all_to_all | solution.py:90

commit v7 on v4

--- a/solution.py
+++ b/solution.py
@@ -14,9 +14,6 @@
 PARAMS = pltpu.CompilerParams(vmem_limit_bytes=16 * 2**20)
 SCALAR = pl.BlockSpec(memory_space=pltpu.SMEM)
 WHOLE = pl.BlockSpec(memory_space=pltpu.VMEM)
-ARRIVAL = [0, 8, 4, 12, 2, 10, 6, 14, 1, 9, 5, 13, 3, 11, 7, 15]
-
-
 def together(*values):
     return lax.optimization_barrier(values)
 
@@ -29,21 +26,17 @@
     return lax.ppermute(value, RING, [(i, (i + hops) % 32) for i in range(32)])
 
 
-def double_z(have, axis):
-    return jnp.concatenate([have, swap(have, axis)], axis=0)
-
-
 def project_kernel(z_ref, near_ref, far_ref, basis_out_ref, basis_in_ref, out_ref):
-    z = z_ref[0]
+    residue = lax.rem(z_ref[0], 4)
     for m, basis_ref in enumerate((basis_out_ref, basis_in_ref)):
         for pair in range(2):
             total = jnp.zeros((256, 256), f32)
             for step in range(8):
                 source = near_ref if step < 4 else far_ref
-                at = 2 * step if step < 4 else 2 * step - 8
+                at = 2 * (step % 4)
                 left = jnp.concatenate([source[at, m], source[at + 1, m]], axis=1)
-                z0 = z ^ ARRIVAL[2 * step]
-                z1 = z ^ ARRIVAL[2 * step + 1]
+                z0 = 4 * (at % 4) + (residue ^ (2 * (at // 4) + step // 4))
+                z1 = z0 + 4
                 columns = [
                     jnp.concatenate([basis_ref[2 * pair + i, z0], basis_ref[2 * pair + i, z1]], axis=0) for i in range(2)
                 ]
@@ -137,18 +130,21 @@
         return jnp.stack([jnp.where(high, other, own), jnp.where(high, own, other)])
 
     basis_out = basis_out.reshape(16, X, 128, 128).transpose(1, 0, 2, 3)
+
     basis_in = basis_in.reshape(16, X, 128, 128).transpose(1, 0, 2, 3)
 
-    grad = grad_eigen.reshape(Y, ZH, C * 8, 512).transpose(1, 0, 2, 3)
-    grad_own = mine(grad)
-    have, grad_other, basis_out = together(
-        double_z(jnp.stack([out_grads, activations])[None], "z8"), swap(theirs(grad), "zh"), basis_out
-    )
+    grad = grad_eigen.reshape(Y, ZH, C, 8, 512).transpose(0, 2, 1, 3, 4).reshape(Y * C, ZH, 8, 512)
+    grad = exchange(grad, ("y", "c"))
+    have, basis_out = together(jnp.stack([out_grads, activations]), basis_out)
+    have = lax.all_gather(have, ("z8", "z4"), axis=0, tiled=False)
+    have, grad, basis_out = together(have, grad, basis_out)
     b_out = exchange(basis_out, "x")
-    have, basis_in = together(double_z(have, "z4"), basis_in)
-    have, b_out = together(double_z(have, "z2"), b_out)
+    have = jnp.concatenate([have, swap(have, "z2")], axis=0)
+    have, b_out, basis_in = together(have, b_out, basis_in)
     b_in = exchange(basis_in, "x")
-    far, have, b_in = together(swap(have, "z1"), have, b_in)
+    grad = grad.transpose(1, 0, 2, 3)
+    grad_own, grad_other = mine(grad), swap(theirs(grad), "zh")
+    far, have, b_in, grad_own, grad_other = together(swap(have, "z1"), have, b_in, grad_own, grad_other)
 
     part = project(z, have, far, b_out, b_in)
     projected = jnp.sum(exchange(part, "x").astype(f32), axis=0)
@@ -160,11 +156,11 @@
     up = jnp.concatenate([squares_out[:128], rows_sent[:, :128], squares_out[128:]], axis=0)
     down = jnp.concatenate([squares_out[:128], rows_sent[:, 128:], squares_out[128:]], axis=0)
     up1, down1 = together(around(up, 4), around(down, -4))
-    up2, down2, grad_own, grad_other = together(around(up1, 4), around(down1, -4), grad_own, grad_other)
-    grad = in_order(grad_own, grad_other).reshape(ZH, Y, C, 8, 512).transpose(1, 2, 0, 3, 4)
-    grad = exchange(grad.reshape(Y * C, ZH, 8, 512), ("y", "c"))
+    grad = in_order(grad_own, grad_other)
+    grad = grad.reshape(ZH, Y, C, 8, 512).transpose(3, 1, 0, 2, 4).reshape(8, 8192)
+    up2, down2, grad = together(around(up1, 4), around(down1, -4), grad)
     up3, down3 = together(around(up2, 4), around(down2, -4))
-    half_low, half_high, grad = together(around(up3[:192], 4), around(down3[128:], -4), grad)
+    half_low, half_high = together(around(up3[:192], 4), around(down3[128:], -4))
     p0 = place(
         (ring // 4).astype(jnp.int32).reshape(1),
         squares_out,
@@ -175,9 +171,7 @@
     rows_in = lax.all_gather(in_order(rows_own, rows_other), "x", axis=0, tiled=False)
     rows_in = rows_in.reshape(X, ZH, Y * C, 8, tokens).transpose(1, 2, 0, 3, 4).reshape(ZH, 256, tokens)
     p3, p1, rows_in = together(around(p0, 1), around(p0, -1), rows_in)
-    p2a, p2b = around(p1[:4], -1), around(p3[4:], 1)
-    grad = grad.reshape(Y, C, ZH, 8, 512).transpose(3, 0, 2, 1, 4).reshape(8, 8192)
-    p2a, p2b, grad = together(p2a, p2b, grad)
+    p2a, p2b, grad = together(around(p1[:4], -1), around(p3[4:], 1), grad)
 
     partial = exchange(scale_part(rows_in, p0, p1, p2a, p2b, p3), ("y", "c", "x"))
     rows = jnp.sum(partial.reshape(Y * C, X, 8, 2048).astype(f32), axis=0).reshape(X, 8, 4, 4, 128)

time: 282 us -> 295 us (1.046)
  blocking collectives: 20.8 us -> 63.1 us
  starting transfers between devices: 163 us -> 137 us
  other arithmetic: 4.92 us -> 1.24 us
    all_gather x0 -> x1, blocking collectives: none -> 42.9 us  [per_device(): have = lax.all_gather(have, ('z8', 'z4'), axis=0, tiled=False)]
    ppermute x5 -> x3, starting transfers between devices: 71.8 us -> 30.5 us  [swap(): return lax.ppermute(value, axis, [(0, 1), (1, 0)])]
    all_to_all x4, starting transfers between devices: 34.3 us -> 48.5 us  [exchange(): return lax.all_to_all(value, axis, split_axis=0, concat_axis=0, tiled=True)]
    ppermute x5 -> x3, waiting for transfers between devices: 40.9 us -> 27.5 us  [swap(): return lax.ppermute(value, axis, [(0, 1), (1, 0)])]
    all_to_all x4, waiting for transfers between devices: 17.6 us -> 25.3 us  [exchange(): return lax.all_to_all(value, axis, split_axis=0, concat_axis=0, tiled=True)]
    ppermute x12, waiting for transfers between devices: 21.4 us -> 26.1 us  [around(): return lax.ppermute(value, RING, [(i, (i + hops) % 32) for i in range(32)])]
  transfers between devices with their start and end apart: 21 -> 19, of which waited for: 14 -> 14; matrix products, arithmetic and copies ran while one was open for 3% -> 2% of each run, Pallas kernels for 0% -> 0%
where the time goes in v7:
time: 295 us; the launch traced here: 294 us
  starting transfers between devices  137 us (46%)
  waiting for transfers between devices  78.9 us (27%)
  blocking collectives  63.1 us (21%)
  local copies, waits for them, and re-layouts  8.27 us (3%)
  Pallas kernels  4.91 us (2%)
    ppermute x12, starting transfers between devices, around(): return lax.ppermute(value, RING, [(i, (i + hops) % 32) for i in range(32)])  57.8 us
    all_to_all x4, starting transfers between devices, exchange(): return lax.all_to_all(value, axis, split_axis=0, concat_axis=0, tiled=True)  48.5 us
    all_gather x1, blocking collectives, per_device(): have = lax.all_gather(have, ('z8', 'z4'), axis=0, tiled=False)  42.9 us
    ppermute x3, starting transfers between devices, swap(): return lax.ppermute(value, axis, [(0, 1), (1, 0)])  30.5 us
    ppermute x3, waiting for transfers between devices, swap(): return lax.ppermute(value, axis, [(0, 1), (1, 0)])  27.5 us
    ppermute x12, waiting for transfers between devices, around(): return lax.ppermute(value, RING, [(i, (i + hops) % 32) for i in range(32)])  26.1 us
    all_to_all x4, waiting for transfers between devices, exchange(): return lax.all_to_all(value, axis, split_axis=0, concat_axis=0, tiled=True)  25.3 us
    all_to_all x1, blocking collectives, exchange(): return lax.all_to_all(value, axis, split_axis=0, concat_axis=0, tiled=True)  10.8 us
  transfers between devices with their start and end apart: 19, of which 14 were waited for; matrix products, arithmetic and copies ran while one was open for 2% of the time, Pallas kernels for 0%

profile of v7, /device:TPU:1, one launch (start us, length us, event | category | flops | bytes accessed | tf_op | source)
XLA Modules:
  0.0 293.6 jit_solution(3619124043579450619)
XLA Ops:
  1.6 17.4 %all-to-all-start = ((bf16[8,2,8,512]{3,2,1,0:T(8,128)(2,1)}), bf16[8,2,8,512]{3,2,1,0:T(8,128)(2,1)S(1)}, u32[]{:S(2)}, u32[]{:S(2)}) async-start(bf16[8,2,8,512]{3,2,1,0:T(8,128)(2,1)} %bitcast.9), calls=%async_computation | async-start | bytes 262144 | tf_op jit(solution)/shard_map/all_to_all | solution.py:114
  19.0 3.2 %copy.43 = bf16[16,4,128,128]{3,2,0,1:T(8,128)(2,1)} copy(bf16[16,4,128,128]{3,2,1,0:T(8,128)(2,1)} %bitcast.75) | data formatting | bytes 4194304 | tf_op jit(solution)/shard_map/reshape | solution.py:132
  22.2 42.9 %all-gather = bf16[8,256,128]{2,1,0:T(8,128)(2,1)S(1)} all-gather(bf16[2,256,128]{2,1,0:T(8,128)(2,1)S(1)} %pad_maximum_fusion.1), channel_id=2, replica_groups=mesh['y'=4,'zh'=2,'c'=2,'z8'=2,'z4'=2,'z2'=2,'z1'=2,'x'=4] {'z8','z4'}, dimensions={0}, use_global_device_ids=true | all-gather | bytes 655360 | tf_op jit(solution)/shard_map/all_gather | solution.py:139
  65.1 3.6 %all-to-all-start.1 = ((bf16[4,16,128,128]{3,2,1,0:T(8,128)(2,1)}), bf16[4,16,128,128]{3,2,1,0:T(8,128)(2,1)S(1)}, u32[]{:S(2)}, u32[]{:S(2)}) async-start(bf16[4,16,128,128]{3,2,1,0:T(8,128)(2,1)} %bitcast.70), calls=%async_computation.1 | async-start | bytes 4194304 | tf_op jit(solution)/shard_map/all_to_all | solution.py:114
  68.7 5.4 %collective-permute-start = (bf16[4,2,256,128]{3,2,1,0:T(8,128)(2,1)S(1)}, bf16[4,2,256,128]{3,2,1,0:T(8,128)(2,1)S(1)}, u32[]{:S(2)}, u32[]{:S(2)}) collective-permute-start(bf16[4,2,256,128]{3,2,1,0:T(8,128)(2,1)S(1)} %bitcast.77), channel_id=1, source_target_pairs={{0,8},{8,0},{1,9},{9,1},{2,10},{10,2},{3,11},{11,3},{4,12},{12,4},... | collective-permute-start | bytes 1572872 | tf_op jit(solution)/shard_map/ppermute | solution.py:22
  74.2 3.3 %copy.42 = bf16[16,4,128,128]{3,2,0,1:T(8,128)(2,1)} copy(bf16[16,4,128,128]{3,2,1,0:T(8,128)(2,1)} %bitcast.76) | data formatting | bytes 4194304 | tf_op jit(solution)/shard_map/reshape | solution.py:134
  77.4 7.7 %collective-permute-done = bf16[4,2,256,128]{3,2,1,0:T(8,128)(2,1)S(1)} collective-permute-done((bf16[4,2,256,128]{3,2,1,0:T(8,128)(2,1)S(1)}, bf16[4,2,256,128]{3,2,1,0:T(8,128)(2,1)S(1)}, u32[]{:S(2)}, u32[]{:S(2)}) %collective-permute-start) | collective-permute-done | bytes 524320 | tf_op jit(solution)/shard_map/ppermute | solution.py:22
  85.2 9.3 %all-to-all-done.1.basis_out_ref = bf16[4,16,128,128]{3,2,1,0:T(8,128)(2,1)S(1)} async-done(((bf16[4,16,128,128]{3,2,1,0:T(8,128)(2,1)}), bf16[4,16,128,128]{3,2,1,0:T(8,128)(2,1)S(1)}, u32[]{:S(2)}, u32[]{:S(2)}) %all-to-all-start.1) | async-done | bytes 2097184 | tf_op jit(solution)/shard_map/all_to_all | solution.py:114
  94.5 4.5 %all-to-all-start.2 = ((bf16[4,16,128,128]{3,2,1,0:T(8,128)(2,1)}), bf16[4,16,128,128]{3,2,1,0:T(8,128)(2,1)}, u32[]{:S(2)}, u32[]{:S(2)}) async-start(bf16[4,16,128,128]{3,2,1,0:T(8,128)(2,1)} %bitcast.69), calls=%async_computation.2 | async-start | bytes 4194304 | tf_op jit(solution)/shard_map/all_to_all | solution.py:114
  99.0 7.0 %collective-permute-start.1 = (bf16[8,2,256,128]{3,2,1,0:T(8,128)(2,1)S(1)}, bf16[8,2,256,128]{3,2,1,0:T(8,128)(2,1)}, u32[]{:S(2)}, u32[]{:S(2)}) collective-permute-start(bf16[8,2,256,128]{3,2,1,0:T(8,128)(2,1)S(1)} %pad_maximum_fusion.near_ref), channel_id=1, source_target_pairs={{0,4},{4,0},{1,5},{5,1},{2,6},{6,2},{3,7},{7,3},{8,12},{12,8},{9,1... | collective-permute-start | bytes 3145736 | tf_op jit(solution)/shard_map/ppermute | solution.py:22
  106.0 18.1 %collective-permute-start.2 = (bf16[8,8,512]{2,1,0:T(8,128)(2,1)S(1)}, bf16[8,8,512]{2,1,0:T(8,128)(2,1)S(1)}, u32[]{:S(2)}, u32[]{:S(2)}) collective-permute-start(bf16[8,8,512]{2,1,0:T(8,128)(2,1)S(1)} %fusion.2), channel_id=1, source_target_pairs={{0,128},{128,0},{1,129},{129,1},{2,130},{130,2},{3,131},{131,3},{4... | collective-permute-start | bytes 196616 | tf_op jit(solution)/shard_map/ppermute | solution.py:22
  124.2 19.8 %collective-permute-done.2 = bf16[8,8,512]{2,1,0:T(8,128)(2,1)S(1)} collective-permute-done((bf16[8,8,512]{2,1,0:T(8,128)(2,1)S(1)}, bf16[8,8,512]{2,1,0:T(8,128)(2,1)S(1)}, u32[]{:S(2)}, u32[]{:S(2)}) %collective-permute-start.2) | collective-permute-done | bytes 65568 | tf_op jit(solution)/shard_map/ppermute | solution.py:22
  143.9 3.2 %project.1 = bf16[4,2,256,128]{3,2,1,0:T(8,128)(2,1)S(1)} custom-call(s32[1]{0:T(128)} %bitcast.1.z_ref, bf16[8,2,256,128]{3,2,1,0:T(8,128)(2,1)S(1)} %pad_maximum_fusion.near_ref, bf16[8,2,256,128]{3,2,1,0:T(8,128)(2,1)} %collective-permute-done.1.far_ref, bf16[4,16,128,128]{3,2,1,0:T(8,128)(2,1)S(1)} %all-to-all-done.1.basis_out_ref, ...), custom_call_target="tpu_custom_call" | custom-call | flops 1073741824 | bytes 6800000 | tf_op jit(solution)/shard_map/project/pallas_call | solution.py:50
  147.1 10.8 %all_to_all.25 = bf16[4,2,256,128]{3,2,1,0:T(8,128)(2,1)S(1)} all-to-all(bf16[4,2,256,128]{3,2,1,0:T(8,128)(2,1)S(1)} %project.1), channel_id=1, replica_groups=mesh['y'=4,'zh'=2,'c'=2,'z8'=2,'z4'=2,'z2'=2,'z1'=2,'x'=4] {'x'}, dimensions={0} | all-to-all | bytes 1048576 | tf_op jit(solution)/shard_map/all_to_all | solution.py:114
  158.2 9.7 %collective-permute-start.4 = (bf16[320,128]{1,0:T(8,128)(2,1)S(1)}, bf16[320,128]{1,0:T(8,128)(2,1)S(1)}, u32[]{:S(2)}, u32[]{:S(2)}) collective-permute-start(bf16[320,128]{1,0:T(8,128)(2,1)S(1)} %get-tuple-element.73), channel_id=1, source_target_pairs={{0,176},{4,180},{8,184},{12,188},{16,0},{20,4},{24,8},{28,12},{32,... | collective-permute-start | bytes 245768 | tf_op jit(solution)/shard_map/ppermute | solution.py:26
  167.9 1.9 collective-permute-start.3
  169.9 7.6 %collective-permute-done.3.refs_5_ = bf16[320,128]{1,0:T(8,128)(2,1)S(1)} collective-permute-done((bf16[320,128]{1,0:T(8,128)(2,1)S(1)}, bf16[320,128]{1,0:T(8,128)(2,1)S(1)}, u32[]{:S(2)}, u32[]{:S(2)}) %collective-permute-start.3) | collective-permute-done | bytes 81952 | tf_op jit(solution)/shard_map/ppermute | solution.py:26
  179.5 7.3 %collective-permute-start.5 = (bf16[320,128]{1,0:T(8,128)(2,1)S(1)}, bf16[320,128]{1,0:T(8,128)(2,1)S(1)}, u32[]{:S(2)}, u32[]{:S(2)}) collective-permute-start(bf16[320,128]{1,0:T(8,128)(2,1)S(1)} %collective-permute-done.3.refs_5_), channel_id=1, source_target_pairs={{0,16},{4,20},{8,24},{12,28},{16,32},{20,36},{24,40},{28,44},{32,4... | collective-permute-start | bytes 245768 | tf_op jit(solution)/shard_map/ppermute | solution.py:26
  188.7 10.5 %collective-permute-start.8 = (bf16[320,128]{1,0:T(8,128)(2,1)S(1)}, bf16[320,128]{1,0:T(8,128)(2,1)S(1)}, u32[]{:S(2)}, u32[]{:S(2)}) collective-permute-start(bf16[320,128]{1,0:T(8,128)(2,1)S(1)} %collective-permute-done.6.refs_1_), channel_id=1, source_target_pairs={{0,176},{4,180},{8,184},{12,188},{16,0},{20,4},{24,8},{28,12},{32,... | collective-permute-start | bytes 245768 | tf_op jit(solution)/shard_map/ppermute | solution.py:26
  199.2 1.9 collective-permute-start.7
  201.1 3.5 %collective-permute-done.8.refs_2_ = bf16[320,128]{1,0:T(8,128)(2,1)S(1)} collective-permute-done((bf16[320,128]{1,0:T(8,128)(2,1)S(1)}, bf16[320,128]{1,0:T(8,128)(2,1)S(1)}, u32[]{:S(2)}, u32[]{:S(2)}) %collective-permute-start.8) | collective-permute-done | bytes 81952 | tf_op jit(solution)/shard_map/ppermute | solution.py:26
  204.6 5.1 %collective-permute-done.7.refs_3_ = bf16[320,128]{1,0:T(8,128)(2,1)S(1)} collective-permute-done((bf16[320,128]{1,0:T(8,128)(2,1)S(1)}, bf16[320,128]{1,0:T(8,128)(2,1)S(1)}, u32[]{:S(2)}, u32[]{:S(2)}) %collective-permute-start.7) | collective-permute-done | bytes 81952 | tf_op jit(solution)/shard_map/ppermute | solution.py:26
  209.7 1.9 collective-permute-start.9
  211.7 7.7 %collective-permute-start.10 = (bf16[192,128]{1,0:T(8,128)(2,1)S(1)}, bf16[192,128]{1,0:T(8,128)(2,1)S(1)}, u32[]{:S(2)}, u32[]{:S(2)}) collective-permute-start(bf16[192,128]{1,0:T(8,128)(2,1)S(1)} %slice.93), channel_id=1, source_target_pairs={{0,176},{4,180},{8,184},{12,188},{16,0},{20,4},{24,8},{28,12},{32,... | collective-permute-start | bytes 147464 | tf_op jit(solution)/shard_map/ppermute | solution.py:26
  220.8 4.5 %collective-permute-start.12 = (bf16[8,256,128]{2,1,0:T(8,128)(2,1)S(1)}, bf16[8,256,128]{2,1,0:T(8,128)(2,1)S(1)}, u32[]{:S(2)}, u32[]{:S(2)}) collective-permute-start(bf16[8,256,128]{2,1,0:T(8,128)(2,1)S(1)} %place.1.p0), channel_id=1, source_target_pairs={{0,188},{4,0},{8,4},{12,8},{16,12},{20,16},{24,20},{28,24},{32,28}... | collective-permute-start | bytes 1572872 | tf_op jit(solution)/shard_map/ppermute | solution.py:26
  225.3 3.6 %collective-permute-start.11 = (bf16[8,256,128]{2,1,0:T(8,128)(2,1)S(1)}, bf16[8,256,128]{2,1,0:T(8,128)(2,1)S(1)}, u32[]{:S(2)}, u32[]{:S(2)}) collective-permute-start(bf16[8,256,128]{2,1,0:T(8,128)(2,1)S(1)} %place.1.p0), channel_id=1, source_target_pairs={{0,4},{4,8},{8,12},{12,16},{16,20},{20,24},{24,28},{28,32},{32,36}... | collective-permute-start | bytes 1572872 | tf_op jit(solution)/shard_map/ppermute | solution.py:26
  229.0 9.4 %all-gather.1 = bf16[8,64,256]{2,1,0:T(8,128)(2,1)S(1)} all-gather(bf16[2,64,256]{2,1,0:T(8,128)(2,1)S(1)} %pad_maximum_fusion.6), channel_id=3, replica_groups=mesh['y'=4,'zh'=2,'c'=2,'z8'=2,'z4'=2,'z2'=2,'z1'=2,'x'=4] {'x'}, dimensions={0}, use_global_device_ids=true | all-gather | bytes 327680 | tf_op jit(solution)/shard_map/all_gather | solution.py:171
  239.4 5.0 %collective-permute-start.14 = (bf16[4,256,128]{2,1,0:T(8,128)(2,1)S(1)}, bf16[4,256,128]{2,1,0:T(8,128)(2,1)S(1)}, u32[]{:S(2)}, u32[]{:S(2)}) collective-permute-start(bf16[4,256,128]{2,1,0:T(8,128)(2,1)S(1)} %slice.97), channel_id=1, source_target_pairs={{0,4},{4,8},{8,12},{12,16},{16,20},{20,24},{24,28},{28,32},{32,36}... | collective-permute-start | bytes 786440 | tf_op jit(solution)/shard_map/ppermute | solution.py:26
  244.4 1.9 collective-permute-start.13
  246.3 4.2 %collective-permute-done.14.p2b = bf16[4,256,128]{2,1,0:T(8,128)(2,1)S(1)} collective-permute-done((bf16[4,256,128]{2,1,0:T(8,128)(2,1)S(1)}, bf16[4,256,128]{2,1,0:T(8,128)(2,1)S(1)}, u32[]{:S(2)}, u32[]{:S(2)}) %collective-permute-start.14) | collective-permute-done | bytes 262176 | tf_op jit(solution)/shard_map/ppermute | solution.py:26
  253.5 23.0 %all-to-all-start.4 = ((bf16[32,8,2048]{2,1,0:T(8,128)(2,1)}), bf16[32,8,2048]{2,1,0:T(8,128)(2,1)S(1)}, u32[]{:S(2)}, u32[]{:S(2)}) async-start(bf16[32,8,2048]{2,1,0:T(8,128)(2,1)} %scale.1), calls=%async_computation.4 | async-start | bytes 2097152 | tf_op jit(solution)/shard_map/all_to_all | solution.py:114
  276.6 16.0 %all-to-all-done.4 = bf16[32,8,2048]{2,1,0:T(8,128)(2,1)S(1)} async-done(((bf16[32,8,2048]{2,1,0:T(8,128)(2,1)}), bf16[32,8,2048]{2,1,0:T(8,128)(2,1)S(1)}, u32[]{:S(2)}, u32[]{:S(2)}) %all-to-all-start.4) | async-done | bytes 1048608 | tf_op jit(solution)/shard_map/all_to_all | solution.py:114
  (54 shorter events, 12.3 us)
Async XLA Ops:
  1.6 63.5 %all-to-all-start = ((bf16[8,2,8,512]{3,2,1,0:T(8,128)(2,1)}), bf16[8,2,8,512]{3,2,1,0:T(8,128)(2,1)S(1)}, u32[]{:S(2)}, u32[]{:S(2)}) async-start(bf16[8,2,8,512]{3,2,1,0:T(8,128)(2,1)} %bitcast.9), calls=%async_computation | async-start | bytes 262144 | tf_op jit(solution)/shard_map/all_to_all | solution.py:114
  19.0 3.2 %copy-start.2 = (bf16[256,128]{1,0:T(8,128)(2,1)S(1)}, bf16[256,128]{1,0:T(8,128)(2,1)}, u32[]{:S(2)}) copy-start(bf16[256,128]{1,0:T(8,128)(2,1)} %param.5) | copy-start | bytes 196612
  19.0 3.2 %copy-start.3 = (bf16[256,128]{1,0:T(8,128)(2,1)S(1)}, bf16[256,128]{1,0:T(8,128)(2,1)}, u32[]{:S(2)}) copy-start(bf16[256,128]{1,0:T(8,128)(2,1)} %param.6) | copy-start | bytes 196612
  65.1 3.6 %copy-start = (bf16[8,256,128]{2,1,0:T(8,128)(2,1)}, bf16[8,256,128]{2,1,0:T(8,128)(2,1)S(1)}, u32[]{:S(2)}) copy-start(bf16[8,256,128]{2,1,0:T(8,128)(2,1)S(1)} %all-gather) | copy-start | bytes 1572868
  65.1 29.4 %all-to-all-start.1 = ((bf16[4,16,128,128]{3,2,1,0:T(8,128)(2,1)}), bf16[4,16,128,128]{3,2,1,0:T(8,128)(2,1)S(1)}, u32[]{:S(2)}, u32[]{:S(2)}) async-start(bf16[4,16,128,128]{3,2,1,0:T(8,128)(2,1)} %bitcast.70), calls=%async_computation.1 | async-start | bytes 4194304 | tf_op jit(solution)/shard_map/all_to_all | solution.py:114
  68.7 16.4 %collective-permute-start = (bf16[4,2,256,128]{3,2,1,0:T(8,128)(2,1)S(1)}, bf16[4,2,256,128]{3,2,1,0:T(8,128)(2,1)S(1)}, u32[]{:S(2)}, u32[]{:S(2)}) collective-permute-start(bf16[4,2,256,128]{3,2,1,0:T(8,128)(2,1)S(1)} %bitcast.77), channel_id=1, source_target_pairs={{0,8},{8,0},{1,9},{9,1},{2,10},{10,2},{3,11},{11,3},{4,12},{12,4},... | collective-permute-start | bytes 1572872 | tf_op jit(solution)/shard_map/ppermute | solution.py:22
  74.2 10.9 %copy-start.1 = (bf16[8,256,128]{2,1,0:T(8,128)(2,1)S(1)}, bf16[8,256,128]{2,1,0:T(8,128)(2,1)}, u32[]{:S(2)}) copy-start(bf16[8,256,128]{2,1,0:T(8,128)(2,1)} %copy-done) | copy-start | bytes 1572868
  94.5 49.4 %all-to-all-start.2 = ((bf16[4,16,128,128]{3,2,1,0:T(8,128)(2,1)}), bf16[4,16,128,128]{3,2,1,0:T(8,128)(2,1)}, u32[]{:S(2)}, u32[]{:S(2)}) async-start(bf16[4,16,128,128]{3,2,1,0:T(8,128)(2,1)} %bitcast.69), calls=%async_computation.2 | async-start | bytes 4194304 | tf_op jit(solution)/shard_map/all_to_all | solution.py:114
  99.0 44.9 %collective-permute-start.1 = (bf16[8,2,256,128]{3,2,1,0:T(8,128)(2,1)S(1)}, bf16[8,2,256,128]{3,2,1,0:T(8,128)(2,1)}, u32[]{:S(2)}, u32[]{:S(2)}) collective-permute-start(bf16[8,2,256,128]{3,2,1,0:T(8,128)(2,1)S(1)} %pad_maximum_fusion.near_ref), channel_id=1, source_target_pairs={{0,4},{4,0},{1,5},{5,1},{2,6},{6,2},{3,7},{7,3},{8,12},{12,8},{9,1... | collective-permute-start | bytes 3145736 | tf_op jit(solution)/shard_map/ppermute | solution.py:22
  106.0 37.9 %collective-permute-start.2 = (bf16[8,8,512]{2,1,0:T(8,128)(2,1)S(1)}, bf16[8,8,512]{2,1,0:T(8,128)(2,1)S(1)}, u32[]{:S(2)}, u32[]{:S(2)}) collective-permute-start(bf16[8,8,512]{2,1,0:T(8,128)(2,1)S(1)} %fusion.2), channel_id=1, source_target_pairs={{0,128},{128,0},{1,129},{129,1},{2,130},{130,2},{3,131},{131,3},{4... | collective-permute-start | bytes 196616 | tf_op jit(solution)/shard_map/ppermute | solution.py:22
  158.2 11.7 %collective-permute-start.4 = (bf16[320,128]{1,0:T(8,128)(2,1)S(1)}, bf16[320,128]{1,0:T(8,128)(2,1)S(1)}, u32[]{:S(2)}, u32[]{:S(2)}) collective-permute-start(bf16[320,128]{1,0:T(8,128)(2,1)S(1)} %get-tuple-element.73), channel_id=1, source_target_pairs={{0,176},{4,180},{8,184},{12,188},{16,0},{20,4},{24,8},{28,12},{32,... | collective-permute-start | bytes 245768 | tf_op jit(solution)/shard_map/ppermute | solution.py:26
  167.9 9.7 %collective-permute-start.3 = (bf16[320,128]{1,0:T(8,128)(2,1)S(1)}, bf16[320,128]{1,0:T(8,128)(2,1)S(1)}, u32[]{:S(2)}, u32[]{:S(2)}) collective-permute-start(bf16[320,128]{1,0:T(8,128)(2,1)S(1)} %get-tuple-element.74), channel_id=1, source_target_pairs={{0,16},{4,20},{8,24},{12,28},{16,32},{20,36},{24,40},{28,44},{32,4... | collective-permute-start | bytes 245768 | tf_op jit(solution)/shard_map/ppermute | solution.py:26
  177.6 10.1 %collective-permute-start.6 = (bf16[320,128]{1,0:T(8,128)(2,1)S(1)}, bf16[320,128]{1,0:T(8,128)(2,1)S(1)}, u32[]{:S(2)}, u32[]{:S(2)}) collective-permute-start(bf16[320,128]{1,0:T(8,128)(2,1)S(1)} %collective-permute-done.4.refs_0_), channel_id=1, source_target_pairs={{0,176},{4,180},{8,184},{12,188},{16,0},{20,4},{24,8},{28,12},{32,... | collective-permute-start | bytes 245768 | tf_op jit(solution)/shard_map/ppermute | solution.py:26
  179.5 9.2 %collective-permute-start.5 = (bf16[320,128]{1,0:T(8,128)(2,1)S(1)}, bf16[320,128]{1,0:T(8,128)(2,1)S(1)}, u32[]{:S(2)}, u32[]{:S(2)}) collective-permute-start(bf16[320,128]{1,0:T(8,128)(2,1)S(1)} %collective-permute-done.3.refs_5_), channel_id=1, source_target_pairs={{0,16},{4,20},{8,24},{12,28},{16,32},{20,36},{24,40},{28,44},{32,4... | collective-permute-start | bytes 245768 | tf_op jit(solution)/shard_map/ppermute | solution.py:26
  188.7 15.9 %collective-permute-start.8 = (bf16[320,128]{1,0:T(8,128)(2,1)S(1)}, bf16[320,128]{1,0:T(8,128)(2,1)S(1)}, u32[]{:S(2)}, u32[]{:S(2)}) collective-permute-start(bf16[320,128]{1,0:T(8,128)(2,1)S(1)} %collective-permute-done.6.refs_1_), channel_id=1, source_target_pairs={{0,176},{4,180},{8,184},{12,188},{16,0},{20,4},{24,8},{28,12},{32,... | collective-permute-start | bytes 245768 | tf_op jit(solution)/shard_map/ppermute | solution.py:26
  199.2 10.5 %collective-permute-start.7 = (bf16[320,128]{1,0:T(8,128)(2,1)S(1)}, bf16[320,128]{1,0:T(8,128)(2,1)S(1)}, u32[]{:S(2)}, u32[]{:S(2)}) collective-permute-start(bf16[320,128]{1,0:T(8,128)(2,1)S(1)} %collective-permute-done.5.refs_4_), channel_id=1, source_target_pairs={{0,16},{4,20},{8,24},{12,28},{16,32},{20,36},{24,40},{28,44},{32,4... | collective-permute-start | bytes 245768 | tf_op jit(solution)/shard_map/ppermute | solution.py:26
  209.7 9.6 %collective-permute-start.9 = (bf16[192,128]{1,0:T(8,128)(2,1)S(1)}, bf16[192,128]{1,0:T(8,128)(2,1)S(1)}, u32[]{:S(2)}, u32[]{:S(2)}) collective-permute-start(bf16[192,128]{1,0:T(8,128)(2,1)S(1)} %slice.92), channel_id=1, source_target_pairs={{0,16},{4,20},{8,24},{12,28},{16,32},{20,36},{24,40},{28,44},{32,4... | collective-permute-start | bytes 147464 | tf_op jit(solution)/shard_map/ppermute | solution.py:26
  211.7 9.1 %collective-permute-start.10 = (bf16[192,128]{1,0:T(8,128)(2,1)S(1)}, bf16[192,128]{1,0:T(8,128)(2,1)S(1)}, u32[]{:S(2)}, u32[]{:S(2)}) collective-permute-start(bf16[192,128]{1,0:T(8,128)(2,1)S(1)} %slice.93), channel_id=1, source_target_pairs={{0,176},{4,180},{8,184},{12,188},{16,0},{20,4},{24,8},{28,12},{32,... | collective-permute-start | bytes 147464 | tf_op jit(solution)/shard_map/ppermute | solution.py:26
  220.8 17.6 %collective-permute-start.12 = (bf16[8,256,128]{2,1,0:T(8,128)(2,1)S(1)}, bf16[8,256,128]{2,1,0:T(8,128)(2,1)S(1)}, u32[]{:S(2)}, u32[]{:S(2)}) collective-permute-start(bf16[8,256,128]{2,1,0:T(8,128)(2,1)S(1)} %place.1.p0), channel_id=1, source_target_pairs={{0,188},{4,0},{8,4},{12,8},{16,12},{20,16},{24,20},{28,24},{32,28}... | collective-permute-start | bytes 1572872 | tf_op jit(solution)/shard_map/ppermute | solution.py:26
  225.3 14.0 %collective-permute-start.11 = (bf16[8,256,128]{2,1,0:T(8,128)(2,1)S(1)}, bf16[8,256,128]{2,1,0:T(8,128)(2,1)S(1)}, u32[]{:S(2)}, u32[]{:S(2)}) collective-permute-start(bf16[8,256,128]{2,1,0:T(8,128)(2,1)S(1)} %place.1.p0), channel_id=1, source_target_pairs={{0,4},{4,8},{8,12},{12,16},{16,20},{20,24},{24,28},{28,32},{32,36}... | collective-permute-start | bytes 1572872 | tf_op jit(solution)/shard_map/ppermute | solution.py:26
  239.4 11.1 %collective-permute-start.14 = (bf16[4,256,128]{2,1,0:T(8,128)(2,1)S(1)}, bf16[4,256,128]{2,1,0:T(8,128)(2,1)S(1)}, u32[]{:S(2)}, u32[]{:S(2)}) collective-permute-start(bf16[4,256,128]{2,1,0:T(8,128)(2,1)S(1)} %slice.97), channel_id=1, source_target_pairs={{0,4},{4,8},{8,12},{12,16},{16,20},{20,24},{24,28},{28,32},{32,36}... | collective-permute-start | bytes 786440 | tf_op jit(solution)/shard_map/ppermute | solution.py:26
  244.4 7.5 %collective-permute-start.13 = (bf16[4,256,128]{2,1,0:T(8,128)(2,1)S(1)}, bf16[4,256,128]{2,1,0:T(8,128)(2,1)S(1)}, u32[]{:S(2)}, u32[]{:S(2)}) collective-permute-start(bf16[4,256,128]{2,1,0:T(8,128)(2,1)S(1)} %slice.96), channel_id=1, source_target_pairs={{0,188},{4,0},{8,4},{12,8},{16,12},{20,16},{24,20},{28,24},{32,28}... | collective-permute-start | bytes 786440 | tf_op jit(solution)/shard_map/ppermute | solution.py:26
  253.5 39.1 %all-to-all-start.4 = ((bf16[32,8,2048]{2,1,0:T(8,128)(2,1)}), bf16[32,8,2048]{2,1,0:T(8,128)(2,1)S(1)}, u32[]{:S(2)}, u32[]{:S(2)}) async-start(bf16[32,8,2048]{2,1,0:T(8,128)(2,1)} %scale.1), calls=%async_computation.4 | async-start | bytes 2097152 | tf_op jit(solution)/shard_map/all_to_all | solution.py:114

commit v8 on v6

--- a/solution.py
+++ b/solution.py
@@ -26,9 +26,9 @@
     return lax.ppermute(value, RING, [(i, (i + hops) % 32) for i in range(32)])
 
 
-def project_kernel(z_ref, near_ref, far_ref, basis_out_ref, basis_in_ref, out_ref):
+def project_kernel(z_ref, near_ref, far_ref, basis_ref, out_ref):
     residue = lax.rem(z_ref[0], 4)
-    for m, basis_ref in enumerate((basis_out_ref, basis_in_ref)):
+    for m in range(2):
         for pair in range(2):
             total = jnp.zeros((256, 256), f32)
             for step in range(8):
@@ -38,7 +38,7 @@
                 z0 = 4 * (at % 4) + (residue ^ (2 * (at // 4) + step // 4))
                 z1 = z0 + 4
                 columns = [
-                    jnp.concatenate([basis_ref[2 * pair + i, z0], basis_ref[2 * pair + i, z1]], axis=0) for i in range(2)
+                    jnp.concatenate([basis_ref[2 * pair + i, m, z0], basis_ref[2 * pair + i, m, z1]], axis=0) for i in range(2)
                 ]
                 right = jnp.concatenate(columns, axis=1)
                 total = total + jnp.dot(left, right, preferred_element_type=f32)
@@ -46,16 +46,16 @@
             out_ref[2 * pair + 1, m] = total[:, 128:].astype(bf16)
 
 
-def project(z, near, far, basis_out, basis_in):
+def project(z, near, far, basis):
     return pl.pallas_call(
         project_kernel,
         out_shape=jax.ShapeDtypeStruct((X, 2, 256, 128), bf16),
-        in_specs=[SCALAR] + [WHOLE] * 4,
+        in_specs=[SCALAR] + [WHOLE] * 3,
         out_specs=WHOLE,
         compiler_params=PARAMS,
         cost_estimate=pl.CostEstimate(flops=4 * 256 * 2048 * 512, bytes_accessed=6800000, transcendentals=0),
         name="project",
-    )(z, near, far, basis_out, basis_in)
+    )(z, near, far, basis)
 
 
 def scale_kernel(rows_ref, p0, p1, p2a, p2b, p3, out_ref):
@@ -105,20 +105,18 @@
     def in_order(own, other):
         return jnp.stack([jnp.where(high, other, own), jnp.where(high, own, other)])
 
-    basis_out = basis_out.reshape(16, X, 128, 128).transpose(1, 0, 2, 3)
+    bases = jnp.stack([basis_out.reshape(16, X, 128, 128), basis_in.reshape(16, X, 128, 128)])
+    bases = exchange(bases.transpose(2, 0, 1, 3, 4), "x")
 
-    b_out = exchange(basis_out, "x")
     have = lax.all_gather(jnp.stack([out_grads, activations]), ("z8", "z4"), axis=0, tiled=False)
-    have, b_out, basis_in, grad_eigen = together(have, b_out, basis_in, grad_eigen)
-    b_in = exchange(basis_in.reshape(16, X, 128, 128).transpose(1, 0, 2, 3), "x")
     have = jnp.concatenate([have, swap(have, "z2")], axis=0)
-    have, b_in, grad_eigen = together(have, b_in, grad_eigen)
+    have, bases, grad_eigen = together(have, bases, grad_eigen)
     grad = grad_eigen.reshape(Y, ZH, C, 8, 512).transpose(0, 2, 1, 3, 4).reshape(Y * C, ZH, 8, 512)
     grad = exchange(grad, ("y", "c"))
     far, have, grad = together(swap(have, "z1"), have, grad)
     grad = grad.transpose(1, 0, 2, 3)
 
-    part = project(z, have, far, b_out, b_in)
+    part = project(z, have, far, bases)
     projected = jnp.sum(exchange(part, "x").astype(f32), axis=0)
     squares = (projected * projected).astype(bf16)
     squares_in = squares[1].T.reshape(Y, ZH, C * 8, tokens).transpose(1, 0, 2, 3).reshape(ZH, 64, tokens)

time: 274 us -> 268 us (0.978)
  starting transfers between devices: 107 us -> 95.8 us
  local copies, waits for them, and re-layouts: 8.23 us -> 0.92 us
  blocking collectives: 97.8 us -> 105 us
  other arithmetic: 2.26 us -> 5.01 us
    all_to_all x5 -> x4, starting transfers between devices: 39.6 us -> 33.1 us  [exchange(): return lax.all_to_all(value, axis, split_axis=0, concat_axis=0, tiled=True)]
    reshape x2 -> x0, local copies, waits for them, and re-layouts: 6.51 us -> none  [the longest x1 3.34 us: per_device(): basis_in.reshape(16, X, 128, 128).transpose(1, 0, 2, 3)]
    transpose x0 -> x1, other arithmetic: none -> 3.78 us  [per_device(): bases = exchange(bases.transpose(2, 0, 1, 3, 4), 'x')]
    all_gather x1, blocking collectives: 46 us -> 49.7 us  [per_device(): p0 = lax.all_gather(squares[0], ('zh', 'z8', 'z4'), axis=0, tiled=False)]
    ppermute x3, starting transfers between devices: 54.1 us -> 51 us  [swap(): return lax.ppermute(value, axis, [(0, 1), (1, 0)])]
    all_gather x1, blocking collectives: 42.4 us -> 45.5 us  [per_device(): lax.all_gather(jnp.stack([out_grads, activations]), ('z8', 'z4'), axis=0,...]
    all_to_all x5 -> x4, waiting for transfers between devices: 28.2 us -> 28.2 us  [exchange(): return lax.all_to_all(value, axis, split_axis=0, concat_axis=0, tiled=True)]
  transfers between devices with their start and end apart: 12 -> 11, of which waited for: 7 -> 7; matrix products, arithmetic and copies ran while one was open for 1% -> 0% of each run, Pallas kernels for 0% -> 0%
where the time goes in v8:
time: 268 us; the launch traced here: 267 us
  blocking collectives  105 us (39%)
  starting transfers between devices  95.8 us (36%)
  waiting for transfers between devices  54.3 us (20%)
  Pallas kernels  5.93 us (2%)
  other arithmetic  5.01 us (2%)
    ppermute x3, starting transfers between devices, swap(): return lax.ppermute(value, axis, [(0, 1), (1, 0)])  51 us
    all_gather x1, blocking collectives, per_device(): p0 = lax.all_gather(squares[0], ('zh', 'z8', 'z4'), axis=0, tiled=False)  49.7 us
    all_gather x1, blocking collectives, per_device(): lax.all_gather(jnp.stack([out_grads, activations]), ('z8', 'z4'), axis=0,...  45.5 us
    all_to_all x4, starting transfers between devices, exchange(): return lax.all_to_all(value, axis, split_axis=0, concat_axis=0, tiled=True)  33.1 us
    all_to_all x4, waiting for transfers between devices, exchange(): return lax.all_to_all(value, axis, split_axis=0, concat_axis=0, tiled=True)  28.2 us
    ppermute x3, waiting for transfers between devices, swap(): return lax.ppermute(value, axis, [(0, 1), (1, 0)])  20.7 us
    ppermute x4, starting transfers between devices, around(): return lax.ppermute(value, RING, [(i, (i + hops) % 32) for i in range(32)])  11.8 us
    all_gather x1, blocking collectives, per_device(): rows_in = lax.all_gather(rows_in, 'x', axis=0, tiled=False)  9.67 us
  transfers between devices with their start and end apart: 11, of which 7 were waited for; matrix products, arithmetic and copies ran while one was open for 0% of the time, Pallas kernels for 0%

profile of v8, /device:TPU:1, one launch (start us, length us, event | category | flops | bytes accessed | tf_op | source)
XLA Modules:
  0.0 267.1 jit_solution(3428704273806652671)
XLA Ops:
  0.0 3.8 %copy_bitcast_fusion = bf16[4,2,16,128,128]{4,3,2,1,0:T(8,128)(2,1)} fusion(bf16[1,16,4,128,128]{4,3,2,1,0:T(8,128)(2,1)} %bitcast.55, bf16[1,16,4,128,128]{4,3,2,1,0:T(8,128)(2,1)} %bitcast.56), kind=kLoop, calls=%fused_computation.1 | loop fusion | flops 2097152 | bytes 8388608 | tf_op jit(solution)/shard_map/transpose | solution.py:109
  3.8 5.0 %all-to-all-start = ((bf16[4,2,16,128,128]{4,3,2,1,0:T(8,128)(2,1)}), bf16[4,2,16,128,128]{4,3,2,1,0:T(8,128)(2,1)}, u32[]{:S(2)}, u32[]{:S(2)}) async-start(bf16[4,2,16,128,128]{4,3,2,1,0:T(8,128)(2,1)} %copy_bitcast_fusion), calls=%async_computation | async-start | bytes 8388608 | tf_op jit(solution)/shard_map/all_to_all | solution.py:90
  8.8 45.5 %all-gather = bf16[8,256,128]{2,1,0:T(8,128)(2,1)S(1)} all-gather(bf16[2,256,128]{2,1,0:T(8,128)(2,1)S(1)} %pad_maximum_fusion.2), channel_id=2, replica_groups=mesh['y'=4,'zh'=2,'c'=2,'z8'=2,'z4'=2,'z2'=2,'z1'=2,'x'=4] {'z8','z4'}, dimensions={0}, use_global_device_ids=true | all-gather | bytes 655360 | tf_op jit(solution)/shard_map/all_gather | solution.py:111
  54.3 14.6 %collective-permute-start = (bf16[4,2,256,128]{3,2,1,0:T(8,128)(2,1)S(1)}, bf16[4,2,256,128]{3,2,1,0:T(8,128)(2,1)S(1)}, u32[]{:S(2)}, u32[]{:S(2)}) collective-permute-start(bf16[4,2,256,128]{3,2,1,0:T(8,128)(2,1)S(1)} %bitcast.53), channel_id=1, source_target_pairs={{0,8},{8,0},{1,9},{9,1},{2,10},{10,2},{3,11},{11,3},{4,12},{12,4},... | collective-permute-start | bytes 1572872 | tf_op jit(solution)/shard_map/ppermute | solution.py:22
  69.0 11.1 %collective-permute-done = bf16[4,2,256,128]{3,2,1,0:T(8,128)(2,1)S(1)} collective-permute-done((bf16[4,2,256,128]{3,2,1,0:T(8,128)(2,1)S(1)}, bf16[4,2,256,128]{3,2,1,0:T(8,128)(2,1)S(1)}, u32[]{:S(2)}, u32[]{:S(2)}) %collective-permute-start) | collective-permute-done | bytes 524320 | tf_op jit(solution)/shard_map/ppermute | solution.py:22
  80.1 0.1 pad_maximum_fusion.1.near_ref
  80.2 0.0 all-to-all-done.basis_ref
  80.2 14.9 %collective-permute-start.1 = (bf16[8,2,256,128]{3,2,1,0:T(8,128)(2,1)S(1)}, bf16[8,2,256,128]{3,2,1,0:T(8,128)(2,1)S(1)}, u32[]{:S(2)}, u32[]{:S(2)}) collective-permute-start(bf16[8,2,256,128]{3,2,1,0:T(8,128)(2,1)S(1)} %pad_maximum_fusion.1.near_ref), channel_id=1, source_target_pairs={{0,4},{4,0},{1,5},{5,1},{2,6},{6,2},{3,7},{7,3},{8,12},{12,8},{9,1... | collective-permute-start | bytes 3145736 | tf_op jit(solution)/shard_map/ppermute | solution.py:22
  95.0 0.7 copy.36
  95.7 6.3 %all-to-all-start.1 = ((bf16[8,2,8,512]{3,2,1,0:T(8,128)(2,1)}), bf16[8,2,8,512]{3,2,1,0:T(8,128)(2,1)S(1)}, u32[]{:S(2)}, u32[]{:S(2)}) async-start(bf16[8,2,8,512]{3,2,1,0:T(8,128)(2,1)} %bitcast.9), calls=%async_computation.1 | async-start | bytes 262144 | tf_op jit(solution)/shard_map/all_to_all | solution.py:90
  102.0 5.3 %all-to-all-done.1 = bf16[8,2,8,512]{3,2,1,0:T(8,128)(2,1)S(1)} async-done(((bf16[8,2,8,512]{3,2,1,0:T(8,128)(2,1)}), bf16[8,2,8,512]{3,2,1,0:T(8,128)(2,1)S(1)}, u32[]{:S(2)}, u32[]{:S(2)}) %all-to-all-start.1) | async-done | bytes 131104 | tf_op jit(solution)/shard_map/all_to_all | solution.py:90
  107.3 9.6 %collective-permute-done.1.far_ref = bf16[8,2,256,128]{3,2,1,0:T(8,128)(2,1)S(1)} collective-permute-done((bf16[8,2,256,128]{3,2,1,0:T(8,128)(2,1)S(1)}, bf16[8,2,256,128]{3,2,1,0:T(8,128)(2,1)S(1)}, u32[]{:S(2)}, u32[]{:S(2)}) %collective-permute-start.1) | collective-permute-done | bytes 1048608 | tf_op jit(solution)/shard_map/ppermute | solution.py:22
  116.9 4.2 %project.1 = bf16[4,2,256,128]{3,2,1,0:T(8,128)(2,1)} custom-call(s32[1]{0:T(128)} %bitcast.z_ref, bf16[8,2,256,128]{3,2,1,0:T(8,128)(2,1)S(1)} %pad_maximum_fusion.1.near_ref, bf16[8,2,256,128]{3,2,1,0:T(8,128)(2,1)S(1)} %collective-permute-done.1.far_ref, bf16[4,2,16,128,128]{4,3,2,1,0:T(8,128)(2,1)} %all-to-all-done.basis_ref), custom_call_target="tpu_custom_call" | custom-call | flops 1073741824 | bytes 6800000 | tf_op jit(solution)/shard_map/project/pallas_call | solution.py:50
  121.1 3.5 %all-to-all-start.2 = ((bf16[4,2,256,128]{3,2,1,0:T(8,128)(2,1)}), bf16[4,2,256,128]{3,2,1,0:T(8,128)(2,1)S(1)}, u32[]{:S(2)}, u32[]{:S(2)}) async-start(bf16[4,2,256,128]{3,2,1,0:T(8,128)(2,1)} %project.1), calls=%async_computation.2 | async-start | bytes 1048576 | tf_op jit(solution)/shard_map/all_to_all | solution.py:90
  124.6 6.9 %all-to-all-done.2 = bf16[4,2,256,128]{3,2,1,0:T(8,128)(2,1)S(1)} async-done(((bf16[4,2,256,128]{3,2,1,0:T(8,128)(2,1)}), bf16[4,2,256,128]{3,2,1,0:T(8,128)(2,1)S(1)}, u32[]{:S(2)}, u32[]{:S(2)}) %all-to-all-start.2) | async-done | bytes 524320 | tf_op jit(solution)/shard_map/all_to_all | solution.py:90
  131.5 0.1 convert_reduce_fusion.1
  131.6 0.1 copy.37
  131.8 21.5 %collective-permute-start.2 = (bf16[64,768]{1,0:T(8,128)(2,1)S(1)}, bf16[64,768]{1,0:T(8,128)(2,1)S(1)}, u32[]{:S(2)}, u32[]{:S(2)}) collective-permute-start(bf16[64,768]{1,0:T(8,128)(2,1)S(1)} %pad_maximum_fusion.3), channel_id=1, source_target_pairs={{0,128},{128,0},{1,129},{129,1},{2,130},{130,2},{3,131},{131,3},{4... | collective-permute-start | bytes 294920 | tf_op jit(solution)/shard_map/ppermute | solution.py:22
  153.3 49.7 %all_gather.17.p0 = bf16[8,256,128]{2,1,0:T(8,128)(2,1)S(1)} all-gather(bf16[1,256,128]{2,1,0:T(8,128)(2,1)S(1)} %get-tuple-element.40), channel_id=1, replica_groups=mesh['y'=4,'zh'=2,'c'=2,'z8'=2,'z4'=2,'z2'=2,'z1'=2,'x'=4] {'zh','z8','z4'}, dimensions={0}, use_global_device_ids=true | all-gather | bytes 589824 | tf_op jit(solution)/shard_map/all_gather | solution.py:125
  203.0 0.0 collective-permute-done.2
  203.0 1.9 collective-permute-start.4
  204.9 3.4 %collective-permute-start.3 = (bf16[8,256,128]{2,1,0:T(8,128)(2,1)S(1)}, bf16[8,256,128]{2,1,0:T(8,128)(2,1)S(1)}, u32[]{:S(2)}, u32[]{:S(2)}) collective-permute-start(bf16[8,256,128]{2,1,0:T(8,128)(2,1)S(1)} %all_gather.17.p0), channel_id=1, source_target_pairs={{0,4},{4,8},{8,12},{12,16},{16,20},{20,24},{24,28},{28,32},{32,36}... | collective-permute-start | bytes 1572872 | tf_op jit(solution)/shard_map/ppermute | solution.py:26
  208.3 9.7 %all-gather.1 = bf16[8,64,256]{2,1,0:T(8,128)(2,1)S(1)} all-gather(bf16[2,64,256]{2,1,0:T(8,128)(2,1)S(1)} %pad_maximum_fusion.4), channel_id=3, replica_groups=mesh['y'=4,'zh'=2,'c'=2,'z8'=2,'z4'=2,'z2'=2,'z1'=2,'x'=4] {'x'}, dimensions={0}, use_global_device_ids=true | all-gather | bytes 327680 | tf_op jit(solution)/shard_map/all_gather | solution.py:128
  218.0 3.0 %collective-permute-start.6 = (bf16[4,256,128]{2,1,0:T(8,128)(2,1)S(1)}, bf16[4,256,128]{2,1,0:T(8,128)(2,1)S(1)}, u32[]{:S(2)}, u32[]{:S(2)}) collective-permute-start(bf16[4,256,128]{2,1,0:T(8,128)(2,1)S(1)} %slice.60), channel_id=1, source_target_pairs={{0,4},{4,8},{8,12},{12,16},{16,20},{20,24},{24,28},{28,32},{32,36}... | collective-permute-start | bytes 786440 | tf_op jit(solution)/shard_map/ppermute | solution.py:26
  221.1 3.5 %collective-permute-start.5 = (bf16[4,256,128]{2,1,0:T(8,128)(2,1)S(1)}, bf16[4,256,128]{2,1,0:T(8,128)(2,1)S(1)}, u32[]{:S(2)}, u32[]{:S(2)}) collective-permute-start(bf16[4,256,128]{2,1,0:T(8,128)(2,1)S(1)} %slice.59), channel_id=1, source_target_pairs={{0,188},{4,0},{8,4},{12,8},{16,12},{20,16},{24,20},{28,24},{32,28}... | collective-permute-start | bytes 786440 | tf_op jit(solution)/shard_map/ppermute | solution.py:26
  224.6 4.9 %collective-permute-done.6.p2b = bf16[4,256,128]{2,1,0:T(8,128)(2,1)S(1)} collective-permute-done((bf16[4,256,128]{2,1,0:T(8,128)(2,1)S(1)}, bf16[4,256,128]{2,1,0:T(8,128)(2,1)S(1)}, u32[]{:S(2)}, u32[]{:S(2)}) %collective-permute-start.6) | collective-permute-done | bytes 262176 | tf_op jit(solution)/shard_map/ppermute | solution.py:26
  229.5 0.6 collective-permute-done.5.p2a
  230.1 1.7 scale.1
  231.8 18.2 %all-to-all-start.3 = ((bf16[32,8,2048]{2,1,0:T(8,128)(2,1)}), bf16[32,8,2048]{2,1,0:T(8,128)(2,1)S(1)}, u32[]{:S(2)}, u32[]{:S(2)}) async-start(bf16[32,8,2048]{2,1,0:T(8,128)(2,1)} %scale.1), calls=%async_computation.3 | async-start | bytes 2097152 | tf_op jit(solution)/shard_map/all_to_all | solution.py:90
  250.1 16.0 %all-to-all-done.3 = bf16[32,8,2048]{2,1,0:T(8,128)(2,1)S(1)} async-done(((bf16[32,8,2048]{2,1,0:T(8,128)(2,1)}), bf16[32,8,2048]{2,1,0:T(8,128)(2,1)S(1)}, u32[]{:S(2)}, u32[]{:S(2)}) %all-to-all-start.3) | async-done | bytes 1048608 | tf_op jit(solution)/shard_map/all_to_all | solution.py:90
  266.1 0.1 convert_reduce_fusion
  266.4 0.7 divide_convert_fusion
  (28 shorter events, 0.4 us)
Async XLA Ops:
  3.8 5.0 %copy-start.1 = (bf16[256,128]{1,0:T(8,128)(2,1)S(1)}, bf16[256,128]{1,0:T(8,128)(2,1)}, u32[]{:S(2)}) copy-start(bf16[256,128]{1,0:T(8,128)(2,1)} %param.5) | copy-start | bytes 196612
  3.8 5.0 %copy-start.2 = (bf16[256,128]{1,0:T(8,128)(2,1)S(1)}, bf16[256,128]{1,0:T(8,128)(2,1)}, u32[]{:S(2)}) copy-start(bf16[256,128]{1,0:T(8,128)(2,1)} %param.6) | copy-start | bytes 196612
  3.8 91.2 %copy-start = (bf16[128,512]{1,0:T(8,128)(2,1)S(1)}, bf16[128,512]{1,0:T(8,128)(2,1)}, u32[]{:S(2)}) copy-start(bf16[128,512]{1,0:T(8,128)(2,1)} %param.9) | copy-start | bytes 393220
  3.8 76.4 %all-to-all-start = ((bf16[4,2,16,128,128]{4,3,2,1,0:T(8,128)(2,1)}), bf16[4,2,16,128,128]{4,3,2,1,0:T(8,128)(2,1)}, u32[]{:S(2)}, u32[]{:S(2)}) async-start(bf16[4,2,16,128,128]{4,3,2,1,0:T(8,128)(2,1)} %copy_bitcast_fusion), calls=%async_computation | async-start | bytes 8388608 | tf_op jit(solution)/shard_map/all_to_all | solution.py:90
  54.3 25.7 %collective-permute-start = (bf16[4,2,256,128]{3,2,1,0:T(8,128)(2,1)S(1)}, bf16[4,2,256,128]{3,2,1,0:T(8,128)(2,1)S(1)}, u32[]{:S(2)}, u32[]{:S(2)}) collective-permute-start(bf16[4,2,256,128]{3,2,1,0:T(8,128)(2,1)S(1)} %bitcast.53), channel_id=1, source_target_pairs={{0,8},{8,0},{1,9},{9,1},{2,10},{10,2},{3,11},{11,3},{4,12},{12,4},... | collective-permute-start | bytes 1572872 | tf_op jit(solution)/shard_map/ppermute | solution.py:22
  80.2 36.7 %collective-permute-start.1 = (bf16[8,2,256,128]{3,2,1,0:T(8,128)(2,1)S(1)}, bf16[8,2,256,128]{3,2,1,0:T(8,128)(2,1)S(1)}, u32[]{:S(2)}, u32[]{:S(2)}) collective-permute-start(bf16[8,2,256,128]{3,2,1,0:T(8,128)(2,1)S(1)} %pad_maximum_fusion.1.near_ref), channel_id=1, source_target_pairs={{0,4},{4,0},{1,5},{5,1},{2,6},{6,2},{3,7},{7,3},{8,12},{12,8},{9,1... | collective-permute-start | bytes 3145736 | tf_op jit(solution)/shard_map/ppermute | solution.py:22
  95.7 11.6 %all-to-all-start.1 = ((bf16[8,2,8,512]{3,2,1,0:T(8,128)(2,1)}), bf16[8,2,8,512]{3,2,1,0:T(8,128)(2,1)S(1)}, u32[]{:S(2)}, u32[]{:S(2)}) async-start(bf16[8,2,8,512]{3,2,1,0:T(8,128)(2,1)} %bitcast.9), calls=%async_computation.1 | async-start | bytes 262144 | tf_op jit(solution)/shard_map/all_to_all | solution.py:90
  121.1 10.4 %all-to-all-start.2 = ((bf16[4,2,256,128]{3,2,1,0:T(8,128)(2,1)}), bf16[4,2,256,128]{3,2,1,0:T(8,128)(2,1)S(1)}, u32[]{:S(2)}, u32[]{:S(2)}) async-start(bf16[4,2,256,128]{3,2,1,0:T(8,128)(2,1)} %project.1), calls=%async_computation.2 | async-start | bytes 1048576 | tf_op jit(solution)/shard_map/all_to_all | solution.py:90
  131.8 71.2 %collective-permute-start.2 = (bf16[64,768]{1,0:T(8,128)(2,1)S(1)}, bf16[64,768]{1,0:T(8,128)(2,1)S(1)}, u32[]{:S(2)}, u32[]{:S(2)}) collective-permute-start(bf16[64,768]{1,0:T(8,128)(2,1)S(1)} %pad_maximum_fusion.3), channel_id=1, source_target_pairs={{0,128},{128,0},{1,129},{129,1},{2,130},{130,2},{3,131},{131,3},{4... | collective-permute-start | bytes 294920 | tf_op jit(solution)/shard_map/ppermute | solution.py:22
  203.0 15.0 %collective-permute-start.4 = (bf16[8,256,128]{2,1,0:T(8,128)(2,1)S(1)}, bf16[8,256,128]{2,1,0:T(8,128)(2,1)S(1)}, u32[]{:S(2)}, u32[]{:S(2)}) collective-permute-start(bf16[8,256,128]{2,1,0:T(8,128)(2,1)S(1)} %all_gather.17.p0), channel_id=1, source_target_pairs={{0,188},{4,0},{8,4},{12,8},{16,12},{20,16},{24,20},{28,24},{32,28}... | collective-permute-start | bytes 1572872 | tf_op jit(solution)/shard_map/ppermute | solution.py:26
  204.9 13.1 %collective-permute-start.3 = (bf16[8,256,128]{2,1,0:T(8,128)(2,1)S(1)}, bf16[8,256,128]{2,1,0:T(8,128)(2,1)S(1)}, u32[]{:S(2)}, u32[]{:S(2)}) collective-permute-start(bf16[8,256,128]{2,1,0:T(8,128)(2,1)S(1)} %all_gather.17.p0), channel_id=1, source_target_pairs={{0,4},{4,8},{8,12},{12,16},{16,20},{20,24},{24,28},{28,32},{32,36}... | collective-permute-start | bytes 1572872 | tf_op jit(solution)/shard_map/ppermute | solution.py:26
  218.0 11.5 %collective-permute-start.6 = (bf16[4,256,128]{2,1,0:T(8,128)(2,1)S(1)}, bf16[4,256,128]{2,1,0:T(8,128)(2,1)S(1)}, u32[]{:S(2)}, u32[]{:S(2)}) collective-permute-start(bf16[4,256,128]{2,1,0:T(8,128)(2,1)S(1)} %slice.60), channel_id=1, source_target_pairs={{0,4},{4,8},{8,12},{12,16},{16,20},{20,24},{24,28},{28,32},{32,36}... | collective-permute-start | bytes 786440 | tf_op jit(solution)/shard_map/ppermute | solution.py:26
  221.1 9.0 %collective-permute-start.5 = (bf16[4,256,128]{2,1,0:T(8,128)(2,1)S(1)}, bf16[4,256,128]{2,1,0:T(8,128)(2,1)S(1)}, u32[]{:S(2)}, u32[]{:S(2)}) collective-permute-start(bf16[4,256,128]{2,1,0:T(8,128)(2,1)S(1)} %slice.59), channel_id=1, source_target_pairs={{0,188},{4,0},{8,4},{12,8},{16,12},{20,16},{24,20},{28,24},{32,28}... | collective-permute-start | bytes 786440 | tf_op jit(solution)/shard_map/ppermute | solution.py:26
  231.8 34.3 %all-to-all-start.3 = ((bf16[32,8,2048]{2,1,0:T(8,128)(2,1)}), bf16[32,8,2048]{2,1,0:T(8,128)(2,1)S(1)}, u32[]{:S(2)}, u32[]{:S(2)}) async-start(bf16[32,8,2048]{2,1,0:T(8,128)(2,1)} %scale.1), calls=%async_computation.3 | async-start | bytes 2097152 | tf_op jit(solution)/shard_map/all_to_all | solution.py:90

commit v9 on v8

--- a/solution.py
+++ b/solution.py
@@ -126,14 +126,15 @@
     p0, got = together(p0, swap(sent, "zh"))
     rows_in = in_order(mine(squares_in), got[:, :tokens])
     rows_in = lax.all_gather(rows_in, "x", axis=0, tiled=False)
-    rows_in = rows_in.reshape(X, ZH, Y * C, 8, tokens).transpose(1, 2, 0, 3, 4).reshape(ZH, 256, tokens)
+    rows_in = rows_in.reshape(X, ZH, Y, C, 8, tokens).transpose(1, 3, 2, 0, 4, 5).reshape(ZH, 256, tokens)
     grad = in_order(mine(grad), got[:, tokens:].reshape(Y * C, 8, 512))
     grad = grad.reshape(ZH, Y, C, 8, 512).transpose(3, 1, 0, 2, 4).reshape(8, 8192)
     p3, p1, rows_in = together(around(p0, 1), around(p0, -1), rows_in)
     p2a, p2b, grad = together(around(p1[:4], -1), around(p3[4:], 1), grad)
 
-    partial = exchange(scale_part(rows_in, p0, p1, p2a, p2b, p3), ("y", "c", "x"))
-    rows = jnp.sum(partial.reshape(Y * C, X, 8, 2048).astype(f32), axis=0).reshape(X, 8, 4, 4, 128)
+    partial = exchange(scale_part(rows_in, p0, p1, p2a, p2b, p3).reshape(C, Y * X, 8, 2048), "c")
+    partial = exchange((partial[0].astype(f32) + partial[1].astype(f32)).astype(bf16), ("y", "x"))
+    rows = jnp.sum(partial.reshape(Y, X, 8, 2048).astype(f32), axis=0).reshape(X, 8, 4, 4, 128)
     rows = rows.transpose(1, 3, 2, 0, 4)
     odd, two = (ring % 2) == 1, ((ring // 2) % 2) == 1
     rows = jnp.where(odd, jnp.roll(rows, 1, axis=2), rows)

time: 268 us -> 266 us (level)
  blocking collectives: 105 us -> 122 us
  starting transfers between devices: 95.8 us -> 82.8 us
  waiting for transfers between devices: 54.3 us -> 49 us
    all_to_all x0 -> x1, blocking collectives: none -> 16.9 us  [exchange(): return lax.all_to_all(value, axis, split_axis=0, concat_axis=0, tiled=True)]
    all_to_all x4, starting transfers between devices: 33.1 us -> 20.1 us  [exchange(): return lax.all_to_all(value, axis, split_axis=0, concat_axis=0, tiled=True)]
    all_to_all x4, waiting for transfers between devices: 28.2 us -> 22.9 us  [exchange(): return lax.all_to_all(value, axis, split_axis=0, concat_axis=0, tiled=True)]
where the time goes in v9:
time: 266 us
  blocking collectives  122 us (46%)
  starting transfers between devices  82.8 us (31%)
  waiting for transfers between devices  49 us (18%)
  other arithmetic  5.86 us (2%)
  Pallas kernels  4.94 us (2%)
    ppermute x3, starting transfers between devices, swap(): return lax.ppermute(value, axis, [(0, 1), (1, 0)])  51 us
    all_gather x1, blocking collectives, per_device(): p0 = lax.all_gather(squares[0], ('zh', 'z8', 'z4'), axis=0, tiled=False)  49.7 us
    all_gather x1, blocking collectives, per_device(): lax.all_gather(jnp.stack([out_grads, activations]), ('z8', 'z4'), axis=0,...  45.5 us
    all_to_all x4, waiting for transfers between devices, exchange(): return lax.all_to_all(value, axis, split_axis=0, concat_axis=0, tiled=True)  22.9 us
    ppermute x3, waiting for transfers between devices, swap(): return lax.ppermute(value, axis, [(0, 1), (1, 0)])  20.7 us
    all_to_all x4, starting transfers between devices, exchange(): return lax.all_to_all(value, axis, split_axis=0, concat_axis=0, tiled=True)  20.1 us
    all_to_all x1, blocking collectives, exchange(): return lax.all_to_all(value, axis, split_axis=0, concat_axis=0, tiled=True)  16.9 us
    ppermute x4, starting transfers between devices, around(): return lax.ppermute(value, RING, [(i, (i + hops) % 32) for i in range(32)])  11.8 us
  transfers between devices with their start and end apart: 11, of which 7 were waited for; matrix products, arithmetic and copies ran while one was open for 0% of the time, Pallas kernels for 0%

profile of v9, /device:TPU:1, one launch (start us, length us, event | category | flops | bytes accessed | tf_op | source)
XLA Modules:
  0.0 265.6 jit_solution(17117780263922579818)
XLA Ops:
  0.0 3.8 %copy_bitcast_fusion = bf16[4,2,16,128,128]{4,3,2,1,0:T(8,128)(2,1)} fusion(bf16[1,16,4,128,128]{4,3,2,1,0:T(8,128)(2,1)} %bitcast.59, bf16[1,16,4,128,128]{4,3,2,1,0:T(8,128)(2,1)} %bitcast.60), kind=kLoop, calls=%fused_computation.1 | loop fusion | flops 2097152 | bytes 8388608 | tf_op jit(solution)/shard_map/transpose | solution.py:109
  3.8 5.0 %all-to-all-start = ((bf16[4,2,16,128,128]{4,3,2,1,0:T(8,128)(2,1)}), bf16[4,2,16,128,128]{4,3,2,1,0:T(8,128)(2,1)}, u32[]{:S(2)}, u32[]{:S(2)}) async-start(bf16[4,2,16,128,128]{4,3,2,1,0:T(8,128)(2,1)} %copy_bitcast_fusion), calls=%async_computation | async-start | bytes 8388608 | tf_op jit(solution)/shard_map/all_to_all | solution.py:90
  8.8 45.5 %all-gather = bf16[8,256,128]{2,1,0:T(8,128)(2,1)S(1)} all-gather(bf16[2,256,128]{2,1,0:T(8,128)(2,1)S(1)} %pad_maximum_fusion.2), channel_id=2, replica_groups=mesh['y'=4,'zh'=2,'c'=2,'z8'=2,'z4'=2,'z2'=2,'z1'=2,'x'=4] {'z8','z4'}, dimensions={0}, use_global_device_ids=true | all-gather | bytes 655360 | tf_op jit(solution)/shard_map/all_gather | solution.py:111
  54.3 14.6 %collective-permute-start = (bf16[4,2,256,128]{3,2,1,0:T(8,128)(2,1)S(1)}, bf16[4,2,256,128]{3,2,1,0:T(8,128)(2,1)S(1)}, u32[]{:S(2)}, u32[]{:S(2)}) collective-permute-start(bf16[4,2,256,128]{3,2,1,0:T(8,128)(2,1)S(1)} %bitcast.57), channel_id=1, source_target_pairs={{0,8},{8,0},{1,9},{9,1},{2,10},{10,2},{3,11},{11,3},{4,12},{12,4},... | collective-permute-start | bytes 1572872 | tf_op jit(solution)/shard_map/ppermute | solution.py:22
  69.0 11.1 %collective-permute-done = bf16[4,2,256,128]{3,2,1,0:T(8,128)(2,1)S(1)} collective-permute-done((bf16[4,2,256,128]{3,2,1,0:T(8,128)(2,1)S(1)}, bf16[4,2,256,128]{3,2,1,0:T(8,128)(2,1)S(1)}, u32[]{:S(2)}, u32[]{:S(2)}) %collective-permute-start) | collective-permute-done | bytes 524320 | tf_op jit(solution)/shard_map/ppermute | solution.py:22
  80.1 0.1 pad_maximum_fusion.1.near_ref
  80.2 14.9 %collective-permute-start.1 = (bf16[8,2,256,128]{3,2,1,0:T(8,128)(2,1)S(1)}, bf16[8,2,256,128]{3,2,1,0:T(8,128)(2,1)S(1)}, u32[]{:S(2)}, u32[]{:S(2)}) collective-permute-start(bf16[8,2,256,128]{3,2,1,0:T(8,128)(2,1)S(1)} %pad_maximum_fusion.1.near_ref), channel_id=1, source_target_pairs={{0,4},{4,0},{1,5},{5,1},{2,6},{6,2},{3,7},{7,3},{8,12},{12,8},{9,1... | collective-permute-start | bytes 3145736 | tf_op jit(solution)/shard_map/ppermute | solution.py:22
  95.0 0.7 copy.36
  95.7 6.3 %all-to-all-start.1 = ((bf16[8,2,8,512]{3,2,1,0:T(8,128)(2,1)}), bf16[8,2,8,512]{3,2,1,0:T(8,128)(2,1)S(1)}, u32[]{:S(2)}, u32[]{:S(2)}) async-start(bf16[8,2,8,512]{3,2,1,0:T(8,128)(2,1)} %bitcast.9), calls=%async_computation.1 | async-start | bytes 262144 | tf_op jit(solution)/shard_map/all_to_all | solution.py:90
  102.0 5.3 %all-to-all-done.1 = bf16[8,2,8,512]{3,2,1,0:T(8,128)(2,1)S(1)} async-done(((bf16[8,2,8,512]{3,2,1,0:T(8,128)(2,1)}), bf16[8,2,8,512]{3,2,1,0:T(8,128)(2,1)S(1)}, u32[]{:S(2)}, u32[]{:S(2)}) %all-to-all-start.1) | async-done | bytes 131104 | tf_op jit(solution)/shard_map/all_to_all | solution.py:90
  107.3 9.6 %collective-permute-done.1.far_ref = bf16[8,2,256,128]{3,2,1,0:T(8,128)(2,1)S(1)} collective-permute-done((bf16[8,2,256,128]{3,2,1,0:T(8,128)(2,1)S(1)}, bf16[8,2,256,128]{3,2,1,0:T(8,128)(2,1)S(1)}, u32[]{:S(2)}, u32[]{:S(2)}) %collective-permute-start.1) | collective-permute-done | bytes 1048608 | tf_op jit(solution)/shard_map/ppermute | solution.py:22
  116.9 4.2 %project.1 = bf16[4,2,256,128]{3,2,1,0:T(8,128)(2,1)} custom-call(s32[1]{0:T(128)} %bitcast.z_ref, bf16[8,2,256,128]{3,2,1,0:T(8,128)(2,1)S(1)} %pad_maximum_fusion.1.near_ref, bf16[8,2,256,128]{3,2,1,0:T(8,128)(2,1)S(1)} %collective-permute-done.1.far_ref, bf16[4,2,16,128,128]{4,3,2,1,0:T(8,128)(2,1)} %all-to-all-done.basis_ref), custom_call_target="tpu_custom_call" | custom-call | flops 1073741824 | bytes 6800000 | tf_op jit(solution)/shard_map/project/pallas_call | solution.py:50
  121.1 3.5 %all-to-all-start.2 = ((bf16[4,2,256,128]{3,2,1,0:T(8,128)(2,1)}), bf16[4,2,256,128]{3,2,1,0:T(8,128)(2,1)S(1)}, u32[]{:S(2)}, u32[]{:S(2)}) async-start(bf16[4,2,256,128]{3,2,1,0:T(8,128)(2,1)} %project.1), calls=%async_computation.2 | async-start | bytes 1048576 | tf_op jit(solution)/shard_map/all_to_all | solution.py:90
  124.6 6.9 %all-to-all-done.2 = bf16[4,2,256,128]{3,2,1,0:T(8,128)(2,1)S(1)} async-done(((bf16[4,2,256,128]{3,2,1,0:T(8,128)(2,1)}), bf16[4,2,256,128]{3,2,1,0:T(8,128)(2,1)S(1)}, u32[]{:S(2)}, u32[]{:S(2)}) %all-to-all-start.2) | async-done | bytes 524320 | tf_op jit(solution)/shard_map/all_to_all | solution.py:90
  131.5 0.1 convert_reduce_fusion.1
  131.6 0.1 copy.37
  131.8 21.5 %collective-permute-start.2 = (bf16[64,768]{1,0:T(8,128)(2,1)S(1)}, bf16[64,768]{1,0:T(8,128)(2,1)S(1)}, u32[]{:S(2)}, u32[]{:S(2)}) collective-permute-start(bf16[64,768]{1,0:T(8,128)(2,1)S(1)} %pad_maximum_fusion.3), channel_id=1, source_target_pairs={{0,128},{128,0},{1,129},{129,1},{2,130},{130,2},{3,131},{131,3},{4... | collective-permute-start | bytes 294920 | tf_op jit(solution)/shard_map/ppermute | solution.py:22
  153.3 49.7 %all_gather.17.p0 = bf16[8,256,128]{2,1,0:T(8,128)(2,1)S(1)} all-gather(bf16[1,256,128]{2,1,0:T(8,128)(2,1)S(1)} %get-tuple-element.40), channel_id=1, replica_groups=mesh['y'=4,'zh'=2,'c'=2,'z8'=2,'z4'=2,'z2'=2,'z1'=2,'x'=4] {'zh','z8','z4'}, dimensions={0}, use_global_device_ids=true | all-gather | bytes 589824 | tf_op jit(solution)/shard_map/all_gather | solution.py:125
  203.0 1.9 collective-permute-start.4
  204.9 3.4 %collective-permute-start.3 = (bf16[8,256,128]{2,1,0:T(8,128)(2,1)S(1)}, bf16[8,256,128]{2,1,0:T(8,128)(2,1)S(1)}, u32[]{:S(2)}, u32[]{:S(2)}) collective-permute-start(bf16[8,256,128]{2,1,0:T(8,128)(2,1)S(1)} %all_gather.17.p0), channel_id=1, source_target_pairs={{0,4},{4,8},{8,12},{12,16},{16,20},{20,24},{24,28},{28,32},{32,36}... | collective-permute-start | bytes 1572872 | tf_op jit(solution)/shard_map/ppermute | solution.py:26
  208.3 9.7 %all-gather.1 = bf16[8,64,256]{2,1,0:T(8,128)(2,1)S(1)} all-gather(bf16[2,64,256]{2,1,0:T(8,128)(2,1)S(1)} %pad_maximum_fusion.4), channel_id=3, replica_groups=mesh['y'=4,'zh'=2,'c'=2,'z8'=2,'z4'=2,'z2'=2,'z1'=2,'x'=4] {'x'}, dimensions={0}, use_global_device_ids=true | all-gather | bytes 327680 | tf_op jit(solution)/shard_map/all_gather | solution.py:128
  218.0 3.0 %collective-permute-start.6 = (bf16[4,256,128]{2,1,0:T(8,128)(2,1)S(1)}, bf16[4,256,128]{2,1,0:T(8,128)(2,1)S(1)}, u32[]{:S(2)}, u32[]{:S(2)}) collective-permute-start(bf16[4,256,128]{2,1,0:T(8,128)(2,1)S(1)} %slice.66), channel_id=1, source_target_pairs={{0,4},{4,8},{8,12},{12,16},{16,20},{20,24},{24,28},{28,32},{32,36}... | collective-permute-start | bytes 786440 | tf_op jit(solution)/shard_map/ppermute | solution.py:26
  221.1 3.5 %collective-permute-start.5 = (bf16[4,256,128]{2,1,0:T(8,128)(2,1)S(1)}, bf16[4,256,128]{2,1,0:T(8,128)(2,1)S(1)}, u32[]{:S(2)}, u32[]{:S(2)}) collective-permute-start(bf16[4,256,128]{2,1,0:T(8,128)(2,1)S(1)} %slice.65), channel_id=1, source_target_pairs={{0,188},{4,0},{8,4},{12,8},{16,12},{20,16},{24,20},{28,24},{32,28}... | collective-permute-start | bytes 786440 | tf_op jit(solution)/shard_map/ppermute | solution.py:26
  224.6 4.9 %collective-permute-done.6.p2b = bf16[4,256,128]{2,1,0:T(8,128)(2,1)S(1)} collective-permute-done((bf16[4,256,128]{2,1,0:T(8,128)(2,1)S(1)}, bf16[4,256,128]{2,1,0:T(8,128)(2,1)S(1)}, u32[]{:S(2)}, u32[]{:S(2)}) %collective-permute-start.6) | collective-permute-done | bytes 262176 | tf_op jit(solution)/shard_map/ppermute | solution.py:26
  229.5 0.6 collective-permute-done.5.p2a
  230.1 0.7 scale.1
  230.8 16.9 %all_to_all.25 = bf16[2,16,8,2048]{3,2,1,0:T(8,128)(2,1)S(1)} all-to-all(bf16[2,16,8,2048]{3,2,1,0:T(8,128)(2,1)S(1)} %bitcast.51), channel_id=1, replica_groups=mesh['y'=4,'zh'=2,'c'=2,'z8'=2,'z4'=2,'z2'=2,'z1'=2,'x'=4] {'c'}, dimensions={0} | all-to-all | bytes 2097152 | tf_op jit(solution)/shard_map/all_to_all | solution.py:90
  247.7 0.9 fusion
  248.6 5.2 %all-to-all-start.4 = ((bf16[16,8,2048]{2,1,0:T(8,128)(2,1)}), bf16[16,8,2048]{2,1,0:T(8,128)(2,1)S(1)}, u32[]{:S(2)}, u32[]{:S(2)}) async-start(bf16[16,8,2048]{2,1,0:T(8,128)(2,1)} %fusion), calls=%async_computation.4 | async-start | bytes 1048576 | tf_op jit(solution)/shard_map/all_to_all | solution.py:90
  253.9 10.7 %all-to-all-done.4 = bf16[16,8,2048]{2,1,0:T(8,128)(2,1)S(1)} async-done(((bf16[16,8,2048]{2,1,0:T(8,128)(2,1)}), bf16[16,8,2048]{2,1,0:T(8,128)(2,1)S(1)}, u32[]{:S(2)}, u32[]{:S(2)}) %all-to-all-start.4) | async-done | bytes 524320 | tf_op jit(solution)/shard_map/all_to_all | solution.py:90
  264.6 0.1 convert_reduce_fusion
  264.9 0.7 divide_convert_fusion
  (30 shorter events, 0.4 us)
Async XLA Ops:
  3.8 5.0 %copy-start.1 = (bf16[256,128]{1,0:T(8,128)(2,1)S(1)}, bf16[256,128]{1,0:T(8,128)(2,1)}, u32[]{:S(2)}) copy-start(bf16[256,128]{1,0:T(8,128)(2,1)} %param.5) | copy-start | bytes 196612
  3.8 5.0 %copy-start.2 = (bf16[256,128]{1,0:T(8,128)(2,1)S(1)}, bf16[256,128]{1,0:T(8,128)(2,1)}, u32[]{:S(2)}) copy-start(bf16[256,128]{1,0:T(8,128)(2,1)} %param.6) | copy-start | bytes 196612
  3.8 91.2 %copy-start = (bf16[128,512]{1,0:T(8,128)(2,1)S(1)}, bf16[128,512]{1,0:T(8,128)(2,1)}, u32[]{:S(2)}) copy-start(bf16[128,512]{1,0:T(8,128)(2,1)} %param.9) | copy-start | bytes 393220
  3.8 76.4 %all-to-all-start = ((bf16[4,2,16,128,128]{4,3,2,1,0:T(8,128)(2,1)}), bf16[4,2,16,128,128]{4,3,2,1,0:T(8,128)(2,1)}, u32[]{:S(2)}, u32[]{:S(2)}) async-start(bf16[4,2,16,128,128]{4,3,2,1,0:T(8,128)(2,1)} %copy_bitcast_fusion), calls=%async_computation | async-start | bytes 8388608 | tf_op jit(solution)/shard_map/all_to_all | solution.py:90
  54.3 25.7 %collective-permute-start = (bf16[4,2,256,128]{3,2,1,0:T(8,128)(2,1)S(1)}, bf16[4,2,256,128]{3,2,1,0:T(8,128)(2,1)S(1)}, u32[]{:S(2)}, u32[]{:S(2)}) collective-permute-start(bf16[4,2,256,128]{3,2,1,0:T(8,128)(2,1)S(1)} %bitcast.57), channel_id=1, source_target_pairs={{0,8},{8,0},{1,9},{9,1},{2,10},{10,2},{3,11},{11,3},{4,12},{12,4},... | collective-permute-start | bytes 1572872 | tf_op jit(solution)/shard_map/ppermute | solution.py:22
  80.2 36.7 %collective-permute-start.1 = (bf16[8,2,256,128]{3,2,1,0:T(8,128)(2,1)S(1)}, bf16[8,2,256,128]{3,2,1,0:T(8,128)(2,1)S(1)}, u32[]{:S(2)}, u32[]{:S(2)}) collective-permute-start(bf16[8,2,256,128]{3,2,1,0:T(8,128)(2,1)S(1)} %pad_maximum_fusion.1.near_ref), channel_id=1, source_target_pairs={{0,4},{4,0},{1,5},{5,1},{2,6},{6,2},{3,7},{7,3},{8,12},{12,8},{9,1... | collective-permute-start | bytes 3145736 | tf_op jit(solution)/shard_map/ppermute | solution.py:22
  95.7 11.6 %all-to-all-start.1 = ((bf16[8,2,8,512]{3,2,1,0:T(8,128)(2,1)}), bf16[8,2,8,512]{3,2,1,0:T(8,128)(2,1)S(1)}, u32[]{:S(2)}, u32[]{:S(2)}) async-start(bf16[8,2,8,512]{3,2,1,0:T(8,128)(2,1)} %bitcast.9), calls=%async_computation.1 | async-start | bytes 262144 | tf_op jit(solution)/shard_map/all_to_all | solution.py:90
  121.1 10.4 %all-to-all-start.2 = ((bf16[4,2,256,128]{3,2,1,0:T(8,128)(2,1)}), bf16[4,2,256,128]{3,2,1,0:T(8,128)(2,1)S(1)}, u32[]{:S(2)}, u32[]{:S(2)}) async-start(bf16[4,2,256,128]{3,2,1,0:T(8,128)(2,1)} %project.1), calls=%async_computation.2 | async-start | bytes 1048576 | tf_op jit(solution)/shard_map/all_to_all | solution.py:90
  131.8 71.2 %collective-permute-start.2 = (bf16[64,768]{1,0:T(8,128)(2,1)S(1)}, bf16[64,768]{1,0:T(8,128)(2,1)S(1)}, u32[]{:S(2)}, u32[]{:S(2)}) collective-permute-start(bf16[64,768]{1,0:T(8,128)(2,1)S(1)} %pad_maximum_fusion.3), channel_id=1, source_target_pairs={{0,128},{128,0},{1,129},{129,1},{2,130},{130,2},{3,131},{131,3},{4... | collective-permute-start | bytes 294920 | tf_op jit(solution)/shard_map/ppermute | solution.py:22
  203.0 15.0 %collective-permute-start.4 = (bf16[8,256,128]{2,1,0:T(8,128)(2,1)S(1)}, bf16[8,256,128]{2,1,0:T(8,128)(2,1)S(1)}, u32[]{:S(2)}, u32[]{:S(2)}) collective-permute-start(bf16[8,256,128]{2,1,0:T(8,128)(2,1)S(1)} %all_gather.17.p0), channel_id=1, source_target_pairs={{0,188},{4,0},{8,4},{12,8},{16,12},{20,16},{24,20},{28,24},{32,28}... | collective-permute-start | bytes 1572872 | tf_op jit(solution)/shard_map/ppermute | solution.py:26
  204.9 13.1 %collective-permute-start.3 = (bf16[8,256,128]{2,1,0:T(8,128)(2,1)S(1)}, bf16[8,256,128]{2,1,0:T(8,128)(2,1)S(1)}, u32[]{:S(2)}, u32[]{:S(2)}) collective-permute-start(bf16[8,256,128]{2,1,0:T(8,128)(2,1)S(1)} %all_gather.17.p0), channel_id=1, source_target_pairs={{0,4},{4,8},{8,12},{12,16},{16,20},{20,24},{24,28},{28,32},{32,36}... | collective-permute-start | bytes 1572872 | tf_op jit(solution)/shard_map/ppermute | solution.py:26
  218.0 11.5 %collective-permute-start.6 = (bf16[4,256,128]{2,1,0:T(8,128)(2,1)S(1)}, bf16[4,256,128]{2,1,0:T(8,128)(2,1)S(1)}, u32[]{:S(2)}, u32[]{:S(2)}) collective-permute-start(bf16[4,256,128]{2,1,0:T(8,128)(2,1)S(1)} %slice.66), channel_id=1, source_target_pairs={{0,4},{4,8},{8,12},{12,16},{16,20},{20,24},{24,28},{28,32},{32,36}... | collective-permute-start | bytes 786440 | tf_op jit(solution)/shard_map/ppermute | solution.py:26
  221.1 9.0 %collective-permute-start.5 = (bf16[4,256,128]{2,1,0:T(8,128)(2,1)S(1)}, bf16[4,256,128]{2,1,0:T(8,128)(2,1)S(1)}, u32[]{:S(2)}, u32[]{:S(2)}) collective-permute-start(bf16[4,256,128]{2,1,0:T(8,128)(2,1)S(1)} %slice.65), channel_id=1, source_target_pairs={{0,188},{4,0},{8,4},{12,8},{16,12},{20,16},{24,20},{28,24},{32,28}... | collective-permute-start | bytes 786440 | tf_op jit(solution)/shard_map/ppermute | solution.py:26
  248.6 16.0 %all-to-all-start.4 = ((bf16[16,8,2048]{2,1,0:T(8,128)(2,1)}), bf16[16,8,2048]{2,1,0:T(8,128)(2,1)S(1)}, u32[]{:S(2)}, u32[]{:S(2)}) async-start(bf16[16,8,2048]{2,1,0:T(8,128)(2,1)} %fusion), calls=%async_computation.4 | async-start | bytes 1048576 | tf_op jit(solution)/shard_map/all_to_all | solution.py:90

commit v10 on v9

--- a/solution.py
+++ b/solution.py
@@ -26,19 +26,16 @@
     return lax.ppermute(value, RING, [(i, (i + hops) % 32) for i in range(32)])
 
 
-def project_kernel(z_ref, near_ref, far_ref, basis_ref, out_ref):
-    residue = lax.rem(z_ref[0], 4)
+def project_kernel(blocks_ref, basis_ref, out_ref):
     for m in range(2):
         for pair in range(2):
             total = jnp.zeros((256, 256), f32)
             for step in range(8):
-                source = near_ref if step < 4 else far_ref
-                at = 2 * (step % 4)
-                left = jnp.concatenate([source[at, m], source[at + 1, m]], axis=1)
-                z0 = 4 * (at % 4) + (residue ^ (2 * (at // 4) + step // 4))
-                z1 = z0 + 4
+                residue, at = step // 2, 2 * (step % 2)
+                left = jnp.concatenate([blocks_ref[residue, at, m], blocks_ref[residue, at + 1, m]], axis=1)
+                z = 4 * at + residue
                 columns = [
-                    jnp.concatenate([basis_ref[2 * pair + i, m, z0], basis_ref[2 * pair + i, m, z1]], axis=0) for i in range(2)
+                    jnp.concatenate([basis_ref[2 * pair + i, m, z], basis_ref[2 * pair + i, m, z + 4]], axis=0) for i in range(2)
                 ]
                 right = jnp.concatenate(columns, axis=1)
                 total = total + jnp.dot(left, right, preferred_element_type=f32)
@@ -46,16 +43,16 @@
             out_ref[2 * pair + 1, m] = total[:, 128:].astype(bf16)
 
 
-def project(z, near, far, basis):
+def project(blocks, basis):
     return pl.pallas_call(
         project_kernel,
         out_shape=jax.ShapeDtypeStruct((X, 2, 256, 128), bf16),
-        in_specs=[SCALAR] + [WHOLE] * 3,
+        in_specs=[WHOLE] * 2,
         out_specs=WHOLE,
         compiler_params=PARAMS,
         cost_estimate=pl.CostEstimate(flops=4 * 256 * 2048 * 512, bytes_accessed=6800000, transcendentals=0),
         name="project",
-    )(z, near, far, basis)
+    )(blocks, basis)
 
 
 def scale_kernel(rows_ref, p0, p1, p2a, p2b, p3, out_ref):
@@ -93,7 +90,6 @@
 def per_device(activations, out_grads, basis_in, basis_out, grad_eigen):
     tokens = activations.shape[0]
     ring = lax.axis_index(RING)
-    z = (ring % 16).astype(jnp.int32).reshape(1)
     high = lax.axis_index("zh") == 1
 
     def mine(halves):
@@ -109,14 +105,11 @@
     bases = exchange(bases.transpose(2, 0, 1, 3, 4), "x")
 
     have = lax.all_gather(jnp.stack([out_grads, activations]), ("z8", "z4"), axis=0, tiled=False)
-    have = jnp.concatenate([have, swap(have, "z2")], axis=0)
-    have, bases, grad_eigen = together(have, bases, grad_eigen)
-    grad = grad_eigen.reshape(Y, ZH, C, 8, 512).transpose(0, 2, 1, 3, 4).reshape(Y * C, ZH, 8, 512)
-    grad = exchange(grad, ("y", "c"))
-    far, have, grad = together(swap(have, "z1"), have, grad)
-    grad = grad.transpose(1, 0, 2, 3)
+    have, bases = together(have, bases)
+    have = exchange(jnp.broadcast_to(have[None], (4,) + have.shape), ("z2", "z1"))
+    grad = grad_eigen.reshape(Y, ZH, C, 8, 512).transpose(1, 0, 2, 3, 4)
 
-    part = project(z, have, far, bases)
+    part = project(have, bases)
     projected = jnp.sum(exchange(part, "x").astype(f32), axis=0)
     squares = (projected * projected).astype(bf16)
     squares_in = squares[1].T.reshape(Y, ZH, C * 8, tokens).transpose(1, 0, 2, 3).reshape(ZH, 64, tokens)
@@ -127,8 +120,8 @@
     rows_in = in_order(mine(squares_in), got[:, :tokens])
     rows_in = lax.all_gather(rows_in, "x", axis=0, tiled=False)
     rows_in = rows_in.reshape(X, ZH, Y, C, 8, tokens).transpose(1, 3, 2, 0, 4, 5).reshape(ZH, 256, tokens)
-    grad = in_order(mine(grad), got[:, tokens:].reshape(Y * C, 8, 512))
-    grad = grad.reshape(ZH, Y, C, 8, 512).transpose(3, 1, 0, 2, 4).reshape(8, 8192)
+    grad = in_order(mine(grad), got[:, tokens:].reshape(Y, C, 8, 512)).transpose(1, 2, 0, 3, 4).reshape(Y * C, ZH, 8, 512)
+    grad = exchange(grad, ("y", "c")).reshape(Y, C, ZH, 8, 512).transpose(3, 0, 2, 1, 4).reshape(8, 8192)
     p3, p1, rows_in = together(around(p0, 1), around(p0, -1), rows_in)
     p2a, p2b, grad = together(around(p1[:4], -1), around(p3[4:], 1), grad)
 

time: 266 us -> 274 us (1.030)
  blocking collectives: 122 us -> 199 us
  starting transfers between devices: 82.8 us -> 42.8 us
  waiting for transfers between devices: 49 us -> 19.3 us
    all_to_all x1 -> x3, blocking collectives: 16.9 us -> 91.3 us  [exchange(): return lax.all_to_all(value, axis, split_axis=0, concat_axis=0, tiled=True)]
    ppermute x3 -> x1, starting transfers between devices: 51 us -> 8.46 us  [swap(): return lax.ppermute(value, axis, [(0, 1), (1, 0)])]
    ppermute x3 -> x1, waiting for transfers between devices: 20.7 us -> 0.01 us  [swap(): return lax.ppermute(value, axis, [(0, 1), (1, 0)])]
    ppermute x4, starting transfers between devices: 11.8 us -> 21.1 us  [around(): return lax.ppermute(value, RING, [(i, (i + hops) % 32) for i in range(32)])]
    all_to_all x4 -> x3, starting transfers between devices: 20.1 us -> 13.2 us  [exchange(): return lax.all_to_all(value, axis, split_axis=0, concat_axis=0, tiled=True)]
    all_to_all x4 -> x3, waiting for transfers between devices: 22.9 us -> 17.8 us  [exchange(): return lax.all_to_all(value, axis, split_axis=0, concat_axis=0, tiled=True)]
    ppermute x4, waiting for transfers between devices: 5.49 us -> 1.56 us  [around(): return lax.ppermute(value, RING, [(i, (i + hops) % 32) for i in range(32)])]
  transfers between devices with their start and end apart: 11 -> 8, of which waited for: 7 -> 3; matrix products, arithmetic and copies ran while one was open for 0% -> 0% of each run, Pallas kernels for 0% -> 0%
where the time goes in v10:
time: 274 us; the launch traced here: 273 us
  blocking collectives  199 us (73%)
  starting transfers between devices  42.8 us (16%)
  waiting for transfers between devices  19.3 us (7%)
  other arithmetic  5.76 us (2%)
  Pallas kernels  4.97 us (2%)
    all_to_all x3, blocking collectives, exchange(): return lax.all_to_all(value, axis, split_axis=0, concat_axis=0, tiled=True)  91.3 us
    all_gather x1, blocking collectives, per_device(): p0 = lax.all_gather(squares[0], ('zh', 'z8', 'z4'), axis=0, tiled=False)  52.3 us
    all_gather x1, blocking collectives, per_device(): lax.all_gather(jnp.stack([out_grads, activations]), ('z8', 'z4'), axis=0,...  45.5 us
    ppermute x4, starting transfers between devices, around(): return lax.ppermute(value, RING, [(i, (i + hops) % 32) for i in range(32)])  21.1 us
    all_to_all x3, waiting for transfers between devices, exchange(): return lax.all_to_all(value, axis, split_axis=0, concat_axis=0, tiled=True)  17.8 us
    all_to_all x3, starting transfers between devices, exchange(): return lax.all_to_all(value, axis, split_axis=0, concat_axis=0, tiled=True)  13.2 us
    all_gather x1, blocking collectives, per_device(): rows_in = lax.all_gather(rows_in, 'x', axis=0, tiled=False)  9.74 us
    ppermute x1, starting transfers between devices, swap(): return lax.ppermute(value, axis, [(0, 1), (1, 0)])  8.46 us
  transfers between devices with their start and end apart: 8, of which 3 were waited for; matrix products, arithmetic and copies ran while one was open for 0% of the time, Pallas kernels for 0%

profile of v10, /device:TPU:1, one launch (start us, length us, event | category | flops | bytes accessed | tf_op | source)
XLA Modules:
  0.0 273.0 jit_solution(14235467347653770085)
XLA Ops:
  0.0 3.8 %copy_bitcast_fusion = bf16[4,2,16,128,128]{4,3,2,1,0:T(8,128)(2,1)} fusion(bf16[1,16,4,128,128]{4,3,2,1,0:T(8,128)(2,1)} %bitcast.51, bf16[1,16,4,128,128]{4,3,2,1,0:T(8,128)(2,1)} %bitcast.52), kind=kLoop, calls=%fused_computation.1 | loop fusion | flops 2097152 | bytes 8388608 | tf_op jit(solution)/shard_map/transpose | solution.py:105
  3.8 5.0 %all-to-all-start = ((bf16[4,2,16,128,128]{4,3,2,1,0:T(8,128)(2,1)}), bf16[4,2,16,128,128]{4,3,2,1,0:T(8,128)(2,1)}, u32[]{:S(2)}, u32[]{:S(2)}) async-start(bf16[4,2,16,128,128]{4,3,2,1,0:T(8,128)(2,1)} %copy_bitcast_fusion), calls=%async_computation | async-start | bytes 8388608 | tf_op jit(solution)/shard_map/all_to_all | solution.py:87
  8.8 45.5 %all-gather = bf16[8,256,128]{2,1,0:T(8,128)(2,1)S(1)} all-gather(bf16[2,256,128]{2,1,0:T(8,128)(2,1)S(1)} %pad_maximum_fusion.1), channel_id=2, replica_groups=mesh['y'=4,'zh'=2,'c'=2,'z8'=2,'z4'=2,'z2'=2,'z1'=2,'x'=4] {'z8','z4'}, dimensions={0}, use_global_device_ids=true | all-gather | bytes 655360 | tf_op jit(solution)/shard_map/all_gather | solution.py:107
  54.3 0.0 all-to-all-done.basis_ref
  54.3 0.5 broadcast_in_dim.2
  54.8 73.6 %all_to_all.30.blocks_ref = bf16[4,4,2,256,128]{4,3,2,1,0:T(8,128)(2,1)S(1)} all-to-all(bf16[4,4,2,256,128]{4,3,2,1,0:T(8,128)(2,1)S(1)} %broadcast_in_dim.2), channel_id=1, replica_groups=mesh['y'=4,'zh'=2,'c'=2,'z8'=2,'z4'=2,'z2'=2,'z1'=2,'x'=4] {'z2','z1'}, dimensions={0} | all-to-all | bytes 4194304 | tf_op jit(solution)/shard_map/all_to_all | solution.py:87
  128.3 4.3 %project.1 = bf16[4,2,256,128]{3,2,1,0:T(8,128)(2,1)} custom-call(bf16[4,4,2,256,128]{4,3,2,1,0:T(8,128)(2,1)S(1)} %all_to_all.30.blocks_ref, bf16[4,2,16,128,128]{4,3,2,1,0:T(8,128)(2,1)} %all-to-all-done.basis_ref), custom_call_target="tpu_custom_call" | custom-call | flops 1073741824 | bytes 6800000 | tf_op jit(solution)/shard_map/project/pallas_call | solution.py:47
  132.6 4.3 %all-to-all-start.2 = ((bf16[4,2,256,128]{3,2,1,0:T(8,128)(2,1)}), bf16[4,2,256,128]{3,2,1,0:T(8,128)(2,1)S(1)}, u32[]{:S(2)}, u32[]{:S(2)}) async-start(bf16[4,2,256,128]{3,2,1,0:T(8,128)(2,1)} %project.1), calls=%async_computation.2 | async-start | bytes 1048576 | tf_op jit(solution)/shard_map/all_to_all | solution.py:87
  136.9 7.1 %all-to-all-done.2 = bf16[4,2,256,128]{3,2,1,0:T(8,128)(2,1)S(1)} async-done(((bf16[4,2,256,128]{3,2,1,0:T(8,128)(2,1)}), bf16[4,2,256,128]{3,2,1,0:T(8,128)(2,1)S(1)}, u32[]{:S(2)}, u32[]{:S(2)}) %all-to-all-start.2) | async-done | bytes 524320 | tf_op jit(solution)/shard_map/all_to_all | solution.py:87
  144.0 0.1 convert_reduce_fusion.1
  144.1 0.1 copy.30
  144.3 8.5 %collective-permute-start = (bf16[64,768]{1,0:T(8,128)(2,1)S(1)}, bf16[64,768]{1,0:T(8,128)(2,1)S(1)}, u32[]{:S(2)}, u32[]{:S(2)}) collective-permute-start(bf16[64,768]{1,0:T(8,128)(2,1)S(1)} %pad_maximum_fusion.2), channel_id=1, source_target_pairs={{0,128},{128,0},{1,129},{129,1},{2,130},{130,2},{3,131},{131,3},{4... | collective-permute-start | bytes 294920 | tf_op jit(solution)/shard_map/ppermute | solution.py:22
  152.7 52.3 %all_gather.17.p0 = bf16[8,256,128]{2,1,0:T(8,128)(2,1)S(1)} all-gather(bf16[1,256,128]{2,1,0:T(8,128)(2,1)S(1)} %get-tuple-element.32), channel_id=1, replica_groups=mesh['y'=4,'zh'=2,'c'=2,'z8'=2,'z4'=2,'z2'=2,'z1'=2,'x'=4] {'zh','z8','z4'}, dimensions={0}, use_global_device_ids=true | all-gather | bytes 589824 | tf_op jit(solution)/shard_map/all_gather | solution.py:118
  205.0 0.0 collective-permute-done
  205.0 13.9 %collective-permute-start.1 = (bf16[8,256,128]{2,1,0:T(8,128)(2,1)S(1)}, bf16[8,256,128]{2,1,0:T(8,128)(2,1)S(1)}, u32[]{:S(2)}, u32[]{:S(2)}) collective-permute-start(bf16[8,256,128]{2,1,0:T(8,128)(2,1)S(1)} %all_gather.17.p0), channel_id=1, source_target_pairs={{0,4},{4,8},{8,12},{12,16},{16,20},{20,24},{24,28},{28,32},{32,36}... | collective-permute-start | bytes 1572872 | tf_op jit(solution)/shard_map/ppermute | solution.py:26
  218.9 1.9 collective-permute-start.2
  220.9 9.7 %all-gather.1 = bf16[8,64,256]{2,1,0:T(8,128)(2,1)S(1)} all-gather(bf16[2,64,256]{2,1,0:T(8,128)(2,1)S(1)} %pad_maximum_fusion.3), channel_id=3, replica_groups=mesh['y'=4,'zh'=2,'c'=2,'z8'=2,'z4'=2,'z2'=2,'z1'=2,'x'=4] {'x'}, dimensions={0}, use_global_device_ids=true | all-gather | bytes 327680 | tf_op jit(solution)/shard_map/all_gather | solution.py:121
  230.7 1.6 collective-permute-done.2.p1
  232.3 3.4 %collective-permute-start.3 = (bf16[4,256,128]{2,1,0:T(8,128)(2,1)S(1)}, bf16[4,256,128]{2,1,0:T(8,128)(2,1)S(1)}, u32[]{:S(2)}, u32[]{:S(2)}) collective-permute-start(bf16[4,256,128]{2,1,0:T(8,128)(2,1)S(1)} %slice.65), channel_id=1, source_target_pairs={{0,188},{4,0},{8,4},{12,8},{16,12},{20,16},{24,20},{28,24},{32,28}... | collective-permute-start | bytes 786440 | tf_op jit(solution)/shard_map/ppermute | solution.py:26
  235.7 1.9 collective-permute-start.4
  237.7 12.7 %all_to_all.31 = bf16[8,2,8,512]{3,2,1,0:T(8,128)(2,1)S(1)} all-to-all(bf16[8,2,8,512]{3,2,1,0:T(8,128)(2,1)S(1)} %bitcast.57), channel_id=1, replica_groups=mesh['y'=4,'zh'=2,'c'=2,'z8'=2,'z4'=2,'z2'=2,'z1'=2,'x'=4] {'y','c'}, dimensions={0} | all-to-all | bytes 262144 | tf_op jit(solution)/shard_map/all_to_all | solution.py:87
  250.4 0.1 copy.33
  250.5 0.1 reshape.66
  250.6 0.0 collective-permute-done.3.p2a
  250.6 0.0 collective-permute-done.4.p2b
  250.6 0.7 scale.1
  251.4 5.1 %all_to_all.32 = bf16[2,16,8,2048]{3,2,1,0:T(8,128)(2,1)S(1)} all-to-all(bf16[2,16,8,2048]{3,2,1,0:T(8,128)(2,1)S(1)} %bitcast.44), channel_id=1, replica_groups=mesh['y'=4,'zh'=2,'c'=2,'z8'=2,'z4'=2,'z2'=2,'z1'=2,'x'=4] {'c'}, dimensions={0} | all-to-all | bytes 2097152 | tf_op jit(solution)/shard_map/all_to_all | solution.py:87
  256.4 0.9 fusion
  257.4 3.9 %all-to-all-start.5 = ((bf16[16,8,2048]{2,1,0:T(8,128)(2,1)}), bf16[16,8,2048]{2,1,0:T(8,128)(2,1)S(1)}, u32[]{:S(2)}, u32[]{:S(2)}) async-start(bf16[16,8,2048]{2,1,0:T(8,128)(2,1)} %fusion), calls=%async_computation.5 | async-start | bytes 1048576 | tf_op jit(solution)/shard_map/all_to_all | solution.py:87
  261.3 10.7 %all-to-all-done.5 = bf16[16,8,2048]{2,1,0:T(8,128)(2,1)S(1)} async-done(((bf16[16,8,2048]{2,1,0:T(8,128)(2,1)}), bf16[16,8,2048]{2,1,0:T(8,128)(2,1)S(1)}, u32[]{:S(2)}, u32[]{:S(2)}) %all-to-all-start.5) | async-done | bytes 524320 | tf_op jit(solution)/shard_map/all_to_all | solution.py:87
  272.0 0.1 convert_reduce_fusion
  272.3 0.7 divide_convert_fusion
  (28 shorter events, 0.4 us)
Async XLA Ops:
  3.8 5.0 %copy-start.1 = (bf16[256,128]{1,0:T(8,128)(2,1)S(1)}, bf16[256,128]{1,0:T(8,128)(2,1)}, u32[]{:S(2)}) copy-start(bf16[256,128]{1,0:T(8,128)(2,1)} %param.5) | copy-start | bytes 196612
  3.8 5.0 %copy-start.2 = (bf16[256,128]{1,0:T(8,128)(2,1)S(1)}, bf16[256,128]{1,0:T(8,128)(2,1)}, u32[]{:S(2)}) copy-start(bf16[256,128]{1,0:T(8,128)(2,1)} %param.6) | copy-start | bytes 196612
  3.8 50.5 %all-to-all-start = ((bf16[4,2,16,128,128]{4,3,2,1,0:T(8,128)(2,1)}), bf16[4,2,16,128,128]{4,3,2,1,0:T(8,128)(2,1)}, u32[]{:S(2)}, u32[]{:S(2)}) async-start(bf16[4,2,16,128,128]{4,3,2,1,0:T(8,128)(2,1)} %copy_bitcast_fusion), calls=%async_computation | async-start | bytes 8388608 | tf_op jit(solution)/shard_map/all_to_all | solution.py:87
  128.3 8.5 %copy-start = (bf16[128,512]{1,0:T(8,128)(2,1)S(1)}, bf16[128,512]{1,0:T(8,128)(2,1)}, u32[]{:S(2)}) copy-start(bf16[128,512]{1,0:T(8,128)(2,1)} %param.9) | copy-start | bytes 393220
  132.6 11.4 %all-to-all-start.2 = ((bf16[4,2,256,128]{3,2,1,0:T(8,128)(2,1)}), bf16[4,2,256,128]{3,2,1,0:T(8,128)(2,1)S(1)}, u32[]{:S(2)}, u32[]{:S(2)}) async-start(bf16[4,2,256,128]{3,2,1,0:T(8,128)(2,1)} %project.1), calls=%async_computation.2 | async-start | bytes 1048576 | tf_op jit(solution)/shard_map/all_to_all | solution.py:87
  144.3 60.8 %collective-permute-start = (bf16[64,768]{1,0:T(8,128)(2,1)S(1)}, bf16[64,768]{1,0:T(8,128)(2,1)S(1)}, u32[]{:S(2)}, u32[]{:S(2)}) collective-permute-start(bf16[64,768]{1,0:T(8,128)(2,1)S(1)} %pad_maximum_fusion.2), channel_id=1, source_target_pairs={{0,128},{128,0},{1,129},{129,1},{2,130},{130,2},{3,131},{131,3},{4... | collective-permute-start | bytes 294920 | tf_op jit(solution)/shard_map/ppermute | solution.py:22
  205.0 25.6 %collective-permute-start.1 = (bf16[8,256,128]{2,1,0:T(8,128)(2,1)S(1)}, bf16[8,256,128]{2,1,0:T(8,128)(2,1)S(1)}, u32[]{:S(2)}, u32[]{:S(2)}) collective-permute-start(bf16[8,256,128]{2,1,0:T(8,128)(2,1)S(1)} %all_gather.17.p0), channel_id=1, source_target_pairs={{0,4},{4,8},{8,12},{12,16},{16,20},{20,24},{24,28},{28,32},{32,36}... | collective-permute-start | bytes 1572872 | tf_op jit(solution)/shard_map/ppermute | solution.py:26
  218.9 13.3 %collective-permute-start.2 = (bf16[8,256,128]{2,1,0:T(8,128)(2,1)S(1)}, bf16[8,256,128]{2,1,0:T(8,128)(2,1)S(1)}, u32[]{:S(2)}, u32[]{:S(2)}) collective-permute-start(bf16[8,256,128]{2,1,0:T(8,128)(2,1)S(1)} %all_gather.17.p0), channel_id=1, source_target_pairs={{0,188},{4,0},{8,4},{12,8},{16,12},{20,16},{24,20},{28,24},{32,28}... | collective-permute-start | bytes 1572872 | tf_op jit(solution)/shard_map/ppermute | solution.py:26
  232.3 18.4 %collective-permute-start.3 = (bf16[4,256,128]{2,1,0:T(8,128)(2,1)S(1)}, bf16[4,256,128]{2,1,0:T(8,128)(2,1)S(1)}, u32[]{:S(2)}, u32[]{:S(2)}) collective-permute-start(bf16[4,256,128]{2,1,0:T(8,128)(2,1)S(1)} %slice.65), channel_id=1, source_target_pairs={{0,188},{4,0},{8,4},{12,8},{16,12},{20,16},{24,20},{28,24},{32,28}... | collective-permute-start | bytes 786440 | tf_op jit(solution)/shard_map/ppermute | solution.py:26
  235.7 14.9 %collective-permute-start.4 = (bf16[4,256,128]{2,1,0:T(8,128)(2,1)S(1)}, bf16[4,256,128]{2,1,0:T(8,128)(2,1)S(1)}, u32[]{:S(2)}, u32[]{:S(2)}) collective-permute-start(bf16[4,256,128]{2,1,0:T(8,128)(2,1)S(1)} %slice.66), channel_id=1, source_target_pairs={{0,4},{4,8},{8,12},{12,16},{16,20},{20,24},{24,28},{28,32},{32,36}... | collective-permute-start | bytes 786440 | tf_op jit(solution)/shard_map/ppermute | solution.py:26
  257.4 14.6 %all-to-all-start.5 = ((bf16[16,8,2048]{2,1,0:T(8,128)(2,1)}), bf16[16,8,2048]{2,1,0:T(8,128)(2,1)S(1)}, u32[]{:S(2)}, u32[]{:S(2)}) async-start(bf16[16,8,2048]{2,1,0:T(8,128)(2,1)} %fusion), calls=%async_computation.5 | async-start | bytes 1048576 | tf_op jit(solution)/shard_map/all_to_all | solution.py:87

commit v11 on v9

--- a/solution.py
+++ b/solution.py
@@ -123,14 +123,15 @@
 
     sent = jnp.concatenate([theirs(squares_in), theirs(grad).reshape(64, 512)], axis=1)
     p0 = lax.all_gather(squares[0], ("zh", "z8", "z4"), axis=0, tiled=False)
-    p0, got = together(p0, swap(sent, "zh"))
+    p0, sent = together(p0, sent)
+    p3, p1, got = together(around(p0, 1), around(p0, -1), swap(sent, "zh"))
+    p2a, p2b = around(p1[:4], -1), around(p3[4:], 1)
     rows_in = in_order(mine(squares_in), got[:, :tokens])
     rows_in = lax.all_gather(rows_in, "x", axis=0, tiled=False)
     rows_in = rows_in.reshape(X, ZH, Y, C, 8, tokens).transpose(1, 3, 2, 0, 4, 5).reshape(ZH, 256, tokens)
     grad = in_order(mine(grad), got[:, tokens:].reshape(Y * C, 8, 512))
     grad = grad.reshape(ZH, Y, C, 8, 512).transpose(3, 1, 0, 2, 4).reshape(8, 8192)
-    p3, p1, rows_in = together(around(p0, 1), around(p0, -1), rows_in)
-    p2a, p2b, grad = together(around(p1[:4], -1), around(p3[4:], 1), grad)
+    p2a, p2b, grad, rows_in = together(p2a, p2b, grad, rows_in)
 
     partial = exchange(scale_part(rows_in, p0, p1, p2a, p2b, p3).reshape(C, Y * X, 8, 2048), "c")
     partial = exchange((partial[0].astype(f32) + partial[1].astype(f32)).astype(bf16), ("y", "x"))

time: 266 us -> 264 us (level)
  waiting for transfers between devices: 49 us -> 65.3 us
  starting transfers between devices: 82.8 us -> 73.1 us
  blocking collectives: 122 us -> 113 us
    ppermute x3, waiting for transfers between devices: 20.7 us -> 42.4 us  [swap(): return lax.ppermute(value, axis, [(0, 1), (1, 0)])]
    ppermute x3, starting transfers between devices: 51 us -> 41.4 us  [swap(): return lax.ppermute(value, axis, [(0, 1), (1, 0)])]
    all_to_all x1, blocking collectives: 16.9 us -> 9.64 us  [exchange(): return lax.all_to_all(value, axis, split_axis=0, concat_axis=0, tiled=True)]
    ppermute x4, waiting for transfers between devices: 5.49 us -> 0.01 us  [around(): return lax.ppermute(value, RING, [(i, (i + hops) % 32) for i in range(32)])]
  transfers between devices with their start and end apart: 11 -> 11, of which waited for: 7 -> 6; matrix products, arithmetic and copies ran while one was open for 0% -> 0% of each run, Pallas kernels for 0% -> 0%
where the time goes in v11:
time: 264 us
  blocking collectives  113 us (43%)
  starting transfers between devices  73.1 us (28%)
  waiting for transfers between devices  65.3 us (25%)
  other arithmetic  5.86 us (2%)
  Pallas kernels  4.95 us (2%)
    all_gather x1, blocking collectives, per_device(): p0 = lax.all_gather(squares[0], ('zh', 'z8', 'z4'), axis=0, tiled=False)  48.1 us
    all_gather x1, blocking collectives, per_device(): lax.all_gather(jnp.stack([out_grads, activations]), ('z8', 'z4'), axis=0,...  45.5 us
    ppermute x3, waiting for transfers between devices, swap(): return lax.ppermute(value, axis, [(0, 1), (1, 0)])  42.4 us
    ppermute x3, starting transfers between devices, swap(): return lax.ppermute(value, axis, [(0, 1), (1, 0)])  41.4 us
    all_to_all x4, waiting for transfers between devices, exchange(): return lax.all_to_all(value, axis, split_axis=0, concat_axis=0, tiled=True)  22.8 us
    all_to_all x4, starting transfers between devices, exchange(): return lax.all_to_all(value, axis, split_axis=0, concat_axis=0, tiled=True)  19.9 us
    ppermute x4, starting transfers between devices, around(): return lax.ppermute(value, RING, [(i, (i + hops) % 32) for i in range(32)])  11.8 us
    all_gather x1, blocking collectives, per_device(): rows_in = lax.all_gather(rows_in, 'x', axis=0, tiled=False)  10 us
  transfers between devices with their start and end apart: 11, of which 6 were waited for; matrix products, arithmetic and copies ran while one was open for 0% of the time, Pallas kernels for 0%

profile of v11, /device:TPU:1, one launch (start us, length us, event | category | flops | bytes accessed | tf_op | source)
XLA Modules:
  0.0 263.7 jit_solution(3697200837860531159)
XLA Ops:
  0.0 3.8 %copy_bitcast_fusion = bf16[4,2,16,128,128]{4,3,2,1,0:T(8,128)(2,1)} fusion(bf16[1,16,4,128,128]{4,3,2,1,0:T(8,128)(2,1)} %bitcast.59, bf16[1,16,4,128,128]{4,3,2,1,0:T(8,128)(2,1)} %bitcast.60), kind=kLoop, calls=%fused_computation.1 | loop fusion | flops 2097152 | bytes 8388608 | tf_op jit(solution)/shard_map/transpose | solution.py:109
  3.8 5.0 %all-to-all-start = ((bf16[4,2,16,128,128]{4,3,2,1,0:T(8,128)(2,1)}), bf16[4,2,16,128,128]{4,3,2,1,0:T(8,128)(2,1)}, u32[]{:S(2)}, u32[]{:S(2)}) async-start(bf16[4,2,16,128,128]{4,3,2,1,0:T(8,128)(2,1)} %copy_bitcast_fusion), calls=%async_computation | async-start | bytes 8388608 | tf_op jit(solution)/shard_map/all_to_all | solution.py:90
  8.8 45.5 %all-gather = bf16[8,256,128]{2,1,0:T(8,128)(2,1)S(1)} all-gather(bf16[2,256,128]{2,1,0:T(8,128)(2,1)S(1)} %pad_maximum_fusion.2), channel_id=2, replica_groups=mesh['y'=4,'zh'=2,'c'=2,'z8'=2,'z4'=2,'z2'=2,'z1'=2,'x'=4] {'z8','z4'}, dimensions={0}, use_global_device_ids=true | all-gather | bytes 655360 | tf_op jit(solution)/shard_map/all_gather | solution.py:111
  54.3 14.6 %collective-permute-start = (bf16[4,2,256,128]{3,2,1,0:T(8,128)(2,1)S(1)}, bf16[4,2,256,128]{3,2,1,0:T(8,128)(2,1)S(1)}, u32[]{:S(2)}, u32[]{:S(2)}) collective-permute-start(bf16[4,2,256,128]{3,2,1,0:T(8,128)(2,1)S(1)} %bitcast.57), channel_id=1, source_target_pairs={{0,8},{8,0},{1,9},{9,1},{2,10},{10,2},{3,11},{11,3},{4,12},{12,4},... | collective-permute-start | bytes 1572872 | tf_op jit(solution)/shard_map/ppermute | solution.py:22
  69.0 11.1 %collective-permute-done = bf16[4,2,256,128]{3,2,1,0:T(8,128)(2,1)S(1)} collective-permute-done((bf16[4,2,256,128]{3,2,1,0:T(8,128)(2,1)S(1)}, bf16[4,2,256,128]{3,2,1,0:T(8,128)(2,1)S(1)}, u32[]{:S(2)}, u32[]{:S(2)}) %collective-permute-start) | collective-permute-done | bytes 524320 | tf_op jit(solution)/shard_map/ppermute | solution.py:22
  80.1 0.1 pad_maximum_fusion.1.near_ref
  80.2 14.9 %collective-permute-start.1 = (bf16[8,2,256,128]{3,2,1,0:T(8,128)(2,1)S(1)}, bf16[8,2,256,128]{3,2,1,0:T(8,128)(2,1)S(1)}, u32[]{:S(2)}, u32[]{:S(2)}) collective-permute-start(bf16[8,2,256,128]{3,2,1,0:T(8,128)(2,1)S(1)} %pad_maximum_fusion.1.near_ref), channel_id=1, source_target_pairs={{0,4},{4,0},{1,5},{5,1},{2,6},{6,2},{3,7},{7,3},{8,12},{12,8},{9,1... | collective-permute-start | bytes 3145736 | tf_op jit(solution)/shard_map/ppermute | solution.py:22
  95.0 0.7 copy.36
  95.7 6.3 %all-to-all-start.1 = ((bf16[8,2,8,512]{3,2,1,0:T(8,128)(2,1)}), bf16[8,2,8,512]{3,2,1,0:T(8,128)(2,1)S(1)}, u32[]{:S(2)}, u32[]{:S(2)}) async-start(bf16[8,2,8,512]{3,2,1,0:T(8,128)(2,1)} %bitcast.9), calls=%async_computation.1 | async-start | bytes 262144 | tf_op jit(solution)/shard_map/all_to_all | solution.py:90
  102.0 5.3 %all-to-all-done.1 = bf16[8,2,8,512]{3,2,1,0:T(8,128)(2,1)S(1)} async-done(((bf16[8,2,8,512]{3,2,1,0:T(8,128)(2,1)}), bf16[8,2,8,512]{3,2,1,0:T(8,128)(2,1)S(1)}, u32[]{:S(2)}, u32[]{:S(2)}) %all-to-all-start.1) | async-done | bytes 131104 | tf_op jit(solution)/shard_map/all_to_all | solution.py:90
  107.3 9.6 %collective-permute-done.1.far_ref = bf16[8,2,256,128]{3,2,1,0:T(8,128)(2,1)S(1)} collective-permute-done((bf16[8,2,256,128]{3,2,1,0:T(8,128)(2,1)S(1)}, bf16[8,2,256,128]{3,2,1,0:T(8,128)(2,1)S(1)}, u32[]{:S(2)}, u32[]{:S(2)}) %collective-permute-start.1) | collective-permute-done | bytes 1048608 | tf_op jit(solution)/shard_map/ppermute | solution.py:22
  116.9 4.2 %project.1 = bf16[4,2,256,128]{3,2,1,0:T(8,128)(2,1)} custom-call(s32[1]{0:T(128)} %bitcast.z_ref, bf16[8,2,256,128]{3,2,1,0:T(8,128)(2,1)S(1)} %pad_maximum_fusion.1.near_ref, bf16[8,2,256,128]{3,2,1,0:T(8,128)(2,1)S(1)} %collective-permute-done.1.far_ref, bf16[4,2,16,128,128]{4,3,2,1,0:T(8,128)(2,1)} %all-to-all-done.basis_ref), custom_call_target="tpu_custom_call" | custom-call | flops 1073741824 | bytes 6800000 | tf_op jit(solution)/shard_map/project/pallas_call | solution.py:50
  121.1 3.5 %all-to-all-start.2 = ((bf16[4,2,256,128]{3,2,1,0:T(8,128)(2,1)}), bf16[4,2,256,128]{3,2,1,0:T(8,128)(2,1)S(1)}, u32[]{:S(2)}, u32[]{:S(2)}) async-start(bf16[4,2,256,128]{3,2,1,0:T(8,128)(2,1)} %project.1), calls=%async_computation.2 | async-start | bytes 1048576 | tf_op jit(solution)/shard_map/all_to_all | solution.py:90
  124.6 6.9 %all-to-all-done.2 = bf16[4,2,256,128]{3,2,1,0:T(8,128)(2,1)S(1)} async-done(((bf16[4,2,256,128]{3,2,1,0:T(8,128)(2,1)}), bf16[4,2,256,128]{3,2,1,0:T(8,128)(2,1)S(1)}, u32[]{:S(2)}, u32[]{:S(2)}) %all-to-all-start.2) | async-done | bytes 524320 | tf_op jit(solution)/shard_map/all_to_all | solution.py:90
  131.5 0.1 convert_reduce_fusion.1
  131.6 0.1 copy.37
  131.8 48.1 %all_gather.17.p0 = bf16[8,256,128]{2,1,0:T(8,128)(2,1)S(1)} all-gather(bf16[1,256,128]{2,1,0:T(8,128)(2,1)S(1)} %get-tuple-element.42), channel_id=1, replica_groups=mesh['y'=4,'zh'=2,'c'=2,'z8'=2,'z4'=2,'z2'=2,'z1'=2,'x'=4] {'zh','z8','z4'}, dimensions={0}, use_global_device_ids=true | all-gather | bytes 589824 | tf_op jit(solution)/shard_map/all_gather | solution.py:125
  179.9 1.9 collective-permute-start.3
  181.8 3.4 %collective-permute-start.2 = (bf16[8,256,128]{2,1,0:T(8,128)(2,1)S(1)}, bf16[8,256,128]{2,1,0:T(8,128)(2,1)S(1)}, u32[]{:S(2)}, u32[]{:S(2)}) collective-permute-start(bf16[8,256,128]{2,1,0:T(8,128)(2,1)S(1)} %all_gather.17.p0), channel_id=1, source_target_pairs={{0,4},{4,8},{8,12},{12,16},{16,20},{20,24},{24,28},{28,32},{32,36}... | collective-permute-start | bytes 1572872 | tf_op jit(solution)/shard_map/ppermute | solution.py:26
  185.2 11.9 %collective-permute-start.4 = (bf16[64,768]{1,0:T(8,128)(2,1)S(1)}, bf16[64,768]{1,0:T(8,128)(2,1)S(1)}, u32[]{:S(2)}, u32[]{:S(2)}) collective-permute-start(bf16[64,768]{1,0:T(8,128)(2,1)S(1)} %pad_maximum_fusion.3), channel_id=1, source_target_pairs={{0,128},{128,0},{1,129},{129,1},{2,130},{130,2},{3,131},{131,3},{4... | collective-permute-start | bytes 294920 | tf_op jit(solution)/shard_map/ppermute | solution.py:22
  197.1 21.7 %collective-permute-done.4 = bf16[64,768]{1,0:T(8,128)(2,1)S(1)} collective-permute-done((bf16[64,768]{1,0:T(8,128)(2,1)S(1)}, bf16[64,768]{1,0:T(8,128)(2,1)S(1)}, u32[]{:S(2)}, u32[]{:S(2)}) %collective-permute-start.4) | collective-permute-done | bytes 98336 | tf_op jit(solution)/shard_map/ppermute | solution.py:22
  218.9 0.0 collective-permute-done.3.p1
  219.0 1.9 collective-permute-start.6
  220.9 4.6 %collective-permute-start.5 = (bf16[4,256,128]{2,1,0:T(8,128)(2,1)S(1)}, bf16[4,256,128]{2,1,0:T(8,128)(2,1)S(1)}, u32[]{:S(2)}, u32[]{:S(2)}) collective-permute-start(bf16[4,256,128]{2,1,0:T(8,128)(2,1)S(1)} %slice.64), channel_id=1, source_target_pairs={{0,188},{4,0},{8,4},{12,8},{16,12},{20,16},{24,20},{28,24},{32,28}... | collective-permute-start | bytes 786440 | tf_op jit(solution)/shard_map/ppermute | solution.py:26
  225.5 10.0 %all-gather.1 = bf16[8,64,256]{2,1,0:T(8,128)(2,1)S(1)} all-gather(bf16[2,64,256]{2,1,0:T(8,128)(2,1)S(1)} %pad_maximum_fusion.4), channel_id=3, replica_groups=mesh['y'=4,'zh'=2,'c'=2,'z8'=2,'z4'=2,'z2'=2,'z1'=2,'x'=4] {'x'}, dimensions={0}, use_global_device_ids=true | all-gather | bytes 327680 | tf_op jit(solution)/shard_map/all_gather | solution.py:130
  235.6 0.7 scale.1
  236.3 9.6 %all_to_all.25 = bf16[2,16,8,2048]{3,2,1,0:T(8,128)(2,1)S(1)} all-to-all(bf16[2,16,8,2048]{3,2,1,0:T(8,128)(2,1)S(1)} %bitcast.51), channel_id=1, replica_groups=mesh['y'=4,'zh'=2,'c'=2,'z8'=2,'z4'=2,'z2'=2,'z1'=2,'x'=4] {'c'}, dimensions={0} | all-to-all | bytes 2097152 | tf_op jit(solution)/shard_map/all_to_all | solution.py:90
  246.0 0.9 fusion
  246.9 5.1 %all-to-all-start.4 = ((bf16[16,8,2048]{2,1,0:T(8,128)(2,1)}), bf16[16,8,2048]{2,1,0:T(8,128)(2,1)S(1)}, u32[]{:S(2)}, u32[]{:S(2)}) async-start(bf16[16,8,2048]{2,1,0:T(8,128)(2,1)} %fusion), calls=%async_computation.4 | async-start | bytes 1048576 | tf_op jit(solution)/shard_map/all_to_all | solution.py:90
  252.1 10.7 %all-to-all-done.4 = bf16[16,8,2048]{2,1,0:T(8,128)(2,1)S(1)} async-done(((bf16[16,8,2048]{2,1,0:T(8,128)(2,1)}), bf16[16,8,2048]{2,1,0:T(8,128)(2,1)S(1)}, u32[]{:S(2)}, u32[]{:S(2)}) %all-to-all-start.4) | async-done | bytes 524320 | tf_op jit(solution)/shard_map/all_to_all | solution.py:90
  262.7 0.1 convert_reduce_fusion
  263.0 0.7 divide_convert_fusion
  (30 shorter events, 0.4 us)
Async XLA Ops:
  3.8 5.0 %copy-start.1 = (bf16[256,128]{1,0:T(8,128)(2,1)S(1)}, bf16[256,128]{1,0:T(8,128)(2,1)}, u32[]{:S(2)}) copy-start(bf16[256,128]{1,0:T(8,128)(2,1)} %param.5) | copy-start | bytes 196612
  3.8 5.0 %copy-start.2 = (bf16[256,128]{1,0:T(8,128)(2,1)S(1)}, bf16[256,128]{1,0:T(8,128)(2,1)}, u32[]{:S(2)}) copy-start(bf16[256,128]{1,0:T(8,128)(2,1)} %param.6) | copy-start | bytes 196612
  3.8 91.2 %copy-start = (bf16[128,512]{1,0:T(8,128)(2,1)S(1)}, bf16[128,512]{1,0:T(8,128)(2,1)}, u32[]{:S(2)}) copy-start(bf16[128,512]{1,0:T(8,128)(2,1)} %param.9) | copy-start | bytes 393220
  3.8 76.4 %all-to-all-start = ((bf16[4,2,16,128,128]{4,3,2,1,0:T(8,128)(2,1)}), bf16[4,2,16,128,128]{4,3,2,1,0:T(8,128)(2,1)}, u32[]{:S(2)}, u32[]{:S(2)}) async-start(bf16[4,2,16,128,128]{4,3,2,1,0:T(8,128)(2,1)} %copy_bitcast_fusion), calls=%async_computation | async-start | bytes 8388608 | tf_op jit(solution)/shard_map/all_to_all | solution.py:90
  54.3 25.7 %collective-permute-start = (bf16[4,2,256,128]{3,2,1,0:T(8,128)(2,1)S(1)}, bf16[4,2,256,128]{3,2,1,0:T(8,128)(2,1)S(1)}, u32[]{:S(2)}, u32[]{:S(2)}) collective-permute-start(bf16[4,2,256,128]{3,2,1,0:T(8,128)(2,1)S(1)} %bitcast.57), channel_id=1, source_target_pairs={{0,8},{8,0},{1,9},{9,1},{2,10},{10,2},{3,11},{11,3},{4,12},{12,4},... | collective-permute-start | bytes 1572872 | tf_op jit(solution)/shard_map/ppermute | solution.py:22
  80.2 36.7 %collective-permute-start.1 = (bf16[8,2,256,128]{3,2,1,0:T(8,128)(2,1)S(1)}, bf16[8,2,256,128]{3,2,1,0:T(8,128)(2,1)S(1)}, u32[]{:S(2)}, u32[]{:S(2)}) collective-permute-start(bf16[8,2,256,128]{3,2,1,0:T(8,128)(2,1)S(1)} %pad_maximum_fusion.1.near_ref), channel_id=1, source_target_pairs={{0,4},{4,0},{1,5},{5,1},{2,6},{6,2},{3,7},{7,3},{8,12},{12,8},{9,1... | collective-permute-start | bytes 3145736 | tf_op jit(solution)/shard_map/ppermute | solution.py:22
  95.7 11.6 %all-to-all-start.1 = ((bf16[8,2,8,512]{3,2,1,0:T(8,128)(2,1)}), bf16[8,2,8,512]{3,2,1,0:T(8,128)(2,1)S(1)}, u32[]{:S(2)}, u32[]{:S(2)}) async-start(bf16[8,2,8,512]{3,2,1,0:T(8,128)(2,1)} %bitcast.9), calls=%async_computation.1 | async-start | bytes 262144 | tf_op jit(solution)/shard_map/all_to_all | solution.py:90
  121.1 10.4 %all-to-all-start.2 = ((bf16[4,2,256,128]{3,2,1,0:T(8,128)(2,1)}), bf16[4,2,256,128]{3,2,1,0:T(8,128)(2,1)S(1)}, u32[]{:S(2)}, u32[]{:S(2)}) async-start(bf16[4,2,256,128]{3,2,1,0:T(8,128)(2,1)} %project.1), calls=%async_computation.2 | async-start | bytes 1048576 | tf_op jit(solution)/shard_map/all_to_all | solution.py:90
  179.9 38.9 %collective-permute-start.3 = (bf16[8,256,128]{2,1,0:T(8,128)(2,1)S(1)}, bf16[8,256,128]{2,1,0:T(8,128)(2,1)S(1)}, u32[]{:S(2)}, u32[]{:S(2)}) collective-permute-start(bf16[8,256,128]{2,1,0:T(8,128)(2,1)S(1)} %all_gather.17.p0), channel_id=1, source_target_pairs={{0,188},{4,0},{8,4},{12,8},{16,12},{20,16},{24,20},{28,24},{32,28}... | collective-permute-start | bytes 1572872 | tf_op jit(solution)/shard_map/ppermute | solution.py:26
  181.8 37.0 %collective-permute-start.2 = (bf16[8,256,128]{2,1,0:T(8,128)(2,1)S(1)}, bf16[8,256,128]{2,1,0:T(8,128)(2,1)S(1)}, u32[]{:S(2)}, u32[]{:S(2)}) collective-permute-start(bf16[8,256,128]{2,1,0:T(8,128)(2,1)S(1)} %all_gather.17.p0), channel_id=1, source_target_pairs={{0,4},{4,8},{8,12},{12,16},{16,20},{20,24},{24,28},{28,32},{32,36}... | collective-permute-start | bytes 1572872 | tf_op jit(solution)/shard_map/ppermute | solution.py:26
  185.2 33.6 %collective-permute-start.4 = (bf16[64,768]{1,0:T(8,128)(2,1)S(1)}, bf16[64,768]{1,0:T(8,128)(2,1)S(1)}, u32[]{:S(2)}, u32[]{:S(2)}) collective-permute-start(bf16[64,768]{1,0:T(8,128)(2,1)S(1)} %pad_maximum_fusion.3), channel_id=1, source_target_pairs={{0,128},{128,0},{1,129},{129,1},{2,130},{130,2},{3,131},{131,3},{4... | collective-permute-start | bytes 294920 | tf_op jit(solution)/shard_map/ppermute | solution.py:22
  219.0 16.6 %collective-permute-start.6 = (bf16[4,256,128]{2,1,0:T(8,128)(2,1)S(1)}, bf16[4,256,128]{2,1,0:T(8,128)(2,1)S(1)}, u32[]{:S(2)}, u32[]{:S(2)}) collective-permute-start(bf16[4,256,128]{2,1,0:T(8,128)(2,1)S(1)} %slice.65), channel_id=1, source_target_pairs={{0,4},{4,8},{8,12},{12,16},{16,20},{20,24},{24,28},{28,32},{32,36}... | collective-permute-start | bytes 786440 | tf_op jit(solution)/shard_map/ppermute | solution.py:26
  220.9 14.7 %collective-permute-start.5 = (bf16[4,256,128]{2,1,0:T(8,128)(2,1)S(1)}, bf16[4,256,128]{2,1,0:T(8,128)(2,1)S(1)}, u32[]{:S(2)}, u32[]{:S(2)}) collective-permute-start(bf16[4,256,128]{2,1,0:T(8,128)(2,1)S(1)} %slice.64), channel_id=1, source_target_pairs={{0,188},{4,0},{8,4},{12,8},{16,12},{20,16},{24,20},{28,24},{32,28}... | collective-permute-start | bytes 786440 | tf_op jit(solution)/shard_map/ppermute | solution.py:26
  246.9 15.8 %all-to-all-start.4 = ((bf16[16,8,2048]{2,1,0:T(8,128)(2,1)}), bf16[16,8,2048]{2,1,0:T(8,128)(2,1)S(1)}, u32[]{:S(2)}, u32[]{:S(2)}) async-start(bf16[16,8,2048]{2,1,0:T(8,128)(2,1)} %fusion), calls=%async_computation.4 | async-start | bytes 1048576 | tf_op jit(solution)/shard_map/all_to_all | solution.py:90
